TPU v7x, 256 devices: a whole 4x4x8 slice. The times are simulated.
256 devices in a mesh: det: 16 (over x, y), tm: 16 (over z, core).
Axes of the slice: x: 4, y: 4, z: 8, core: 2. Of those that a mesh axis runs over, the one named last changes fastest.
Arguments:
- tod: float32 [512, 32768], P('det', 'tm'), may hold values from -6 to 6
- pointing: int32 [512, 32768], P('det', 'tm'), may hold values from 0 to 12287
- noise_level: float32 [8, 512], P(None, 'det'), may hold values from 0.5 to 4
- modes: float32 [8, 512, 128], P(None, 'det'), may hold values from -0.75 to 0.75
Outputs:
- filtered: float32 [512, 32768], P('det', 'tm')
- binned: float32 [12288], P(('det', 'tm'))
All inputs are finite; a program needn't handle non-finite values.
Results may differ from a plain program's by a relative error of at most 0.00026.
Values sent between devices are 32-bit elements; how exact they have to be, the bound alone decides.
No kernel may reach another device: no remote copies, remote signals or barrier semaphores. Data moves between devices by JAX's collectives and lax.ppermute only.
A program may use at most 64 MiB of HBM per device.

v0:
```python
import math

import jax
import jax.numpy as jnp
from jax import lax
from jax.sharding import PartitionSpec as P

FA = 128
FB = 256
TPIX = 48


HIGHEST = lax.Precision.HIGHEST


def rotation_table(size, total, sign):
    index = jnp.arange(size, dtype=jnp.int32)
    product = index[:, None] * index[None, :] % total
    angle = 2.0 * math.pi / total * product.astype(jnp.float32)
    return (jnp.cos(angle), sign * jnp.sin(angle))


def transform(real_in, imag_in, rows, cols, sign, real_out):
    length = rows * cols
    count = real_in.shape[0]
    first_cos, first_sin = rotation_table(rows, rows, sign)
    last_cos, last_sin = rotation_table(cols, cols, sign)
    grid_real = real_in.reshape(count, rows, cols)
    section_real = jnp.einsum("jm,rmq->rjq", first_cos, grid_real, precision=HIGHEST)
    section_imag = jnp.einsum("jm,rmq->rjq", first_sin, grid_real, precision=HIGHEST)
    if imag_in is not None:
        grid_imag = imag_in.reshape(count, rows, cols)
        section_real = section_real - jnp.einsum(
            "jm,rmq->rjq", first_sin, grid_imag, precision=HIGHEST
        )
        section_imag = section_imag + jnp.einsum(
            "jm,rmq->rjq", first_cos, grid_imag, precision=HIGHEST
        )
    row_index = jnp.arange(rows, dtype=jnp.int32)
    col_index = jnp.arange(cols, dtype=jnp.int32)
    turn = (row_index[:, None] * col_index[None, :] % length).astype(jnp.float32) * (
        2.0 * math.pi / length
    )
    turn_cos = jnp.cos(turn)
    turn_sin = sign * jnp.sin(turn)
    mixed_real = section_real * turn_cos - section_imag * turn_sin
    mixed_imag = section_real * turn_sin + section_imag * turn_cos
    out_real = jnp.einsum("km,rjm->rkj", last_cos, mixed_real, precision=HIGHEST) - jnp.einsum(
        "km,rjm->rkj", last_sin, mixed_imag, precision=HIGHEST
    )
    if real_out:
        return out_real.reshape(count, length)
    out_imag = jnp.einsum("km,rjm->rkj", last_sin, mixed_real, precision=HIGHEST) + jnp.einsum(
        "km,rjm->rkj", last_cos, mixed_imag, precision=HIGHEST
    )
    return (out_real.reshape(count, length), out_imag.reshape(count, length))


def solve_modes(factor, rhs):
    lower_part = lax.linalg.triangular_solve(factor, rhs, left_side=True, lower=True)
    return lax.linalg.triangular_solve(
        factor, lower_part, left_side=True, lower=True, transpose_a=True
    )


def band_of(freq, length, width, bands):
    folded = jnp.minimum(freq, length - freq)
    return jnp.minimum(folded // width, bands - 1)


def pick(array, index):
    return lax.dynamic_index_in_dim(array, index, 0, keepdims=False)


def body(tod, pointing, noise_level, modes):
    groups = lax.axis_size("tm")
    row_pos = lax.axis_index("tm")
    det_dev, block = tod.shape
    det_row = det_dev // groups
    length = block * groups
    bands = noise_level.shape[0]
    width = length // groups
    mode_count = modes.shape[2]
    eye = jnp.eye(mode_count, dtype=jnp.float32)
    start = row_pos * width
    main_band = band_of(start + 1, length, width, bands)
    side_band = band_of(start, length, width, bands)
    scaled = modes / noise_level[:, :, None]
    partial_all = jnp.einsum("bdm,bdn->bmn", modes, scaled, precision=HIGHEST)
    summed = lax.psum(partial_all, "det")
    gram_main = pick(summed, main_band) + eye
    gram_side = pick(summed, side_band) + eye
    factor_main = jnp.linalg.cholesky(gram_main)
    factor_side = jnp.linalg.cholesky(gram_side)
    arranged = tod.reshape(groups, det_row, block)
    spec_real, spec_imag = transform(
        lax.all_to_all(arranged, "tm", split_axis=0, concat_axis=2, tiled=True)[0],
        None,
        FA,
        FB,
        -1.0,
        False,
    )
    spec_real, spec_imag = (spec_real[None], spec_imag[None])
    spec_real = spec_real[0]
    spec_imag = spec_imag[0]
    basis_main = pick(modes, main_band)
    inverse_main = 1.0 / pick(noise_level, main_band)
    basis_side = pick(modes, side_band)
    inverse_side = 1.0 / pick(noise_level, side_band)
    band_real, band_imag = (
        lax.all_to_all(spec_real, "tm", split_axis=1, concat_axis=0, tiled=True),
        lax.all_to_all(spec_imag, "tm", split_axis=1, concat_axis=0, tiled=True),
    )
    stacked = jnp.concatenate([band_real, band_imag], axis=1) * inverse_main[:, None]
    first = jnp.stack([band_real[:, 0], band_imag[:, 0]], axis=1) * inverse_side[:, None]
    proj_main = jnp.dot(
        basis_main.T, stacked, precision=HIGHEST, preferred_element_type=jnp.float32
    )
    proj_side = jnp.dot(basis_side.T, first, precision=HIGHEST, preferred_element_type=jnp.float32)
    proj_main, proj_side = lax.psum((proj_main, proj_side), "det")
    coef_main = solve_modes(factor_main, proj_main)
    coef_side = solve_modes(factor_side, proj_side)
    out_main = (
        stacked
        - jnp.dot(basis_main, coef_main, precision=HIGHEST, preferred_element_type=jnp.float32)
        * inverse_main[:, None]
    )
    out_side = (
        first
        - jnp.dot(basis_side, coef_side, precision=HIGHEST, preferred_element_type=jnp.float32)
        * inverse_side[:, None]
    )
    out_real = out_main[:, :width].at[:, 0].set(out_side[:, 0])
    out_imag = out_main[:, width:].at[:, 0].set(out_side[:, 1])
    full_real, full_imag = (
        lax.all_to_all(out_real, "tm", split_axis=0, concat_axis=1, tiled=True),
        lax.all_to_all(out_imag, "tm", split_axis=0, concat_axis=1, tiled=True),
    )
    filtered_rows = transform(full_real, full_imag, FB, FA, 1.0, True) * (1.0 / length)
    filtered = lax.all_to_all(filtered_rows, "tm", split_axis=1, concat_axis=0, tiled=True)
    pixels = TPIX * lax.axis_size("det") * groups
    flat_pointing = pointing.reshape(-1)
    sums = jax.ops.segment_sum(filtered.reshape(-1), flat_pointing, num_segments=pixels)
    hits = jax.ops.segment_sum(
        jnp.ones(flat_pointing.shape, jnp.float32), flat_pointing, num_segments=pixels
    )
    sums, hits = (
        lax.psum_scatter(sums, ("det", "tm"), scatter_dimension=0, tiled=True),
        lax.psum_scatter(hits, ("det", "tm"), scatter_dimension=0, tiled=True),
    )
    return (filtered, sums / jnp.sqrt(1.0 + hits))


def solution(mesh):
    placed = (P("det", "tm"), P("det", "tm"), P(None, "det"), P(None, "det", None))
    return jax.shard_map(
        body,
        mesh=mesh,
        in_specs=placed,
        out_specs=(P("det", "tm"), P(("det", "tm"))),
        check_vma=False,
    )
```

profile of v0, /device:TPU:1, one launch (start us, length us, event | category | flops | bytes accessed | tf_op | source)
XLA Modules:
  0.0 1424.8 jit_solution(13933355479438649841)
XLA Ops:
  7.2 1.8 reshape.191
  9.0 10.0 all-to-all-start
  18.9 0.5 sine_multiply_fusion
  19.5 11.1 all-to-all-done
  30.5 0.2 copy.69
  30.7 0.6 fusion.86
  31.4 0.6 fusion.89
  32.0 1.4 fusion.24
  33.4 1.4 fusion.6
  35.0 0.9 copy.71
  35.9 3.4 all-to-all-start.1
  39.3 1.4 fusion.15
  40.7 1.4 fusion.5
  42.3 0.9 copy.73
  43.2 7.3 all-to-all-done.1
  50.5 3.4 all-to-all-start.2
  53.9 0.2 all-reduce.9.cloned.1.call-start
  54.2 1.9 convolution_bitcast_fusion
  56.1 0.2 all_to_all.81
  56.3 9.4 all-to-all-done.2
  65.6 0.2 all_to_all.85
  65.8 3.2 fusion.8
  69.0 0.6 compare_reduce_fusion.2
  69.6 0.3 fusion.111
  69.9 34.0 %psum.23 = f32[128,2]{0,1:T(2,128)S(1)} all-reduce(f32[128,2]{0,1:T(2,128)S(1)} %fusion.111), channel_id=1, replica_groups=mesh['det'=16,'tm'=16] {'det'}, use_global_device_ids=true, to_apply=%region_5.7 | all-reduce | flops 256 | bytes 2048 | tf_op jit(solution)/shard_map/psum | solution.py:121
  103.9 64.2 %all-reduce.9.cloned.1.call-done = (f32[128,4096]{1,0:T(8,128)}, f32[8,128,128]{1,2,0:T(8,128)}) async-done(((f32[128,4096]{1,0:T(8,128)}, f32[8,128,128]{1,2,0:T(8,128)}), (f32[128,4096]{1,0:T(8,128)}, f32[8,128,128]{1,2,0:T(8,128)})) %all-reduce.9.cloned.1.call-update) | async-done | bytes 2621456 | tf_op jit(solution)/shard_map/psum | solution.py:121
  168.1 0.9 convert_add_fusion
  169.1 11.7 cholesky.55
  180.9 0.6 compare_reduce_fusion
  181.5 0.7 fusion.71
  182.2 9.8 custom-call.13
  192.0 0.2 fusion.78
  192.2 0.2 fusion.76
  192.4 0.2 fusion.7
  192.7 11.7 cholesky.44
  204.4 0.6 compare_reduce_fusion.1
  205.1 0.7 fusion.70
  205.7 10.0 custom-call.12
  215.7 3.5 fusion.83
  219.2 1.9 fusion.81
  221.2 1.2 fusion
  222.4 0.7 slice_select_fusion
  223.2 0.8 all_to_all.86
  224.0 8.6 all-to-all-start.3
  232.7 0.8 all_to_all.89
  233.6 10.7 all-to-all-done.3
  244.2 3.4 all-to-all-start.4
  247.6 0.5 fusion.91
  248.2 0.2 copy.77
  248.4 1.5 fusion.21
  249.9 1.5 fusion.12
  251.3 7.4 all-to-all-done.4
  258.8 0.2 copy.79
  259.0 1.5 fusion.4
  260.5 1.5 fusion.3
  262.0 0.8 fusion.31
  262.7 0.8 fusion.2
  263.7 0.9 copy.86
  264.6 3.4 all-to-all-start.5
  268.2 452.3 %scatter_custom_fusion.1 = f32[12288]{0:T(1024)} fusion(s32[65536]{0:T(1024)S(1)} %bitcast.127, f32[65536]{0:T(1024)S(1)} %broadcast.281, f32[]{:T(128)} %constant.212.clone.1), kind=kCustom, calls=%fused_computation.131 | custom fusion | flops 65536 | bytes 49156 | tf_op jit(solution)/shard_map/scatter-add | solution.py:145
  720.5 452.3 %scatter_custom_fusion = f32[12288]{0:T(1024)} fusion(s32[65536]{0:T(1024)S(1)} %bitcast.128, f32[65536]{0:T(1024)S(1)} %bitcast.129, f32[]{:T(128)} %constant.212.clone.1), kind=kCustom, calls=%fused_computation.133 | custom fusion | flops 65536 | bytes 49156 | tf_op jit(solution)/shard_map/scatter-add | solution.py:144
  1172.8 0.9 all_to_all.94
  1173.7 242.5 %all-reduce.7.cloned.1.call-done = (f32[12288]{0:T(1024)}, f32[12288]{0:T(1024)}) async-done(((f32[12288]{0:T(1024)}, f32[12288]{0:T(1024)}), (f32[12288]{0:T(1024)}, f32[12288]{0:T(1024)})) %all-reduce.7.cloned.1.call-update) | async-done | bytes 98320
  1416.3 1.3 fusion.138
  (34 shorter events, 1.3 us)
Async XLA Ops:
  9.0 21.6 %all-to-all-start = ((f32[16,2,2048]{2,1,0:T(2,128)}), f32[16,2,2048]{2,1,0:T(2,128)S(1)}, u32[]{:S(2)}, u32[]{:S(2)}) async-start(f32[16,2,2048]{2,1,0:T(2,128)} %reshape.191), calls=%async_computation | async-start | bytes 524288 | tf_op jit(solution)/shard_map/all_to_all | solution.py:97
  35.9 14.6 %all-to-all-start.1 = ((f32[2,16,2048]{2,0,1:T(2,128)}), f32[2,16,2048]{2,0,1:T(2,128)S(1)}, u32[]{:S(2)}, u32[]{:S(2)}) async-start(f32[2,16,2048]{2,0,1:T(2,128)} %copy.71), calls=%async_computation.1 | async-start | bytes 524288 | tf_op jit(solution)/shard_map/all_to_all | solution.py:112
  40.7 13.4 copy-start.2
  40.7 13.5 copy-start
  50.5 15.2 %all-to-all-start.2 = ((f32[2,16,2048]{2,0,1:T(2,128)}), f32[2,16,2048]{2,0,1:T(2,128)S(1)}, u32[]{:S(2)}, u32[]{:S(2)}) async-start(f32[2,16,2048]{2,0,1:T(2,128)} %copy.73), calls=%async_computation.2 | async-start | bytes 524288 | tf_op jit(solution)/shard_map/all_to_all | solution.py:113
  53.9 114.2 %all-reduce.9.cloned.1.call-start = ((), (), s32[]{:S(2)}) async-start(), calls=%async_computation.7 | async-start | bytes 5242880 | tf_op jit(solution)/shard_map/psum | solution.py:121
  224.0 20.2 %all-to-all-start.3 = ((f32[16,2,2048]{2,1,0:T(2,128)}), f32[16,2,2048]{2,1,0:T(2,128)S(1)}, u32[]{:S(2)}, u32[]{:S(2)}) async-start(f32[16,2,2048]{2,1,0:T(2,128)} %all_to_all.86), calls=%async_computation.3 | async-start | bytes 524288 | tf_op jit(solution)/shard_map/all_to_all | solution.py:137
  244.2 14.6 %all-to-all-start.4 = ((f32[16,2,2048]{2,1,0:T(2,128)}), f32[16,2,2048]{2,1,0:T(2,128)S(1)}, u32[]{:S(2)}, u32[]{:S(2)}) async-start(f32[16,2,2048]{2,1,0:T(2,128)} %all_to_all.89), calls=%async_computation.4 | async-start | bytes 524288 | tf_op jit(solution)/shard_map/all_to_all | solution.py:138
  262.0 6.1 copy-start.1
  264.6 455.9 %all-to-all-start.5 = ((f32[2,16,2048]{2,0,1:T(2,128)}), f32[2,16,2048]{2,0,1:T(2,128)S(1)}, u32[]{:S(2)}, u32[]{:S(2)}) async-start(f32[2,16,2048]{2,0,1:T(2,128)} %copy.86), calls=%async_computation.5 | async-start | bytes 524288 | tf_op jit(solution)/shard_map/all_to_all | solution.py:141
  268.0 1148.2 %all-reduce.7.cloned.1.call-start = ((), (), s32[]{:S(2)}) async-start(), calls=%async_computation.6 | async-start | bytes 196608
Sparse Core Ops, SparseCore 0:
  69.1 98.9 all-reduce.8
  1172.9 243.2 all-reduce.6
where the time goes:
time: 1430 us; the launch traced here: 1420 us
  other arithmetic  955 us (67%)
  waiting for transfers between devices  353 us (25%)
  blocking collectives  34 us (2%)
  starting transfers between devices  32.5 us (2%)
  matrix products  26.6 us (2%)
  between operations  14.9 us (1%)
    scatter-add x1, other arithmetic, body(): jax.ops.segment_sum(filtered.reshape(-1), flat_pointing, num_segments=pix...  452 us
    scatter-add x1, other arithmetic, body(): jax.ops.segment_sum(jnp.ones(flat_pointing.shape, jnp.float32), flat_poin...  452 us
    unnamed x3, waiting for transfers between devices  243 us
    psum x1, waiting for transfers between devices, body(): proj_main, proj_side = lax.psum((proj_main, proj_side), 'det')  64.2 us
    psum x1, blocking collectives, body(): proj_main, proj_side = lax.psum((proj_main, proj_side), 'det')  34 us
  transfers between devices with their start and end apart: 8, of which 7 were waited for; matrix products, arithmetic and copies ran while one was open for 33% of the time, Pallas kernels for 0%

commit v1 on v0

v1 whole, which is shorter than its diff:
```python
import numpy as np
import jax
import jax.numpy as jnp
from jax import lax
from jax.experimental import pallas as pl
from jax.experimental.pallas import tpu as pltpu
from jax.sharding import PartitionSpec as P


HIGHEST = lax.Precision.HIGHEST
NS = 32768
N1 = 128
N2 = 256
BANDS = 8
TPIX = 48
F32 = jnp.float32
BF16 = jnp.bfloat16


def _slots():
    dev, step = np.meshgrid(np.arange(16), np.arange(8), indexing="ij")
    top = (16 * step + dev).reshape(-1)
    bottom = (16 * (step + 8) + dev).reshape(-1)
    return top, bottom


def _forward_tables():
    n1 = np.arange(N1)[:, None]
    k1 = np.arange(64)[None, :]
    angle = 2 * np.pi * (n1 * k1 % N1) / N1
    first = np.concatenate([np.cos(angle), -np.sin(angle)], axis=1)
    first[:, 64] = np.cos(np.pi * np.arange(N1))
    n2 = np.arange(N2)[:, None]
    turn = 2 * np.pi * (n2 * k1) / NS
    keep = np.concatenate([np.cos(turn), np.cos(turn)], axis=1)
    swap = np.concatenate([np.sin(turn), -np.sin(turn)], axis=1)
    edge = 2 * np.pi * 64 * np.arange(N2) / NS
    keep[:, 0] = 1.0
    swap[:, 0] = np.cos(edge)
    keep[:, 64] = -np.sin(edge)
    swap[:, 64] = 0.0
    last = []
    for rows in _slots():
        phase = 2 * np.pi * (rows[:, None] * np.arange(N2)[None, :] % N2) / N2
        last.append(np.concatenate([np.cos(phase), np.sin(phase)], axis=1))
    return [np.asarray(a, np.float32) for a in (first, keep, swap, last[0], last[1])]


def _inverse_tables():
    na = np.arange(N2)
    first = []
    for position, rows in enumerate(_slots()):
        phase = 2 * np.pi * (na[:, None] * rows[None, :] % N2) / N2
        sine = np.sin(phase)
        if position == 0:
            sine[:, 0] = np.where(na % 2 == 0, 1.0, -1.0)
        first.append(np.concatenate([np.cos(phase), sine], axis=1))
    k1 = np.arange(64)[None, :]
    turn = 2 * np.pi * (na[:, None] * k1) / NS
    keep = np.concatenate([2 * np.cos(turn), 2 * np.cos(turn)], axis=1)
    swap = np.concatenate([-2 * np.sin(turn), 2 * np.sin(turn)], axis=1)
    edge = 2 * np.pi * 64 * na / NS
    keep[:, 0] = 2.0
    swap[:, 0] = 0.0
    keep[:, 64] = -2 * np.sin(edge)
    swap[:, 64] = 2 * np.cos(edge)
    nb = np.arange(N1)[:, None]
    angle = 2 * np.pi * (nb * k1 % N1) / N1
    last = np.concatenate([np.cos(angle), -np.sin(angle)], axis=1) / NS
    last[:, 64] = np.cos(np.pi * np.arange(N1)) / NS
    return [np.asarray(a, np.float32) for a in (first[0], first[1], keep, swap, last)]


def _dot(a, b):
    return jnp.dot(a, b, precision=HIGHEST, preferred_element_type=F32)


def _dot_tn(a, b):
    return lax.dot_general(
        a, b, (((0,), (0,)), ((), ())), precision=HIGHEST, preferred_element_type=F32
    )


def _dot_nt(a, b):
    return lax.dot_general(
        a, b, (((1,), (1,)), ((), ())), precision=HIGHEST, preferred_element_type=F32
    )


def _lanes(shape):
    return lax.broadcasted_iota(jnp.int32, shape, 1)


def prep_kernel(where_ref, tod_ref, point_ref, modes_ref, noise_ref, tod_out, v_out, tod_tmp, point_tmp):
    for octet in range(4):
        for r in range(8):
            for h in range(2):
                cols = pl.ds(256 * r + 128 * h, 128)
                rows = pl.ds(256 * h + 64 * octet + r, 8, stride=8)
                tod_tmp[rows, :] = tod_ref[8 * octet : 8 * octet + 8, cols]
                point_tmp[rows, :] = point_ref[8 * octet : 8 * octet + 8, cols].astype(F32)
    for h in range(2):
        cols = slice(128 * h, 128 * h + 128)
        part = slice(256 * h, 256 * h + 256)
        tod_out[:, 0:16, cols] = tod_tmp[part, :].reshape(16, 16, 128)
        tod_out[:, 16:32, cols] = point_tmp[part, :].reshape(16, 16, 128)
    band = where_ref[0]
    root = lax.rsqrt(noise_ref[...])
    eye = lax.broadcasted_iota(jnp.int32, (32, 32), 0) == _lanes((32, 32))
    row_of = lax.broadcasted_iota(jnp.int32, (BANDS, 32), 0)
    for part, which in enumerate((band, BANDS - 1)):
        row = jnp.sum(jnp.where(row_of == which, root, 0.0), axis=0, keepdims=True)
        col = jnp.sum(jnp.where(eye, row, 0.0), axis=1, keepdims=True)
        vee = modes_ref[which] * col
        for dest in range(16):
            v_out[dest, 32 * part : 32 * part + 32, :] = vee


def scales_kernel(where_ref, noise_ref, scale_out):
    pos = where_ref[1]
    root = lax.rsqrt(noise_ref[...])
    noise_ref_lane = _lanes((BANDS, 32))
    flipped = jnp.concatenate([root[BANDS - 1 - j : BANDS - j] for j in range(BANDS)], axis=0)
    for e in range(2):
        mask = noise_ref_lane == 16 * e + pos
        lanes = pl.ds(128 * e, 128)
        up = jnp.sum(jnp.where(mask, root, 0.0), axis=1, keepdims=True)
        down = jnp.sum(jnp.where(mask, flipped, 0.0), axis=1, keepdims=True)
        scale_out[0:8, lanes] = jnp.broadcast_to(up, (8, 128))
        scale_out[8:16, lanes] = jnp.broadcast_to(down, (8, 128))
        scale_out[16:24, lanes] = jnp.broadcast_to(up[7:8], (8, 128))


def _first_scale(scale_ref):
    lane = _lanes((8, 256)) % 128
    row = lax.broadcasted_iota(jnp.int32, (8, 256), 0)
    return jnp.where((lane == 64) & (row == 0), scale_ref[16:24, :], scale_ref[0:8, :])


def forward_kernel(x_ref, scale_ref, first_ref, keep_ref, swap_ref, top_ref, bottom_ref, out_ref):
    lane = _lanes((N2, 128))
    sign = jnp.where(lane < 64, 1.0, -1.0)
    parity = lax.broadcasted_iota(jnp.int32, (N2, 128), 0) % 2
    alternate = jnp.where(lane == 64, jnp.where(parity == 0, -1.0, 1.0), 0.0)
    tops, bottoms, nyquist = [], [], []
    for e in range(2):
        x = x_ref[:, 8 * e : 8 * e + 8, :].reshape(N1, N2)
        s = _dot_tn(x, first_ref[...])
        a = keep_ref[...] * s
        b = swap_ref[...] * pltpu.roll(s, 64, 1)
        both = a + b
        top = jnp.where(lane == 0, a, jnp.where(lane == 64, 0.0, both))
        bottom = jnp.where(lane == 0, b, jnp.where(lane == 64, a, both))
        top_turn = pltpu.roll(top, 64, 1) * sign
        bottom_turn = pltpu.roll(bottom, 64, 1) * sign
        nyquist.append(jnp.sum(top_turn * alternate, axis=0, keepdims=True))
        tops.append(jnp.concatenate([top, top_turn], axis=0))
        bottoms.append(jnp.concatenate([bottom, bottom_turn], axis=0))
    out_top = _dot(top_ref[...], jnp.concatenate(tops, axis=1))
    out_bottom = _dot(bottom_ref[...], jnp.concatenate(bottoms, axis=1))
    nyq = jnp.concatenate(nyquist, axis=1)
    row0 = lax.broadcasted_iota(jnp.int32, (8, 256), 0) == 0
    for d in range(16):
        up = out_top[8 * d : 8 * d + 8]
        if d == 0:
            up = (up + jnp.where(row0, nyq, 0.0)) * _first_scale(scale_ref)
        else:
            up = up * scale_ref[0:8, :]
        down = out_bottom[8 * d : 8 * d + 8] * scale_ref[8:16, :]
        for e in range(2):
            cols = slice(128 * e, 128 * e + 128)
            out_ref[pl.ds(32 * d + e, 8, stride=2), :] = up[:, cols]
            out_ref[pl.ds(32 * d + 16 + e, 8, stride=2), :] = down[:, cols]


def gram_kernel(v_ref, trans_ref, gain_ref, mats_ref):
    parts = []
    for e in range(2):
        row = []
        for part in range(2):
            low = 32 * part + 0
            row.append(v_ref[:, low + 16 * e : low + 16 * e + 16, :].reshape(256, 128))
        parts.append(row)
    eye = lax.broadcasted_iota(jnp.int32, (128, 128), 0) == _lanes((128, 128))
    for part in range(2):
        mats_ref[part] = (
            jnp.where(eye, 1.0, 0.0)
            + _dot_tn(parts[0][part], parts[0][part])
            + _dot_tn(parts[1][part], parts[1][part])
        )
    lane = _lanes((1, 128))
    sub = lax.broadcasted_iota(jnp.int32, (128, 1), 0)

    def step(k, carry):
        here = lane == k
        there = sub == k
        for part in range(2):
            mat = mats_ref[part]
            row = mats_ref[part, pl.ds(k, 1), :]
            pivot = jnp.sum(jnp.where(here, row, 0.0), axis=1, keepdims=True)
            inverse = 1.0 / pivot
            col = jnp.sum(jnp.where(here, mat, 0.0), axis=1, keepdims=True)
            scaled = jnp.where(here, inverse, row * inverse)
            cleared = jnp.where(here, 0.0, mat)
            mats_ref[part] = jnp.where(there, scaled, cleared - col * scaled)
        return carry

    lax.fori_loop(0, 128, step, 0)
    for e in range(2):
        trans_ref[e] = jnp.concatenate([parts[e][0], parts[e][1]], axis=1).T
        gain_ref[e] = jnp.concatenate(
            [_dot(parts[e][0], mats_ref[0]), _dot(parts[e][1], mats_ref[1])], axis=1
        )


def apply_kernel(where_ref, x_ref, trans_ref, gain_ref, out_ref):
    xs = [x_ref[pl.ds(e, 256, stride=2), :] for e in range(2)]
    proj = _dot(trans_ref[0], xs[0]) + _dot(trans_ref[1], xs[1])
    special = (_lanes((256, 128)) == 64) & (where_ref[2] == 0)
    second = lax.broadcasted_iota(jnp.int32, (256, 128), 0) >= 128
    proj = jnp.where(special == second, proj, 0.0)
    for e in range(2):
        out_ref[pl.ds(e, 256, stride=2), :] = xs[e] - _dot(gain_ref[e], proj)


def inverse_kernel(y_ref, scale_ref, top_ref, bottom_ref, keep_ref, swap_ref, last_ref, out_ref):
    lane2 = _lanes((128, 256)) % 128
    sign2 = jnp.where(lane2 < 64, -1.0, 1.0)
    ups, downs = [], []
    for d in range(16):
        up, down = [
            jnp.concatenate(
                [y_ref[pl.ds(32 * d + 16 * half + e, 8, stride=2), :] for e in range(2)], axis=1
            )
            for half in range(2)
        ]
        ups.append(up * (_first_scale(scale_ref) if d == 0 else scale_ref[0:8, :]))
        downs.append(down * scale_ref[8:16, :])
    top = jnp.concatenate(ups, axis=0)
    bottom = jnp.concatenate(downs, axis=0)

    def turned(v):
        halves = [pltpu.roll(v[:, 128 * e : 128 * e + 128], 64, 1) for e in range(2)]
        return jnp.concatenate(halves, axis=1)

    first_row = lax.broadcasted_iota(jnp.int32, (128, 256), 0) == 0
    top_turn = turned(top)
    nyquist = jnp.where(lane2 == 0, 0.5 * top_turn, 0.0)
    top_turn = jnp.where(first_row, nyquist, top_turn * sign2)
    top = jnp.where(first_row & (lane2 == 0), 0.5 * top, top)
    bottom_turn = turned(bottom) * sign2
    a_top = _dot(top_ref[...], jnp.concatenate([top, top_turn], axis=0))
    a_bottom = _dot(bottom_ref[...], jnp.concatenate([bottom, bottom_turn], axis=0))
    lane = _lanes((N2, 128))
    for e in range(2):
        cols = slice(128 * e, 128 * e + 128)
        up, down = a_top[:, cols], a_bottom[:, cols]
        both = up + down
        direct = jnp.where(lane == 0, up, jnp.where(lane == 64, down, both))
        rolled = pltpu.roll(jnp.where(lane == 0, down, both), 64, 1)
        z = keep_ref[...] * direct + swap_ref[...] * rolled
        x = _dot_nt(last_ref[...], z)
        out_ref[:, 8 * e : 8 * e + 8, :] = x.reshape(16, 8, N2)


def split_pixel(point):
    owner = jnp.floor((point + 0.5) * (1.0 / TPIX))
    return owner, point - owner * TPIX


def _one_hot(row, count):
    index = lax.broadcasted_iota(jnp.int32, (count, 256), 0).astype(F32).astype(BF16)
    return index == jnp.broadcast_to(row, (count, 256)).astype(BF16)


def hits_kernel(point_ref, out_ref, owner_ref, inner_ref):
    owner, inner = split_pixel(point_ref[:, 16:32, :].reshape(256, 256))
    owner_ref[...] = owner
    inner_ref[...] = inner
    one = jnp.ones((), BF16)
    zero = jnp.zeros((), BF16)

    def step(r, acc):
        big = jnp.where(_one_hot(owner_ref[pl.ds(r, 1), :], 256), one, zero)
        small = jnp.where(_one_hot(inner_ref[pl.ds(r, 1), :], TPIX), one, zero)
        return acc + lax.dot_general(
            small, big, (((1,), (1,)), ((), ())), preferred_element_type=F32
        )

    out_ref[...] = lax.fori_loop(0, 256, step, jnp.zeros((TPIX, 256), F32), unroll=4)


def sums_kernel(value_ref, owner_ref, inner_ref, hits_ref, out_ref):
    zero = jnp.zeros((), BF16)

    def step(r, acc):
        value = value_ref[pl.ds(r, 1), :]
        high = value.astype(BF16)
        low = (value - high.astype(F32)).astype(BF16)
        big = jnp.where(_one_hot(owner_ref[pl.ds(r, 1), :], 256), jnp.ones((), BF16), zero)
        pick = _one_hot(inner_ref[pl.ds(r, 1), :], TPIX)
        small = jnp.concatenate(
            [
                jnp.where(pick, jnp.broadcast_to(high.astype(F32), (TPIX, 256)).astype(BF16), zero),
                jnp.where(pick, jnp.broadcast_to(low.astype(F32), (TPIX, 256)).astype(BF16), zero),
            ],
            axis=0,
        )
        return acc + lax.dot_general(
            small, big, (((1,), (1,)), ((), ())), preferred_element_type=F32
        )

    acc = lax.fori_loop(0, 256, step, jnp.zeros((2 * TPIX, 256), F32), unroll=4)
    sums = acc[:TPIX] + acc[TPIX:]
    full = jnp.concatenate([sums, hits_ref[...], jnp.zeros((32, 256), F32)], axis=0)
    out_ref[...] = full.T


def spread_kernel(x_ref, out_ref, tmp_ref):
    for h in range(2):
        tmp_ref[256 * h : 256 * h + 256, :] = x_ref[:, 128 * h : 128 * h + 128]
    for octet in range(4):
        for r in range(8):
            for h in range(2):
                rows = pl.ds(256 * h + 64 * octet + r, 8, stride=8)
                cols = pl.ds(256 * r + 128 * h, 128)
                out_ref[8 * octet : 8 * octet + 8, cols] = tmp_ref[rows, :]


def finish_kernel(x_ref, out_ref):
    total = jnp.sum(x_ref[...], axis=0, keepdims=True)
    hits = pltpu.roll(total, 128 - TPIX, 1)
    out_ref[...] = total / jnp.sqrt(1.0 + hits)


VMEM = pl.BlockSpec(memory_space=pltpu.VMEM)
SMEM = pl.BlockSpec(memory_space=pltpu.SMEM)


def call(kernel, outs, scratch=(), smem=0):
    many = isinstance(outs, list)
    shapes = [jax.ShapeDtypeStruct(s, d) for s, d in (outs if many else [outs])]

    def run(*args):
        return pl.pallas_call(
            kernel,
            out_shape=shapes if many else shapes[0],
            in_specs=[SMEM] * smem + [VMEM] * (len(args) - smem),
            out_specs=[VMEM] * len(shapes) if many else VMEM,
            scratch_shapes=list(scratch),
        )(*args)

    return run


def exchange(value, axes):
    return lax.all_to_all(value, axes, split_axis=0, concat_axis=0, tiled=True)


def steps(tod, pointing, noise_level, modes):
    d = lax.axis_index("det")
    t = lax.axis_index("tm")
    forward = [jnp.asarray(a) for a in _forward_tables()]
    inverse = [jnp.asarray(a) for a in _inverse_tables()]
    band = jnp.where(t < BANDS, t, 2 * BANDS - 1 - t)
    where = jnp.stack([band, t, d * 16 + t]).astype(jnp.int32)
    paired = modes.reshape(BANDS, 16, 2, 128).transpose(0, 2, 1, 3).reshape(BANDS, 32, 128)
    paired_noise = noise_level.reshape(BANDS, 16, 2).transpose(0, 2, 1).reshape(BANDS, 32)
    scale = call(scales_kernel, ((24, 256), F32), smem=1)(where, paired_noise)
    send_tod, send_v = call(
        prep_kernel,
        [((16, 32, 256), F32), ((16, 64, 128), F32)],
        scratch=[pltpu.VMEM((512, 128), F32), pltpu.VMEM((512, 128), F32)],
        smem=1,
    )(where, tod, pointing, paired, paired_noise)
    got_tod = exchange(send_tod, "tm")
    got_v = exchange(send_v, "det")
    spectra = call(forward_kernel, ((512, 128), F32))(got_tod, scale, *forward)
    trans, gain = call(
        gram_kernel,
        [((2, 256, 256), F32), ((2, 256, 256), F32)],
        scratch=[pltpu.VMEM((2, 128, 128), F32)],
    )(got_v)
    mixed = exchange(spectra.reshape(256, 2, 128), ("det", "tm")).reshape(512, 128)
    weighted = call(apply_kernel, ((512, 128), F32), smem=1)(where, mixed, trans, gain)
    hits, owner, inner = call(
        hits_kernel, [((TPIX, 256), F32), ((256, 256), F32), ((256, 256), F32)]
    )(got_tod)
    back = exchange(weighted.reshape(256, 2, 128), ("det", "tm")).reshape(512, 128)
    series = call(inverse_kernel, ((16, 16, 256), F32))(back, scale, *inverse)
    got_series = exchange(series, "tm").reshape(256, 256)
    bins = call(sums_kernel, ((256, 128), F32))(series.reshape(256, 256), owner, inner, hits)
    filtered = call(
        spread_kernel, ((32, 2048), F32), scratch=[pltpu.VMEM((512, 128), F32)]
    )(got_series)
    got_bins = exchange(bins, ("det", "tm"))
    binned = call(finish_kernel, ((1, 128), F32))(got_bins)
    return filtered, binned[0, :TPIX]


def solution(mesh):
    placed = (P("det", "tm"), P("det", "tm"), P(None, "det"), P(None, "det", None))
    return jax.shard_map(
        steps,
        mesh=mesh,
        in_specs=placed,
        out_specs=(P("det", "tm"), P(("det", "tm"))),
        check_vma=False,
    )
```

time: 1430 us -> 195 us (0.14)
  other arithmetic: 955 us -> 0.66 us
  waiting for transfers between devices: 353 us -> 15.7 us
  Pallas kernels: 0 us -> 85.8 us
  matrix products: 26.6 us -> 0 us
  blocking collectives: 34 us -> 54.7 us
    scatter-add x2 -> x0, other arithmetic: 905 us -> none  [the longest x1 452 us: body(): jax.ops.segment_sum(filtered.reshape(-1), flat_pointing, num_segments=pix...]
    unnamed x3 -> x0, waiting for transfers between devices: 243 us -> none
    pallas_call x0 -> x10, Pallas kernels: none -> 85.8 us  [run(): pl.pallas_call(kernel, out_shape=shapes if many else shapes[0], in_specs=...]
    psum x1 -> x0, waiting for transfers between devices: 64.2 us -> none  [body(): proj_main, proj_side = lax.psum((proj_main, proj_side), 'det')]
    all_to_all x0 -> x2, blocking collectives: none -> 54.7 us  [exchange(): return lax.all_to_all(value, axes, split_axis=0, concat_axis=0, tiled=True)]
    another operation x12 -> x1, other arithmetic: 47.3 us -> 0.66 us  [steps(): where = jnp.stack([band, t, d * 16 + t]).astype(jnp.int32)]
    psum x1 -> x0, blocking collectives: 34 us -> none  [body(): proj_main, proj_side = lax.psum((proj_main, proj_side), 'det')]
    all_to_all x6 -> x4, waiting for transfers between devices: 45.8 us -> 15.7 us  [exchange(): return lax.all_to_all(value, axes, split_axis=0, concat_axis=0, tiled=True)]
  transfers between devices with their start and end apart: 8 -> 4, of which waited for: 7 -> 2; matrix products, arithmetic and copies ran while one was open for 33% -> 1% of each run, Pallas kernels for 0% -> 28%
where the time goes in v1:
time: 195 us; the launch traced here: 194 us
  Pallas kernels  85.8 us (44%)
  blocking collectives  54.7 us (28%)
  starting transfers between devices  30.1 us (15%)
  waiting for transfers between devices  15.7 us (8%)
  local copies, waits for them, and re-layouts  6.35 us (3%)
    pallas_call x10, Pallas kernels, run(): pl.pallas_call(kernel, out_shape=shapes if many else shapes[0], in_specs=...  85.8 us
    all_to_all x2, blocking collectives, exchange(): return lax.all_to_all(value, axes, split_axis=0, concat_axis=0, tiled=True)  54.7 us
    all_to_all x4, starting transfers between devices, exchange(): return lax.all_to_all(value, axes, split_axis=0, concat_axis=0, tiled=True)  30.1 us
    all_to_all x4, waiting for transfers between devices, exchange(): return lax.all_to_all(value, axes, split_axis=0, concat_axis=0, tiled=True)  15.7 us
  transfers between devices with their start and end apart: 4, of which 2 were waited for; matrix products, arithmetic and copies ran while one was open for 1% of the time, Pallas kernels for 28%

profile of v1, /device:TPU:1, one launch (start us, length us, event | category | flops | bytes accessed | tf_op | source)
XLA Modules:
  0.0 194.0 jit_solution(4534653911574210998)
XLA Ops:
  0.6 0.0 copy-start.4
  0.6 0.7 copy-done.4
  1.3 0.1 copy.22
  1.4 0.1 copy.23
  1.5 0.7 reshape.39.noise_ref
  2.2 1.6 copy.21
  3.7 0.7 pad_add_fusion.where_ref
  4.4 2.2 %shard_map.149 = (f32[16,32,256]{2,1,0:T(8,128)}, f32[16,64,128]{2,1,0:T(8,128)}) custom-call(s32[3]{0:T(128)} %pad_add_fusion.where_ref, f32[32,2048]{1,0:T(8,128)} %tod_ref.1, s32[32,2048]{1,0:T(8,128)} %point_ref.1, f32[8,32,128]{2,1,0:T(8,128)} %bitcast.28, f32[8,32]{1,0:T(8,128)} %reshape.39.noise_ref), custom_call_target="tpu_custom_call" | custom-call | tf_op jit(solution)/shard_map/pallas_call | solution.py:345
  6.6 27.3 %all_to_all.36.x_ref.point_ref = f32[16,32,256]{2,1,0:T(8,128)} all-to-all(f32[16,32,256]{2,1,0:T(8,128)} %get-tuple-element.9), channel_id=1, replica_groups=mesh['det'=16,'tm'=16] {'tm'}, dimensions={0} | all-to-all | bytes 1048576 | tf_op jit(solution)/shard_map/all_to_all | solution.py:357
  33.8 6.8 %all-to-all-start.2 = ((f32[16,64,128]{2,1,0:T(8,128)}), f32[16,64,128]{2,1,0:T(8,128)S(1)}, u32[]{:S(2)}, u32[]{:S(2)}) async-start(f32[16,64,128]{2,1,0:T(8,128)} %get-tuple-element.10), calls=%async_computation.2 | async-start | bytes 1048576 | tf_op jit(solution)/shard_map/all_to_all | solution.py:357
  40.6 1.4 shard_map.150.scale_ref
  42.0 3.3 %shard_map.151 = f32[512,128]{1,0:T(8,128)} custom-call(f32[16,32,256]{2,1,0:T(8,128)} %all_to_all.36.x_ref.point_ref, f32[24,256]{1,0:T(8,128)} %shard_map.150.scale_ref, f32[128,128]{1,0:T(8,128)} %constant.33.clone.first_ref, f32[256,128]{1,0:T(8,128)} %constant.34.clone.keep_ref, f32[256,128]{1,0:T(8,128)} %constant.35.clone.swap_ref, ...), custom_call_target="tpu_custom_call" | custom-call | tf_op jit(solution)/shard_map/pallas_call | solution.py:345
  45.3 6.7 %all-to-all-done.2.v_ref = f32[16,64,128]{2,1,0:T(8,128)S(1)} async-done(((f32[16,64,128]{2,1,0:T(8,128)}), f32[16,64,128]{2,1,0:T(8,128)S(1)}, u32[]{:S(2)}, u32[]{:S(2)}) %all-to-all-start.2) | async-done | bytes 524320 | tf_op jit(solution)/shard_map/all_to_all | solution.py:357
  51.9 0.0 copy-start
  51.9 5.8 %all-to-all-start.1 = ((f32[256,2,128]{2,1,0:T(2,128)}), f32[256,2,128]{2,1,0:T(2,128)S(1)}, u32[]{:S(2)}, u32[]{:S(2)}) async-start(f32[256,2,128]{2,1,0:T(2,128)} %bitcast.22), calls=%async_computation.1 | async-start | bytes 524288 | tf_op jit(solution)/shard_map/all_to_all | solution.py:357
  57.7 0.0 copy-done
  57.7 28.0 %shard_map.152 = (f32[2,256,256]{2,1,0:T(8,128)}, f32[2,256,256]{2,1,0:T(8,128)}) custom-call(f32[16,64,128]{2,1,0:T(8,128)} %copy-done), custom_call_target="tpu_custom_call" | custom-call | tf_op jit(solution)/shard_map/pallas_call | solution.py:345
  85.8 0.0 all-to-all-done.1
  85.8 0.0 copy-start.3
  85.8 0.7 copy-done.3
  86.5 3.9 %shard_map.153 = f32[512,128]{1,0:T(8,128)} custom-call(s32[3]{0:T(128)} %pad_add_fusion.where_ref, f32[512,128]{1,0:T(8,128)} %bitcast.25, f32[2,256,256]{2,1,0:T(8,128)} %get-tuple-element.11.trans_ref, f32[2,256,256]{2,1,0:T(8,128)} %get-tuple-element.12.gain_ref), custom_call_target="tpu_custom_call" | custom-call | tf_op jit(solution)/shard_map/pallas_call | solution.py:345
  90.4 13.7 %all-to-all-start.3 = ((f32[256,2,128]{2,1,0:T(2,128)}), f32[256,2,128]{2,1,0:T(2,128)S(1)}, u32[]{:S(2)}, u32[]{:S(2)}) async-start(f32[256,2,128]{2,1,0:T(2,128)} %bitcast.26), calls=%async_computation.3 | async-start | bytes 524288 | tf_op jit(solution)/shard_map/all_to_all | solution.py:357
  104.1 19.5 %shard_map.156 = (f32[48,256]{1,0:T(8,128)}, f32[256,256]{1,0:T(8,128)}, f32[256,256]{1,0:T(8,128)}) custom-call(f32[16,32,256]{2,1,0:T(8,128)} %all_to_all.36.x_ref.point_ref), custom_call_target="tpu_custom_call" | custom-call | tf_op jit(solution)/shard_map/pallas_call | solution.py:345
  123.6 0.0 all-to-all-done.3
  123.6 0.0 copy-start.2
  123.6 0.7 copy-done.2
  124.3 3.1 %shard_map.154 = f32[16,16,256]{2,1,0:T(8,128)} custom-call(f32[512,128]{1,0:T(8,128)} %bitcast.24, f32[24,256]{1,0:T(8,128)} %shard_map.150.scale_ref, f32[256,256]{1,0:T(8,128)} %constant.38.clone.top_ref, f32[256,256]{1,0:T(8,128)} %constant.39.clone.bottom_ref, f32[256,128]{1,0:T(8,128)} %constant.40.clone.keep_ref, f32[256,128]{1,0:T(8,128)} %constant.41.clone.swap_ref, ...), custom_call_target="tpu_custom_call" | custom-call | tf_op jit(solution)/shard_map/pallas_call | solution.py:345
  127.3 21.3 %shard_map.157 = f32[256,128]{1,0:T(8,128)} custom-call(f32[256,256]{1,0:T(8,128)} %bitcast.13.value_ref, f32[256,256]{1,0:T(8,128)} %get-tuple-element.13.owner_ref, f32[256,256]{1,0:T(8,128)} %get-tuple-element.14.inner_ref, f32[48,256]{1,0:T(8,128)} %get-tuple-element.15.hits_ref), custom_call_target="tpu_custom_call" | custom-call | tf_op jit(solution)/shard_map/pallas_call | solution.py:345
  148.6 27.4 %all_to_all.37 = f32[256,1,128]{2,1,0:T(1,128)} all-to-all(f32[256,1,128]{2,1,0:T(1,128)} %bitcast.29), channel_id=1, replica_groups=mesh['det'=16,'tm'=16] {'det','tm'}, dimensions={0} | all-to-all | bytes 262144 | tf_op jit(solution)/shard_map/all_to_all | solution.py:357
  176.0 3.9 %all-to-all-start.4 = ((f32[16,16,256]{2,1,0:T(8,128)}), f32[16,16,256]{2,1,0:T(8,128)S(1)}, u32[]{:S(2)}, u32[]{:S(2)}) async-start(f32[16,16,256]{2,1,0:T(8,128)} %shard_map.154), calls=%async_computation.4 | async-start | bytes 524288 | tf_op jit(solution)/shard_map/all_to_all | solution.py:357
  179.9 1.5 shard_map.158
  181.4 1.2 slice_bitcast_fusion
  182.6 9.0 %all-to-all-done.4 = f32[16,16,256]{2,1,0:T(8,128)S(1)} async-done(((f32[16,16,256]{2,1,0:T(8,128)}), f32[16,16,256]{2,1,0:T(8,128)S(1)}, u32[]{:S(2)}, u32[]{:S(2)}) %all-to-all-start.4) | async-done | bytes 262176 | tf_op jit(solution)/shard_map/all_to_all | solution.py:357
  191.6 0.0 copy-start.1
  191.6 0.7 copy-done.1
  192.3 1.7 shard_map.155
Async XLA Ops:
  0.6 0.7 copy-start.4
  33.8 18.1 %all-to-all-start.2 = ((f32[16,64,128]{2,1,0:T(8,128)}), f32[16,64,128]{2,1,0:T(8,128)S(1)}, u32[]{:S(2)}, u32[]{:S(2)}) async-start(f32[16,64,128]{2,1,0:T(8,128)} %get-tuple-element.10), calls=%async_computation.2 | async-start | bytes 1048576 | tf_op jit(solution)/shard_map/all_to_all | solution.py:357
  51.9 5.8 %copy-start = (f32[16,64,128]{2,1,0:T(8,128)}, f32[16,64,128]{2,1,0:T(8,128)S(1)}, u32[]{:S(2)}) copy-start(f32[16,64,128]{2,1,0:T(8,128)S(1)} %all-to-all-done.2.v_ref) | copy-start | bytes 1572868
  51.9 33.8 %all-to-all-start.1 = ((f32[256,2,128]{2,1,0:T(2,128)}), f32[256,2,128]{2,1,0:T(2,128)S(1)}, u32[]{:S(2)}, u32[]{:S(2)}) async-start(f32[256,2,128]{2,1,0:T(2,128)} %bitcast.22), calls=%async_computation.1 | async-start | bytes 524288 | tf_op jit(solution)/shard_map/all_to_all | solution.py:357
  85.8 0.7 copy-start.3
  90.4 33.2 %all-to-all-start.3 = ((f32[256,2,128]{2,1,0:T(2,128)}), f32[256,2,128]{2,1,0:T(2,128)S(1)}, u32[]{:S(2)}, u32[]{:S(2)}) async-start(f32[256,2,128]{2,1,0:T(2,128)} %bitcast.26), calls=%async_computation.3 | async-start | bytes 524288 | tf_op jit(solution)/shard_map/all_to_all | solution.py:357
  123.6 0.7 copy-start.2
  176.0 15.6 %all-to-all-start.4 = ((f32[16,16,256]{2,1,0:T(8,128)}), f32[16,16,256]{2,1,0:T(8,128)S(1)}, u32[]{:S(2)}, u32[]{:S(2)}) async-start(f32[16,16,256]{2,1,0:T(8,128)} %shard_map.154), calls=%async_computation.4 | async-start | bytes 524288 | tf_op jit(solution)/shard_map/all_to_all | solution.py:357
  191.6 0.7 copy-start.1

commit v2 on v1

--- a/solution.py
+++ b/solution.py
@@ -91,7 +91,37 @@
     return lax.broadcasted_iota(jnp.int32, shape, 1)
 
 
-def prep_kernel(where_ref, tod_ref, point_ref, modes_ref, noise_ref, tod_out, v_out, tod_tmp, point_tmp):
+def _position():
+    return lax.axis_index("det"), lax.axis_index("tm")
+
+
+def basis_kernel(modes_ref, noise_ref, v_out, scale_out, tmp_ref):
+    _, pos = _position()
+    band = jnp.where(pos < BANDS, pos, 2 * BANDS - 1 - pos)
+    root = lax.rsqrt(noise_ref[...])
+    eye = lax.broadcasted_iota(jnp.int32, (32, 32), 0) == _lanes((32, 32))
+    row_of = lax.broadcasted_iota(jnp.int32, (BANDS, 32), 0)
+    for part, which in enumerate((band, BANDS - 1)):
+        row = jnp.sum(jnp.where(row_of == which, root, 0.0), axis=0, keepdims=True)
+        col = jnp.sum(jnp.where(eye, row, 0.0), axis=1, keepdims=True)
+        tmp_ref[part] = modes_ref[which] * col
+        for e in range(2):
+            vee = tmp_ref[part, pl.ds(e, 16, stride=2), :]
+            low = 32 * part + 16 * e
+            for dest in range(16):
+                v_out[dest, low : low + 16, :] = vee
+    flipped = jnp.concatenate([root[BANDS - 1 - j : BANDS - j] for j in range(BANDS)], axis=0)
+    for e in range(2):
+        mask = _lanes((BANDS, 32)) == 2 * pos + e
+        lanes = pl.ds(128 * e, 128)
+        up = jnp.sum(jnp.where(mask, root, 0.0), axis=1, keepdims=True)
+        down = jnp.sum(jnp.where(mask, flipped, 0.0), axis=1, keepdims=True)
+        scale_out[0:8, lanes] = jnp.broadcast_to(up, (8, 128))
+        scale_out[8:16, lanes] = jnp.broadcast_to(down, (8, 128))
+        scale_out[16:24, lanes] = jnp.broadcast_to(up[7:8], (8, 128))
+
+
+def prep_kernel(tod_ref, point_ref, tod_out, tod_tmp, point_tmp):
     for octet in range(4):
         for r in range(8):
             for h in range(2):
@@ -104,31 +134,6 @@
         part = slice(256 * h, 256 * h + 256)
         tod_out[:, 0:16, cols] = tod_tmp[part, :].reshape(16, 16, 128)
         tod_out[:, 16:32, cols] = point_tmp[part, :].reshape(16, 16, 128)
-    band = where_ref[0]
-    root = lax.rsqrt(noise_ref[...])
-    eye = lax.broadcasted_iota(jnp.int32, (32, 32), 0) == _lanes((32, 32))
-    row_of = lax.broadcasted_iota(jnp.int32, (BANDS, 32), 0)
-    for part, which in enumerate((band, BANDS - 1)):
-        row = jnp.sum(jnp.where(row_of == which, root, 0.0), axis=0, keepdims=True)
-        col = jnp.sum(jnp.where(eye, row, 0.0), axis=1, keepdims=True)
-        vee = modes_ref[which] * col
-        for dest in range(16):
-            v_out[dest, 32 * part : 32 * part + 32, :] = vee
-
-
-def scales_kernel(where_ref, noise_ref, scale_out):
-    pos = where_ref[1]
-    root = lax.rsqrt(noise_ref[...])
-    noise_ref_lane = _lanes((BANDS, 32))
-    flipped = jnp.concatenate([root[BANDS - 1 - j : BANDS - j] for j in range(BANDS)], axis=0)
-    for e in range(2):
-        mask = noise_ref_lane == 16 * e + pos
-        lanes = pl.ds(128 * e, 128)
-        up = jnp.sum(jnp.where(mask, root, 0.0), axis=1, keepdims=True)
-        down = jnp.sum(jnp.where(mask, flipped, 0.0), axis=1, keepdims=True)
-        scale_out[0:8, lanes] = jnp.broadcast_to(up, (8, 128))
-        scale_out[8:16, lanes] = jnp.broadcast_to(down, (8, 128))
-        scale_out[16:24, lanes] = jnp.broadcast_to(up[7:8], (8, 128))
 
 
 def _first_scale(scale_ref):
@@ -173,6 +178,72 @@
             out_ref[pl.ds(32 * d + 16 + e, 8, stride=2), :] = down[:, cols]
 
 
+def _pair_inverse(a, b, c):
+    r = 1.0 / (a * c - b * b)
+    return c * r, -b * r, a * r
+
+
+def _quad_inverse(m):
+    a0, a1, a2 = _pair_inverse(m[0][0], m[0][1], m[1][1])
+    w00 = a0 * m[0][2] + a1 * m[1][2]
+    w01 = a0 * m[0][3] + a1 * m[1][3]
+    w10 = a1 * m[0][2] + a2 * m[1][2]
+    w11 = a1 * m[0][3] + a2 * m[1][3]
+    q0, q1, q2 = _pair_inverse(
+        m[2][2] - (m[0][2] * w00 + m[1][2] * w10),
+        m[2][3] - (m[0][2] * w01 + m[1][2] * w11),
+        m[3][3] - (m[0][3] * w01 + m[1][3] * w11),
+    )
+    x00 = -(w00 * q0 + w01 * q1)
+    x01 = -(w00 * q1 + w01 * q2)
+    x10 = -(w10 * q0 + w11 * q1)
+    x11 = -(w10 * q1 + w11 * q2)
+    i00 = a0 - (x00 * w00 + x01 * w01)
+    i01 = a1 - (x00 * w10 + x01 * w11)
+    i11 = a2 - (x10 * w10 + x11 * w11)
+    return [
+        [i00, i01, x00, x01],
+        [i01, i11, x10, x11],
+        [x00, x10, q0, q1],
+        [x01, x11, q1, q2],
+    ]
+
+
+def invert_in_place(mats_ref):
+    lane = _lanes((128, 128))
+    lane8 = _lanes((8, 128))
+
+    def step(panel, carry):
+        base = 4 * panel
+        within = (lane >= base) & (lane < base + 4)
+        index = [jnp.full((128, 128), base + j, jnp.int32) for j in range(4)]
+        for part in range(2):
+            mat = mats_ref[part]
+            rows = [
+                jnp.broadcast_to(mats_ref[part, pl.ds(base + j, 1), :], (8, 128)) for j in range(4)
+            ]
+            pivots = [
+                [jnp.take_along_axis(rows[i], index[j][:8], axis=1) for j in range(4)]
+                for i in range(4)
+            ]
+            inverse = _quad_inverse(pivots)
+            new = jnp.where(within, 0.0, mat)
+            scaled = []
+            for i in range(4):
+                row = sum(inverse[i][j] * rows[j] for j in range(4))
+                for j in range(4):
+                    row = jnp.where(lane8 == base + j, inverse[i][j], row)
+                scaled.append(row)
+                col = jnp.take_along_axis(mat, index[i], axis=1)
+                new = new - col * jnp.concatenate([row] * 16, axis=0)
+            mats_ref[part] = new
+            for i in range(4):
+                mats_ref[part, pl.ds(base + i, 1), :] = scaled[i][0:1]
+        return carry
+
+    lax.fori_loop(0, 32, step, 0)
+
+
 def gram_kernel(v_ref, trans_ref, gain_ref, mats_ref):
     parts = []
     for e in range(2):
@@ -188,24 +259,7 @@
             + _dot_tn(parts[0][part], parts[0][part])
             + _dot_tn(parts[1][part], parts[1][part])
         )
-    lane = _lanes((1, 128))
-    sub = lax.broadcasted_iota(jnp.int32, (128, 1), 0)
-
-    def step(k, carry):
-        here = lane == k
-        there = sub == k
-        for part in range(2):
-            mat = mats_ref[part]
-            row = mats_ref[part, pl.ds(k, 1), :]
-            pivot = jnp.sum(jnp.where(here, row, 0.0), axis=1, keepdims=True)
-            inverse = 1.0 / pivot
-            col = jnp.sum(jnp.where(here, mat, 0.0), axis=1, keepdims=True)
-            scaled = jnp.where(here, inverse, row * inverse)
-            cleared = jnp.where(here, 0.0, mat)
-            mats_ref[part] = jnp.where(there, scaled, cleared - col * scaled)
-        return carry
-
-    lax.fori_loop(0, 128, step, 0)
+    invert_in_place(mats_ref)
     for e in range(2):
         trans_ref[e] = jnp.concatenate([parts[e][0], parts[e][1]], axis=1).T
         gain_ref[e] = jnp.concatenate(
@@ -213,10 +267,11 @@
         )
 
 
-def apply_kernel(where_ref, x_ref, trans_ref, gain_ref, out_ref):
+def apply_kernel(x_ref, trans_ref, gain_ref, out_ref):
     xs = [x_ref[pl.ds(e, 256, stride=2), :] for e in range(2)]
     proj = _dot(trans_ref[0], xs[0]) + _dot(trans_ref[1], xs[1])
-    special = (_lanes((256, 128)) == 64) & (where_ref[2] == 0)
+    dev, pos = _position()
+    special = (_lanes((256, 128)) == 64) & (dev * 16 + pos == 0)
     second = lax.broadcasted_iota(jnp.int32, (256, 128), 0) >= 128
     proj = jnp.where(special == second, proj, 0.0)
     for e in range(2):
@@ -263,57 +318,75 @@
         out_ref[:, 8 * e : 8 * e + 8, :] = x.reshape(16, 8, N2)
 
 
-def split_pixel(point):
-    owner = jnp.floor((point + 0.5) * (1.0 / TPIX))
-    return owner, point - owner * TPIX
-
-
 def _one_hot(row, count):
     index = lax.broadcasted_iota(jnp.int32, (count, 256), 0).astype(F32).astype(BF16)
     return index == jnp.broadcast_to(row, (count, 256)).astype(BF16)
 
 
-def hits_kernel(point_ref, out_ref, owner_ref, inner_ref):
-    owner, inner = split_pixel(point_ref[:, 16:32, :].reshape(256, 256))
-    owner_ref[...] = owner
-    inner_ref[...] = inner
-    one = jnp.ones((), BF16)
-    zero = jnp.zeros((), BF16)
+def _pick(mask, row, count):
+    return jnp.where(mask, jnp.broadcast_to(row, (count, 256)).astype(BF16), jnp.zeros((), BF16))
+
+
+def _tally(small, big):
+    return lax.dot_general(small, big, (((1,), (1,)), ((), ())), preferred_element_type=F32)
+
+
+def _tiles(grid_ref, shift, out_fn):
+    lane = _lanes((32, 128))
+    rows = [grid_ref[pl.ds(r, 32, stride=3), :] for r in range(3)]
+
+    def turned(value, amount):
+        amount %= 128
+        return pltpu.roll(value, amount, 1) if amount else value
+
+    for j in range(8):
+        first, offset = divmod(TPIX * j, 128)
+        value = turned(rows[first], shift - offset)
+        if offset + TPIX > 128:
+            rest = turned(rows[first + 1], shift + 128 - offset)
+            value = jnp.where(lane < shift + 128 - offset, value, rest)
+        keep = (lane >= shift) & (lane < shift + TPIX)
+        out_fn(pl.ds(j, 32, stride=8), jnp.where(keep, value, 0.0))
+
+
+def hits_kernel(point_ref, out_ref, high_ref, low_ref, grid_ref):
+    point = point_ref[:, 16:32, :].reshape(256, 256)
+    high = jnp.floor(point * (1.0 / 128))
+    high_ref[...] = high
+    low_ref[...] = point - 128.0 * high
+    one = jnp.ones((1, 256), F32)
 
     def step(r, acc):
-        big = jnp.where(_one_hot(owner_ref[pl.ds(r, 1), :], 256), one, zero)
-        small = jnp.where(_one_hot(inner_ref[pl.ds(r, 1), :], TPIX), one, zero)
-        return acc + lax.dot_general(
-            small, big, (((1,), (1,)), ((), ())), preferred_element_type=F32
-        )
-
-    out_ref[...] = lax.fori_loop(0, 256, step, jnp.zeros((TPIX, 256), F32), unroll=4)
-
-
-def sums_kernel(value_ref, owner_ref, inner_ref, hits_ref, out_ref):
-    zero = jnp.zeros((), BF16)
+        big = _pick(_one_hot(low_ref[pl.ds(r, 1), :], 128), one, 128)
+        small = _pick(_one_hot(high_ref[pl.ds(r, 1), :], 96), one, 96)
+        return acc + _tally(small, big)
+
+    grid_ref[...] = lax.fori_loop(0, 256, step, jnp.zeros((96, 128), F32), unroll=32)
+
+    def put(rows, value):
+        out_ref[rows, :] = value
+
+    _tiles(grid_ref, TPIX, put)
+
+
+def sums_kernel(value_ref, high_ref, low_ref, hits_ref, out_ref, grid_ref):
+    one = jnp.ones((1, 256), F32)
 
     def step(r, acc):
         value = value_ref[pl.ds(r, 1), :]
-        high = value.astype(BF16)
-        low = (value - high.astype(F32)).astype(BF16)
-        big = jnp.where(_one_hot(owner_ref[pl.ds(r, 1), :], 256), jnp.ones((), BF16), zero)
-        pick = _one_hot(inner_ref[pl.ds(r, 1), :], TPIX)
-        small = jnp.concatenate(
-            [
-                jnp.where(pick, jnp.broadcast_to(high.astype(F32), (TPIX, 256)).astype(BF16), zero),
-                jnp.where(pick, jnp.broadcast_to(low.astype(F32), (TPIX, 256)).astype(BF16), zero),
-            ],
-            axis=0,
-        )
-        return acc + lax.dot_general(
-            small, big, (((1,), (1,)), ((), ())), preferred_element_type=F32
-        )
-
-    acc = lax.fori_loop(0, 256, step, jnp.zeros((2 * TPIX, 256), F32), unroll=4)
-    sums = acc[:TPIX] + acc[TPIX:]
-    full = jnp.concatenate([sums, hits_ref[...], jnp.zeros((32, 256), F32)], axis=0)
-    out_ref[...] = full.T
+        upper = value.astype(BF16).astype(F32)
+        big = _pick(_one_hot(low_ref[pl.ds(r, 1), :], 128), one, 128)
+        mask = _one_hot(high_ref[pl.ds(r, 1), :], 96)
+        small = jnp.concatenate([_pick(mask, upper, 96), _pick(mask, value - upper, 96)], axis=0)
+        return acc + _tally(small, big)
+
+    acc = lax.fori_loop(0, 256, step, jnp.zeros((192, 128), F32), unroll=32)
+    grid_ref[...] = acc[:96] + acc[96:]
+
+    def put(rows, value):
+        out_ref[rows, :] = value + hits_ref[rows, :]
+
+    _tiles(grid_ref, 0, put)
 
 
 def spread_kernel(x_ref, out_ref, tmp_ref):
@@ -330,14 +403,13 @@
 def finish_kernel(x_ref, out_ref):
     total = jnp.sum(x_ref[...], axis=0, keepdims=True)
     hits = pltpu.roll(total, 128 - TPIX, 1)
-    out_ref[...] = total / jnp.sqrt(1.0 + hits)
+    out_ref[...] = (total / jnp.sqrt(1.0 + hits))[:, :TPIX]
 
 
 VMEM = pl.BlockSpec(memory_space=pltpu.VMEM)
-SMEM = pl.BlockSpec(memory_space=pltpu.SMEM)
-
-
-def call(kernel, outs, scratch=(), smem=0):
+
+
+def call(kernel, outs, scratch=()):
     many = isinstance(outs, list)
     shapes = [jax.ShapeDtypeStruct(s, d) for s, d in (outs if many else [outs])]
 
@@ -345,7 +417,7 @@
         return pl.pallas_call(
             kernel,
             out_shape=shapes if many else shapes[0],
-            in_specs=[SMEM] * smem + [VMEM] * (len(args) - smem),
+            in_specs=[VMEM] * len(args),
             out_specs=[VMEM] * len(shapes) if many else VMEM,
             scratch_shapes=list(scratch),
         )(*args)
@@ -358,23 +430,20 @@
 
 
 def steps(tod, pointing, noise_level, modes):
-    d = lax.axis_index("det")
-    t = lax.axis_index("tm")
     forward = [jnp.asarray(a) for a in _forward_tables()]
     inverse = [jnp.asarray(a) for a in _inverse_tables()]
-    band = jnp.where(t < BANDS, t, 2 * BANDS - 1 - t)
-    where = jnp.stack([band, t, d * 16 + t]).astype(jnp.int32)
-    paired = modes.reshape(BANDS, 16, 2, 128).transpose(0, 2, 1, 3).reshape(BANDS, 32, 128)
-    paired_noise = noise_level.reshape(BANDS, 16, 2).transpose(0, 2, 1).reshape(BANDS, 32)
-    scale = call(scales_kernel, ((24, 256), F32), smem=1)(where, paired_noise)
-    send_tod, send_v = call(
+    send_v, scale = call(
+        basis_kernel,
+        [((16, 64, 128), F32), ((24, 256), F32)],
+        scratch=[pltpu.VMEM((2, 32, 128), F32)],
+    )(modes, noise_level)
+    send_tod = call(
         prep_kernel,
-        [((16, 32, 256), F32), ((16, 64, 128), F32)],
+        ((16, 32, 256), F32),
         scratch=[pltpu.VMEM((512, 128), F32), pltpu.VMEM((512, 128), F32)],
-        smem=1,
-    )(where, tod, pointing, paired, paired_noise)
+    )(tod, pointing)
+    got_v = exchange(send_v, "det")
     got_tod = exchange(send_tod, "tm")
-    got_v = exchange(send_v, "det")
     spectra = call(forward_kernel, ((512, 128), F32))(got_tod, scale, *forward)
     trans, gain = call(
         gram_kernel,
@@ -382,20 +451,24 @@
         scratch=[pltpu.VMEM((2, 128, 128), F32)],
     )(got_v)
     mixed = exchange(spectra.reshape(256, 2, 128), ("det", "tm")).reshape(512, 128)
-    weighted = call(apply_kernel, ((512, 128), F32), smem=1)(where, mixed, trans, gain)
-    hits, owner, inner = call(
-        hits_kernel, [((TPIX, 256), F32), ((256, 256), F32), ((256, 256), F32)]
+    weighted = call(apply_kernel, ((512, 128), F32))(mixed, trans, gain)
+    hits, high, low = call(
+        hits_kernel,
+        [((256, 128), F32), ((256, 256), F32), ((256, 256), F32)],
+        scratch=[pltpu.VMEM((96, 128), F32)],
     )(got_tod)
     back = exchange(weighted.reshape(256, 2, 128), ("det", "tm")).reshape(512, 128)
     series = call(inverse_kernel, ((16, 16, 256), F32))(back, scale, *inverse)
     got_series = exchange(series, "tm").reshape(256, 256)
-    bins = call(sums_kernel, ((256, 128), F32))(series.reshape(256, 256), owner, inner, hits)
+    bins = call(
+        sums_kernel, ((256, 128), F32), scratch=[pltpu.VMEM((96, 128), F32)]
+    )(series.reshape(256, 256), high, low, hits)
     filtered = call(
         spread_kernel, ((32, 2048), F32), scratch=[pltpu.VMEM((512, 128), F32)]
     )(got_series)
     got_bins = exchange(bins, ("det", "tm"))
-    binned = call(finish_kernel, ((1, 128), F32))(got_bins)
-    return filtered, binned[0, :TPIX]
+    binned = call(finish_kernel, ((1, TPIX), F32))(got_bins)
+    return filtered, binned.reshape(TPIX)
 
 
 def solution(mesh):

time: 195 us -> 156 us (0.80)
  Pallas kernels: 85.8 us -> 49.7 us
  blocking collectives: 54.7 us -> 20.3 us
  waiting for transfers between devices: 15.7 us -> 42.9 us
  starting transfers between devices: 30.1 us -> 38.5 us
  local copies, waits for them, and re-layouts: 6.35 us -> 2.89 us
    pallas_call x10, Pallas kernels: 85.8 us -> 49.7 us  [run(): pl.pallas_call(kernel, out_shape=shapes if many else shapes[0], in_specs=...]
    all_to_all x2 -> x1, blocking collectives: 54.7 us -> 20.3 us  [exchange(): return lax.all_to_all(value, axes, split_axis=0, concat_axis=0, tiled=True)]
    all_to_all x4 -> x5, waiting for transfers between devices: 15.7 us -> 42.9 us  [exchange(): return lax.all_to_all(value, axes, split_axis=0, concat_axis=0, tiled=True)]
    all_to_all x4 -> x5, starting transfers between devices: 30.1 us -> 38.5 us  [exchange(): return lax.all_to_all(value, axes, split_axis=0, concat_axis=0, tiled=True)]
    reshape x2 -> x0, local copies, waits for them, and re-layouts: 2.24 us -> none  [the longest x1 1.57 us: steps(): modes.reshape(BANDS, 16, 2, 128).transpose(0, 2, 1, 3)]
  transfers between devices with their start and end apart: 4 -> 5, of which waited for: 2 -> 5; matrix products, arithmetic and copies ran while one was open for 1% -> 0% of each run, Pallas kernels for 28% -> 19%
where the time goes in v2:
time: 156 us; the launch traced here: 155 us
  Pallas kernels  49.7 us (32%)
  waiting for transfers between devices  42.9 us (28%)
  starting transfers between devices  38.5 us (25%)
  blocking collectives  20.3 us (13%)
  local copies, waits for them, and re-layouts  2.89 us (2%)
    pallas_call x10, Pallas kernels, run(): pl.pallas_call(kernel, out_shape=shapes if many else shapes[0], in_specs=...  49.7 us
    all_to_all x5, waiting for transfers between devices, exchange(): return lax.all_to_all(value, axes, split_axis=0, concat_axis=0, tiled=True)  42.9 us
    all_to_all x5, starting transfers between devices, exchange(): return lax.all_to_all(value, axes, split_axis=0, concat_axis=0, tiled=True)  38.5 us
    all_to_all x1, blocking collectives, exchange(): return lax.all_to_all(value, axes, split_axis=0, concat_axis=0, tiled=True)  20.3 us
  transfers between devices with their start and end apart: 5, of which 5 were waited for; matrix products, arithmetic and copies ran while one was open for 0% of the time, Pallas kernels for 19%

profile of v2, /device:TPU:1, one launch (start us, length us, event | category | flops | bytes accessed | tf_op | source)
XLA Modules:
  0.0 154.9 jit_solution(10211584836873797268)
XLA Ops:
  0.6 1.9 %shard_map.149 = f32[16,32,256]{2,1,0:T(8,128)} custom-call(f32[32,2048]{1,0:T(8,128)} %tod_ref.1, s32[32,2048]{1,0:T(8,128)} %point_ref.1), custom_call_target="tpu_custom_call" | custom-call | tf_op jit(solution)/shard_map/pallas_call | solution.py:417
  2.6 10.0 %all-to-all-start = ((f32[16,32,256]{2,1,0:T(8,128)}), f32[16,32,256]{2,1,0:T(8,128)S(1)}, u32[]{:S(2)}, u32[]{:S(2)}) async-start(f32[16,32,256]{2,1,0:T(8,128)} %shard_map.149), calls=%async_computation | async-start | bytes 1048576 | tf_op jit(solution)/shard_map/all_to_all | solution.py:429
  12.5 1.9 %shard_map.150 = (f32[16,64,128]{2,1,0:T(8,128)}, f32[24,256]{1,0:T(8,128)}) custom-call(f32[8,32,128]{2,1,0:T(8,128)} %modes_ref.1, f32[8,32]{1,0:T(8,128)} %noise_ref.1), custom_call_target="tpu_custom_call" | custom-call | tf_op jit(solution)/shard_map/pallas_call | solution.py:417
  14.4 15.3 %all-to-all-done.x_ref.point_ref = f32[16,32,256]{2,1,0:T(8,128)S(1)} async-done(((f32[16,32,256]{2,1,0:T(8,128)}), f32[16,32,256]{2,1,0:T(8,128)S(1)}, u32[]{:S(2)}, u32[]{:S(2)}) %all-to-all-start) | async-done | bytes 524320 | tf_op jit(solution)/shard_map/all_to_all | solution.py:429
  29.7 0.0 copy-start
  29.7 0.8 copy-done
  30.5 6.8 %all-to-all-start.2 = ((f32[16,64,128]{2,1,0:T(8,128)}), f32[16,64,128]{2,1,0:T(8,128)S(1)}, u32[]{:S(2)}, u32[]{:S(2)}) async-start(f32[16,64,128]{2,1,0:T(8,128)} %get-tuple-element.10), calls=%async_computation.2 | async-start | bytes 1048576 | tf_op jit(solution)/shard_map/all_to_all | solution.py:429
  37.3 3.3 %shard_map.151 = f32[512,128]{1,0:T(8,128)} custom-call(f32[16,32,256]{2,1,0:T(8,128)} %copy-done, f32[24,256]{1,0:T(8,128)} %get-tuple-element.9.scale_ref, f32[128,128]{1,0:T(8,128)} %constant.20.clone.first_ref, f32[256,128]{1,0:T(8,128)} %constant.21.clone.keep_ref, f32[256,128]{1,0:T(8,128)} %constant.22.clone.swap_ref, ...), custom_call_target="tpu_custom_call" | custom-call | tf_op jit(solution)/shard_map/pallas_call | solution.py:417
  40.6 8.0 %all-to-all-done.2.v_ref = f32[16,64,128]{2,1,0:T(8,128)S(1)} async-done(((f32[16,64,128]{2,1,0:T(8,128)}), f32[16,64,128]{2,1,0:T(8,128)S(1)}, u32[]{:S(2)}, u32[]{:S(2)}) %all-to-all-start.2) | async-done | bytes 524320 | tf_op jit(solution)/shard_map/all_to_all | solution.py:429
  48.6 0.0 copy-start.1
  48.6 5.8 %all-to-all-start.1 = ((f32[256,2,128]{2,1,0:T(2,128)}), f32[256,2,128]{2,1,0:T(2,128)S(1)}, u32[]{:S(2)}, u32[]{:S(2)}) async-start(f32[256,2,128]{2,1,0:T(2,128)} %bitcast.11), calls=%async_computation.1 | async-start | bytes 524288 | tf_op jit(solution)/shard_map/all_to_all | solution.py:429
  54.4 0.0 copy-done.1
  54.4 14.3 %shard_map.152 = (f32[2,256,256]{2,1,0:T(8,128)}, f32[2,256,256]{2,1,0:T(8,128)}) custom-call(f32[16,64,128]{2,1,0:T(8,128)} %copy-done.1), custom_call_target="tpu_custom_call" | custom-call | tf_op jit(solution)/shard_map/pallas_call | solution.py:417
  68.8 1.6 %all-to-all-done.1 = f32[256,2,128]{2,1,0:T(2,128)S(1)} async-done(((f32[256,2,128]{2,1,0:T(2,128)}), f32[256,2,128]{2,1,0:T(2,128)S(1)}, u32[]{:S(2)}, u32[]{:S(2)}) %all-to-all-start.1) | async-done | bytes 262176 | tf_op jit(solution)/shard_map/all_to_all | solution.py:429
  70.4 0.0 copy-start.4
  70.4 0.7 copy-done.4
  71.1 3.9 %shard_map.153 = f32[512,128]{1,0:T(8,128)} custom-call(f32[512,128]{1,0:T(8,128)} %bitcast.14, f32[2,256,256]{2,1,0:T(8,128)} %get-tuple-element.11.trans_ref, f32[2,256,256]{2,1,0:T(8,128)} %get-tuple-element.12.gain_ref), custom_call_target="tpu_custom_call" | custom-call | tf_op jit(solution)/shard_map/pallas_call | solution.py:417
  74.9 12.1 %all-to-all-start.3 = ((f32[256,2,128]{2,1,0:T(2,128)}), f32[256,2,128]{2,1,0:T(2,128)S(1)}, u32[]{:S(2)}, u32[]{:S(2)}) async-start(f32[256,2,128]{2,1,0:T(2,128)} %bitcast.15), calls=%async_computation.3 | async-start | bytes 524288 | tf_op jit(solution)/shard_map/all_to_all | solution.py:429
  87.1 8.3 %shard_map.156 = (f32[256,128]{1,0:T(8,128)}, f32[256,256]{1,0:T(8,128)}, f32[256,256]{1,0:T(8,128)}) custom-call(f32[16,32,256]{2,1,0:T(8,128)} %copy-done), custom_call_target="tpu_custom_call" | custom-call | tf_op jit(solution)/shard_map/pallas_call | solution.py:417
  95.3 7.7 %all-to-all-done.3 = f32[256,2,128]{2,1,0:T(2,128)S(1)} async-done(((f32[256,2,128]{2,1,0:T(2,128)}), f32[256,2,128]{2,1,0:T(2,128)S(1)}, u32[]{:S(2)}, u32[]{:S(2)}) %all-to-all-start.3) | async-done | bytes 262176 | tf_op jit(solution)/shard_map/all_to_all | solution.py:429
  103.0 0.0 copy-start.3
  103.0 0.7 copy-done.3
  103.7 3.1 %shard_map.154 = f32[16,16,256]{2,1,0:T(8,128)} custom-call(f32[512,128]{1,0:T(8,128)} %bitcast.13, f32[24,256]{1,0:T(8,128)} %get-tuple-element.9.scale_ref, f32[256,256]{1,0:T(8,128)} %constant.25.clone.top_ref, f32[256,256]{1,0:T(8,128)} %constant.26.clone.bottom_ref, f32[256,128]{1,0:T(8,128)} %constant.27.clone.keep_ref, ...), custom_call_target="tpu_custom_call" | custom-call | tf_op jit(solution)/shard_map/pallas_call | solution.py:417
  106.8 9.8 %shard_map.157 = f32[256,128]{1,0:T(8,128)} custom-call(f32[256,256]{1,0:T(8,128)} %bitcast.5.value_ref, f32[256,256]{1,0:T(8,128)} %get-tuple-element.13.high_ref, f32[256,256]{1,0:T(8,128)} %get-tuple-element.14.low_ref, f32[256,128]{1,0:T(8,128)} %get-tuple-element.15.hits_ref), custom_call_target="tpu_custom_call" | custom-call | tf_op jit(solution)/shard_map/pallas_call | solution.py:417
  116.6 20.3 %all_to_all.36 = f32[256,1,128]{2,1,0:T(1,128)} all-to-all(f32[256,1,128]{2,1,0:T(1,128)} %bitcast.17), channel_id=1, replica_groups=mesh['det'=16,'tm'=16] {'det','tm'}, dimensions={0} | all-to-all | bytes 262144 | tf_op jit(solution)/shard_map/all_to_all | solution.py:429
  136.8 3.9 %all-to-all-start.4 = ((f32[16,16,256]{2,1,0:T(8,128)}), f32[16,16,256]{2,1,0:T(8,128)S(1)}, u32[]{:S(2)}, u32[]{:S(2)}) async-start(f32[16,16,256]{2,1,0:T(8,128)} %shard_map.154), calls=%async_computation.4 | async-start | bytes 524288 | tf_op jit(solution)/shard_map/all_to_all | solution.py:429
  140.7 1.5 shard_map.158
  142.2 10.2 %all-to-all-done.4 = f32[16,16,256]{2,1,0:T(8,128)S(1)} async-done(((f32[16,16,256]{2,1,0:T(8,128)}), f32[16,16,256]{2,1,0:T(8,128)S(1)}, u32[]{:S(2)}, u32[]{:S(2)}) %all-to-all-start.4) | async-done | bytes 262176 | tf_op jit(solution)/shard_map/all_to_all | solution.py:429
  152.5 0.0 copy-start.2
  152.5 0.7 copy-done.2
  153.2 1.7 %shard_map.155 = f32[32,2048]{1,0:T(8,128)} custom-call(f32[256,256]{1,0:T(8,128)} %bitcast.12), custom_call_target="tpu_custom_call" | custom-call | tf_op jit(solution)/shard_map/pallas_call | solution.py:417
Async XLA Ops:
  2.6 27.2 %all-to-all-start = ((f32[16,32,256]{2,1,0:T(8,128)}), f32[16,32,256]{2,1,0:T(8,128)S(1)}, u32[]{:S(2)}, u32[]{:S(2)}) async-start(f32[16,32,256]{2,1,0:T(8,128)} %shard_map.149), calls=%async_computation | async-start | bytes 1048576 | tf_op jit(solution)/shard_map/all_to_all | solution.py:429
  29.7 0.8 copy-start
  30.5 18.1 %all-to-all-start.2 = ((f32[16,64,128]{2,1,0:T(8,128)}), f32[16,64,128]{2,1,0:T(8,128)S(1)}, u32[]{:S(2)}, u32[]{:S(2)}) async-start(f32[16,64,128]{2,1,0:T(8,128)} %get-tuple-element.10), calls=%async_computation.2 | async-start | bytes 1048576 | tf_op jit(solution)/shard_map/all_to_all | solution.py:429
  48.6 5.8 %copy-start.1 = (f32[16,64,128]{2,1,0:T(8,128)}, f32[16,64,128]{2,1,0:T(8,128)S(1)}, u32[]{:S(2)}) copy-start(f32[16,64,128]{2,1,0:T(8,128)S(1)} %all-to-all-done.2.v_ref) | copy-start | bytes 1572868
  48.6 21.8 %all-to-all-start.1 = ((f32[256,2,128]{2,1,0:T(2,128)}), f32[256,2,128]{2,1,0:T(2,128)S(1)}, u32[]{:S(2)}, u32[]{:S(2)}) async-start(f32[256,2,128]{2,1,0:T(2,128)} %bitcast.11), calls=%async_computation.1 | async-start | bytes 524288 | tf_op jit(solution)/shard_map/all_to_all | solution.py:429
  70.4 0.7 copy-start.4
  74.9 28.1 %all-to-all-start.3 = ((f32[256,2,128]{2,1,0:T(2,128)}), f32[256,2,128]{2,1,0:T(2,128)S(1)}, u32[]{:S(2)}, u32[]{:S(2)}) async-start(f32[256,2,128]{2,1,0:T(2,128)} %bitcast.15), calls=%async_computation.3 | async-start | bytes 524288 | tf_op jit(solution)/shard_map/all_to_all | solution.py:429
  103.0 0.7 copy-start.3
  136.8 15.6 %all-to-all-start.4 = ((f32[16,16,256]{2,1,0:T(8,128)}), f32[16,16,256]{2,1,0:T(8,128)S(1)}, u32[]{:S(2)}, u32[]{:S(2)}) async-start(f32[16,16,256]{2,1,0:T(8,128)} %shard_map.154), calls=%async_computation.4 | async-start | bytes 524288 | tf_op jit(solution)/shard_map/all_to_all | solution.py:429
  152.5 0.7 copy-start.2

commit v3 on v2

--- a/solution.py
+++ b/solution.py
@@ -13,6 +13,7 @@
 N2 = 256
 BANDS = 8
 TPIX = 48
+GRANT = 12 << 20
 F32 = jnp.float32
 BF16 = jnp.bfloat16
 
@@ -68,7 +69,12 @@
     angle = 2 * np.pi * (nb * k1 % N1) / N1
     last = np.concatenate([np.cos(angle), -np.sin(angle)], axis=1) / NS
     last[:, 64] = np.cos(np.pi * np.arange(N1)) / NS
-    return [np.asarray(a, np.float32) for a in (first[0], first[1], keep, swap, last)]
+    tables = [np.asarray(a, np.float32) for a in (keep, swap)]
+    for a in (first[0], first[1], last):
+        upper = np.asarray(a, jnp.bfloat16)
+        lower = np.asarray(a - upper.astype(np.float64), jnp.bfloat16)
+        tables.append(np.stack([upper, lower]))
+    return tables
 
 
 def _dot(a, b):
@@ -81,9 +87,19 @@
     )
 
 
-def _dot_nt(a, b):
-    return lax.dot_general(
-        a, b, (((1,), (1,)), ((), ())), precision=HIGHEST, preferred_element_type=F32
+def _parts(a):
+    upper = a.astype(BF16)
+    return upper, (a - upper.astype(F32)).astype(BF16)
+
+
+def _dot3(table_ref, b, dims):
+    upper, lower = _parts(b)
+
+    def product(x, y):
+        return lax.dot_general(x, y, (dims, ((), ())), preferred_element_type=F32)
+
+    return product(table_ref[0], upper) + (
+        product(table_ref[0], lower) + product(table_ref[1], upper)
     )
 
 
@@ -209,7 +225,7 @@
     ]
 
 
-def invert_in_place(mats_ref):
+def invert_in_place(mat_refs):
     lane = _lanes((128, 128))
     lane8 = _lanes((8, 128))
 
@@ -217,34 +233,38 @@
         base = 4 * panel
         within = (lane >= base) & (lane < base + 4)
         index = [jnp.full((128, 128), base + j, jnp.int32) for j in range(4)]
-        for part in range(2):
-            mat = mats_ref[part]
-            rows = [
-                jnp.broadcast_to(mats_ref[part, pl.ds(base + j, 1), :], (8, 128)) for j in range(4)
-            ]
-            pivots = [
-                [jnp.take_along_axis(rows[i], index[j][:8], axis=1) for j in range(4)]
-                for i in range(4)
-            ]
-            inverse = _quad_inverse(pivots)
+        mats = [ref[...] for ref in mat_refs]
+        rows = [
+            [jnp.broadcast_to(ref[pl.ds(base + j, 1), :], (8, 128)) for j in range(4)]
+            for ref in mat_refs
+        ]
+        pivots = [
+            [[jnp.take_along_axis(r[i], index[j][:8], axis=1) for j in range(4)] for i in range(4)]
+            for r in rows
+        ]
+        inverses = [_quad_inverse(p) for p in pivots]
+        results = []
+        for mat, row, inverse in zip(mats, rows, inverses):
             new = jnp.where(within, 0.0, mat)
             scaled = []
             for i in range(4):
-                row = sum(inverse[i][j] * rows[j] for j in range(4))
+                line = sum(inverse[i][j] * row[j] for j in range(4))
                 for j in range(4):
-                    row = jnp.where(lane8 == base + j, inverse[i][j], row)
-                scaled.append(row)
+                    line = jnp.where(lane8 == base + j, inverse[i][j], line)
+                scaled.append(line)
                 col = jnp.take_along_axis(mat, index[i], axis=1)
-                new = new - col * jnp.concatenate([row] * 16, axis=0)
-            mats_ref[part] = new
+                new = new - col * jnp.concatenate([line] * 16, axis=0)
+            results.append((new, scaled))
+        for ref, (new, scaled) in zip(mat_refs, results):
+            ref[...] = new
             for i in range(4):
-                mats_ref[part, pl.ds(base + i, 1), :] = scaled[i][0:1]
+                ref[pl.ds(base + i, 1), :] = scaled[i][0:1]
         return carry
 
     lax.fori_loop(0, 32, step, 0)
 
 
-def gram_kernel(v_ref, trans_ref, gain_ref, mats_ref):
+def gram_kernel(v_ref, trans_ref, gain_ref, *mat_refs):
     parts = []
     for e in range(2):
         row = []
@@ -254,16 +274,16 @@
         parts.append(row)
     eye = lax.broadcasted_iota(jnp.int32, (128, 128), 0) == _lanes((128, 128))
     for part in range(2):
-        mats_ref[part] = (
+        mat_refs[part][...] = (
             jnp.where(eye, 1.0, 0.0)
             + _dot_tn(parts[0][part], parts[0][part])
             + _dot_tn(parts[1][part], parts[1][part])
         )
-    invert_in_place(mats_ref)
+    invert_in_place(mat_refs)
     for e in range(2):
         trans_ref[e] = jnp.concatenate([parts[e][0], parts[e][1]], axis=1).T
         gain_ref[e] = jnp.concatenate(
-            [_dot(parts[e][0], mats_ref[0]), _dot(parts[e][1], mats_ref[1])], axis=1
+            [_dot(parts[e][part], mat_refs[part][...]) for part in range(2)], axis=1
         )
 
 
@@ -278,7 +298,7 @@
         out_ref[pl.ds(e, 256, stride=2), :] = xs[e] - _dot(gain_ref[e], proj)
 
 
-def inverse_kernel(y_ref, scale_ref, top_ref, bottom_ref, keep_ref, swap_ref, last_ref, out_ref):
+def inverse_kernel(y_ref, scale_ref, keep_ref, swap_ref, top_ref, bottom_ref, last_ref, out_ref):
     lane2 = _lanes((128, 256)) % 128
     sign2 = jnp.where(lane2 < 64, -1.0, 1.0)
     ups, downs = [], []
@@ -304,8 +324,8 @@
     top_turn = jnp.where(first_row, nyquist, top_turn * sign2)
     top = jnp.where(first_row & (lane2 == 0), 0.5 * top, top)
     bottom_turn = turned(bottom) * sign2
-    a_top = _dot(top_ref[...], jnp.concatenate([top, top_turn], axis=0))
-    a_bottom = _dot(bottom_ref[...], jnp.concatenate([bottom, bottom_turn], axis=0))
+    a_top = _dot3(top_ref, jnp.concatenate([top, top_turn], axis=0), ((1,), (0,)))
+    a_bottom = _dot3(bottom_ref, jnp.concatenate([bottom, bottom_turn], axis=0), ((1,), (0,)))
     lane = _lanes((N2, 128))
     for e in range(2):
         cols = slice(128 * e, 128 * e + 128)
@@ -314,7 +334,7 @@
         direct = jnp.where(lane == 0, up, jnp.where(lane == 64, down, both))
         rolled = pltpu.roll(jnp.where(lane == 0, down, both), 64, 1)
         z = keep_ref[...] * direct + swap_ref[...] * rolled
-        x = _dot_nt(last_ref[...], z)
+        x = _dot3(last_ref, z, ((1,), (1,)))
         out_ref[:, 8 * e : 8 * e + 8, :] = x.reshape(16, 8, N2)
 
 
@@ -349,19 +369,24 @@
         out_fn(pl.ds(j, 32, stride=8), jnp.where(keep, value, 0.0))
 
 
+def _split_pixel(point):
+    high = jnp.floor(point * (1.0 / 128))
+    return high, point - 128.0 * high
+
+
 def hits_kernel(point_ref, out_ref, high_ref, low_ref, grid_ref):
-    point = point_ref[:, 16:32, :].reshape(256, 256)
-    high = jnp.floor(point * (1.0 / 128))
-    high_ref[...] = high
-    low_ref[...] = point - 128.0 * high
+    high_ref[...], low_ref[...] = _split_pixel(point_ref[...].astype(F32))
     one = jnp.ones((1, 256), F32)
 
     def step(r, acc):
-        big = _pick(_one_hot(low_ref[pl.ds(r, 1), :], 128), one, 128)
-        small = _pick(_one_hot(high_ref[pl.ds(r, 1), :], 96), one, 96)
-        return acc + _tally(small, big)
-
-    grid_ref[...] = lax.fori_loop(0, 256, step, jnp.zeros((96, 128), F32), unroll=32)
+        for c in range(8):
+            cols = slice(256 * c, 256 * c + 256)
+            big = _pick(_one_hot(low_ref[pl.ds(r, 1), cols], 128), one, 128)
+            small = _pick(_one_hot(high_ref[pl.ds(r, 1), cols], 96), one, 96)
+            acc = acc + _tally(small, big)
+        return acc
+
+    grid_ref[...] = lax.fori_loop(0, 32, step, jnp.zeros((96, 128), F32), unroll=4)
 
     def put(rows, value):
         out_ref[rows, :] = value
@@ -369,7 +394,8 @@
     _tiles(grid_ref, TPIX, put)
 
 
-def sums_kernel(value_ref, high_ref, low_ref, hits_ref, out_ref, grid_ref):
+def sums_kernel(value_ref, point_ref, hits_ref, out_ref, high_ref, low_ref, grid_ref):
+    high_ref[...], low_ref[...] = _split_pixel(point_ref[:, 16:32, :].reshape(256, 256))
     one = jnp.ones((1, 256), F32)
 
     def step(r, acc):
@@ -420,6 +446,7 @@
             in_specs=[VMEM] * len(args),
             out_specs=[VMEM] * len(shapes) if many else VMEM,
             scratch_shapes=list(scratch),
+            compiler_params=pltpu.CompilerParams(vmem_limit_bytes=GRANT),
         )(*args)
 
     return run
@@ -448,21 +475,31 @@
     trans, gain = call(
         gram_kernel,
         [((2, 256, 256), F32), ((2, 256, 256), F32)],
-        scratch=[pltpu.VMEM((2, 128, 128), F32)],
+        scratch=[pltpu.VMEM((128, 128), F32), pltpu.VMEM((128, 128), F32)],
     )(got_v)
     mixed = exchange(spectra.reshape(256, 2, 128), ("det", "tm")).reshape(512, 128)
     weighted = call(apply_kernel, ((512, 128), F32))(mixed, trans, gain)
-    hits, high, low = call(
+    hits = call(
         hits_kernel,
-        [((256, 128), F32), ((256, 256), F32), ((256, 256), F32)],
-        scratch=[pltpu.VMEM((96, 128), F32)],
-    )(got_tod)
+        ((256, 128), F32),
+        scratch=[
+            pltpu.VMEM((32, 2048), F32),
+            pltpu.VMEM((32, 2048), F32),
+            pltpu.VMEM((96, 128), F32),
+        ],
+    )(pointing)
     back = exchange(weighted.reshape(256, 2, 128), ("det", "tm")).reshape(512, 128)
     series = call(inverse_kernel, ((16, 16, 256), F32))(back, scale, *inverse)
     got_series = exchange(series, "tm").reshape(256, 256)
     bins = call(
-        sums_kernel, ((256, 128), F32), scratch=[pltpu.VMEM((96, 128), F32)]
-    )(series.reshape(256, 256), high, low, hits)
+        sums_kernel,
+        ((256, 128), F32),
+        scratch=[
+            pltpu.VMEM((256, 256), F32),
+            pltpu.VMEM((256, 256), F32),
+            pltpu.VMEM((96, 128), F32),
+        ],
+    )(series.reshape(256, 256), got_tod, hits)
     filtered = call(
         spread_kernel, ((32, 2048), F32), scratch=[pltpu.VMEM((512, 128), F32)]
     )(got_series)

time: 156 us -> 143 us (0.917)
  Pallas kernels: 49.7 us -> 35.2 us
  waiting for transfers between devices: 42.9 us -> 51.7 us
  starting transfers between devices: 38.5 us -> 35 us
  blocking collectives: 20.3 us -> 18.2 us
    pallas_call x10, Pallas kernels: 49.7 us -> 35.2 us  [run(): pl.pallas_call(kernel, out_shape=shapes if many else shapes[0], in_specs=...]
    all_to_all x5, waiting for transfers between devices: 42.9 us -> 51.7 us  [exchange(): return lax.all_to_all(value, axes, split_axis=0, concat_axis=0, tiled=True)]
    all_to_all x5, starting transfers between devices: 38.5 us -> 35 us  [exchange(): return lax.all_to_all(value, axes, split_axis=0, concat_axis=0, tiled=True)]
    all_to_all x1, blocking collectives: 20.3 us -> 18.2 us  [exchange(): return lax.all_to_all(value, axes, split_axis=0, concat_axis=0, tiled=True)]
  transfers between devices with their start and end apart: 5 -> 5, of which waited for: 5 -> 5; matrix products, arithmetic and copies ran while one was open for 0% -> 0% of each run, Pallas kernels for 19% -> 14%
where the time goes in v3:
time: 143 us
  waiting for transfers between devices  51.7 us (36%)
  Pallas kernels  35.2 us (25%)
  starting transfers between devices  35 us (24%)
  blocking collectives  18.2 us (13%)
  local copies, waits for them, and re-layouts  1.95 us (1%)
    all_to_all x5, waiting for transfers between devices, exchange(): return lax.all_to_all(value, axes, split_axis=0, concat_axis=0, tiled=True)  51.7 us
    pallas_call x10, Pallas kernels, run(): pl.pallas_call(kernel, out_shape=shapes if many else shapes[0], in_specs=...  35.2 us
    all_to_all x5, starting transfers between devices, exchange(): return lax.all_to_all(value, axes, split_axis=0, concat_axis=0, tiled=True)  35 us
    all_to_all x1, blocking collectives, exchange(): return lax.all_to_all(value, axes, split_axis=0, concat_axis=0, tiled=True)  18.2 us
  transfers between devices with their start and end apart: 5, of which 5 were waited for; matrix products, arithmetic and copies ran while one was open for 0% of the time, Pallas kernels for 14%

profile of v3, /device:TPU:1, one launch (start us, length us, event | category | flops | bytes accessed | tf_op | source)
XLA Modules:
  0.0 142.8 jit_solution(5737039803722705267)
XLA Ops:
  0.6 0.0 copy-start
  0.6 0.9 copy-done
  1.6 0.0 copy-start.4
  1.6 0.9 copy-done.4
  2.5 0.9 shard_map.149
  3.4 0.0 copy-start.9
  3.5 0.0 copy-start.14
  3.5 10.1 %all-to-all-start = ((f32[16,32,256]{2,1,0:T(8,128)}), f32[16,32,256]{2,1,0:T(8,128)S(1)}, u32[]{:S(2)}, u32[]{:S(2)}) async-start(f32[16,32,256]{2,1,0:T(8,128)} %shard_map.149), calls=%async_computation | async-start | bytes 1048576 | tf_op jit(solution)/shard_map/all_to_all | solution.py:456
  13.6 0.0 copy-done.9
  13.6 0.0 copy-done.14
  13.6 1.0 shard_map.150
  14.5 16.2 %all-to-all-done.x_ref.point_ref = f32[16,32,256]{2,1,0:T(8,128)S(1)} async-done(((f32[16,32,256]{2,1,0:T(8,128)}), f32[16,32,256]{2,1,0:T(8,128)S(1)}, u32[]{:S(2)}, u32[]{:S(2)}) %all-to-all-start) | async-done | bytes 524320 | tf_op jit(solution)/shard_map/all_to_all | solution.py:456
  30.8 0.0 copy-start.2
  30.8 0.0 copy-start.3
  30.8 0.0 copy-start.7
  30.8 0.0 copy-start.8
  30.8 0.0 copy-start.13
  30.8 6.9 %all-to-all-start.2 = ((f32[16,64,128]{2,1,0:T(8,128)}), f32[16,64,128]{2,1,0:T(8,128)S(1)}, u32[]{:S(2)}, u32[]{:S(2)}) async-start(f32[16,64,128]{2,1,0:T(8,128)} %get-tuple-element.7), calls=%async_computation.2 | async-start | bytes 1048576 | tf_op jit(solution)/shard_map/all_to_all | solution.py:456
  37.7 0.0 copy-done.2
  37.7 0.0 copy-done.3
  37.7 0.0 copy-done.7
  37.7 0.0 copy-done.8
  37.7 0.0 copy-done.13
  37.7 2.0 %shard_map.151 = f32[512,128]{1,0:T(8,128)} custom-call(f32[16,32,256]{2,1,0:T(8,128)S(1)} %all-to-all-done.x_ref.point_ref, f32[24,256]{1,0:T(8,128)S(1)} %get-tuple-element.6.scale_ref, f32[128,128]{1,0:T(8,128)S(1)} %copy-done.13, f32[256,128]{1,0:T(8,128)S(1)} %copy-done.7, f32[256,128]{1,0:T(8,128)S(1)} %copy-done.8, f32[128,512]{1,0:T(8,128)S(1)} %copy-done.2, ...), custom_call_target="tpu_custom_call" | custom-call | tf_op jit(solution)/shard_map/pallas_call | solution.py:443
  39.7 9.3 %all-to-all-done.2.v_ref = f32[16,64,128]{2,1,0:T(8,128)S(1)} async-done(((f32[16,64,128]{2,1,0:T(8,128)}), f32[16,64,128]{2,1,0:T(8,128)S(1)}, u32[]{:S(2)}, u32[]{:S(2)}) %all-to-all-start.2) | async-done | bytes 524320 | tf_op jit(solution)/shard_map/all_to_all | solution.py:456
  49.0 5.8 %all-to-all-start.1 = ((f32[256,2,128]{2,1,0:T(2,128)}), f32[256,2,128]{2,1,0:T(2,128)S(1)}, u32[]{:S(2)}, u32[]{:S(2)}) async-start(f32[256,2,128]{2,1,0:T(2,128)} %bitcast), calls=%async_computation.1 | async-start | bytes 524288 | tf_op jit(solution)/shard_map/all_to_all | solution.py:456
  54.8 10.2 %shard_map.152 = (f32[2,256,256]{2,1,0:T(8,128)S(1)}, f32[2,256,256]{2,1,0:T(8,128)S(1)}) custom-call(f32[16,64,128]{2,1,0:T(8,128)S(1)} %all-to-all-done.2.v_ref), custom_call_target="tpu_custom_call" | custom-call | tf_op jit(solution)/shard_map/pallas_call | solution.py:443
  65.1 5.7 %all-to-all-done.1 = f32[256,2,128]{2,1,0:T(2,128)S(1)} async-done(((f32[256,2,128]{2,1,0:T(2,128)}), f32[256,2,128]{2,1,0:T(2,128)S(1)}, u32[]{:S(2)}, u32[]{:S(2)}) %all-to-all-start.1) | async-done | bytes 262176 | tf_op jit(solution)/shard_map/all_to_all | solution.py:456
  70.8 0.0 copy-start.11
  70.8 0.0 copy-start.12
  70.8 2.6 %shard_map.153 = f32[512,128]{1,0:T(8,128)} custom-call(f32[512,128]{1,0:T(8,128)S(1)} %bitcast.13, f32[2,256,256]{2,1,0:T(8,128)S(1)} %get-tuple-element.8.trans_ref, f32[2,256,256]{2,1,0:T(8,128)S(1)} %get-tuple-element.9.gain_ref), custom_call_target="tpu_custom_call" | custom-call | tf_op jit(solution)/shard_map/pallas_call | solution.py:443
  73.4 0.0 copy-start.1
  73.4 0.0 copy-start.6
  73.4 8.1 %all-to-all-start.3 = ((f32[256,2,128]{2,1,0:T(2,128)}), f32[256,2,128]{2,1,0:T(2,128)S(1)}, u32[]{:S(2)}, u32[]{:S(2)}) async-start(f32[256,2,128]{2,1,0:T(2,128)} %bitcast.2), calls=%async_computation.3 | async-start | bytes 524288 | tf_op jit(solution)/shard_map/all_to_all | solution.py:456
  81.4 0.0 copy-done.1
  81.4 0.0 copy-start.5
  81.5 0.0 copy-start.10
  81.5 6.6 %shard_map.156.hits_ref = f32[256,128]{1,0:T(8,128)S(1)} custom-call(s32[32,2048]{1,0:T(8,128)S(1)} %copy-done.1), custom_call_target="tpu_custom_call" | custom-call | tf_op jit(solution)/shard_map/pallas_call | solution.py:443
  88.1 9.3 %all-to-all-done.3 = f32[256,2,128]{2,1,0:T(2,128)S(1)} async-done(((f32[256,2,128]{2,1,0:T(2,128)}), f32[256,2,128]{2,1,0:T(2,128)S(1)}, u32[]{:S(2)}, u32[]{:S(2)}) %all-to-all-start.3) | async-done | bytes 262176 | tf_op jit(solution)/shard_map/all_to_all | solution.py:456
  97.4 0.0 copy-done.11
  97.4 0.0 copy-done.12
  97.4 0.0 copy-done.6
  97.4 0.0 copy-done.5
  97.4 0.0 copy-done.10
  97.4 1.5 %shard_map.154 = f32[16,16,256]{2,1,0:T(8,128)} custom-call(f32[512,128]{1,0:T(8,128)S(1)} %bitcast.12, f32[24,256]{1,0:T(8,128)S(1)} %get-tuple-element.6.scale_ref, f32[256,128]{1,0:T(8,128)S(1)} %copy-done.10, f32[256,128]{1,0:T(8,128)S(1)} %copy-done.11, bf16[2,256,256]{2,1,0:T(8,128)(2,1)S(1)} %copy-done.5, bf16[2,256,256]{2,1,0:T(8,128)(2,1)S(1)} %copy-done.6, ...), custom_call_target="tpu_custom_call" | custom-call | tf_op jit(solution)/shard_map/pallas_call | solution.py:443
  98.9 9.0 %shard_map.157 = f32[256,128]{1,0:T(8,128)S(1)} custom-call(f32[256,256]{1,0:T(8,128)} %bitcast.5.value_ref, f32[16,32,256]{2,1,0:T(8,128)S(1)} %all-to-all-done.x_ref.point_ref, f32[256,128]{1,0:T(8,128)S(1)} %shard_map.156.hits_ref), custom_call_target="tpu_custom_call" | custom-call | tf_op jit(solution)/shard_map/pallas_call | solution.py:443
  107.9 18.2 %all_to_all.36 = f32[256,1,128]{2,1,0:T(1,128)S(1)} all-to-all(f32[256,1,128]{2,1,0:T(1,128)S(1)} %bitcast.15), channel_id=1, replica_groups=mesh['det'=16,'tm'=16] {'det','tm'}, dimensions={0} | all-to-all | bytes 262144 | tf_op jit(solution)/shard_map/all_to_all | solution.py:456
  126.1 4.2 %all-to-all-start.4 = ((f32[16,16,256]{2,1,0:T(8,128)}), f32[16,16,256]{2,1,0:T(8,128)S(1)}, u32[]{:S(2)}, u32[]{:S(2)}) async-start(f32[16,16,256]{2,1,0:T(8,128)} %shard_map.154), calls=%async_computation.4 | async-start | bytes 524288 | tf_op jit(solution)/shard_map/all_to_all | solution.py:456
  130.3 0.6 shard_map.158
  130.9 11.1 %all-to-all-done.4 = f32[16,16,256]{2,1,0:T(8,128)S(1)} async-done(((f32[16,16,256]{2,1,0:T(8,128)}), f32[16,16,256]{2,1,0:T(8,128)S(1)}, u32[]{:S(2)}, u32[]{:S(2)}) %all-to-all-start.4) | async-done | bytes 262176 | tf_op jit(solution)/shard_map/all_to_all | solution.py:456
  142.0 0.8 shard_map.155
Async XLA Ops:
  0.6 1.0 copy-start
  1.6 0.9 copy-start.4
  3.4 10.1 %copy-start.9 = (f32[8,32,128]{2,1,0:T(8,128)S(1)}, f32[8,32,128]{2,1,0:T(8,128)}, u32[]{:S(2)}) copy-start(f32[8,32,128]{2,1,0:T(8,128)} %modes_ref.1) | copy-start | bytes 393220
  3.5 10.1 %copy-start.14 = (f32[8,32]{1,0:T(8,128)S(1)}, f32[8,32]{1,0:T(8,128)}, u32[]{:S(2)}) copy-start(f32[8,32]{1,0:T(8,128)} %noise_ref.1) | copy-start | bytes 3076
  3.5 27.3 %all-to-all-start = ((f32[16,32,256]{2,1,0:T(8,128)}), f32[16,32,256]{2,1,0:T(8,128)S(1)}, u32[]{:S(2)}, u32[]{:S(2)}) async-start(f32[16,32,256]{2,1,0:T(8,128)} %shard_map.149), calls=%async_computation | async-start | bytes 1048576 | tf_op jit(solution)/shard_map/all_to_all | solution.py:456
  30.8 6.9 %copy-start.2 = (f32[128,512]{1,0:T(8,128)S(1)}, f32[128,512]{1,0:T(8,128)}, u32[]{:S(2)}) copy-start(f32[128,512]{1,0:T(8,128)} %constant.23.clone.top_ref) | copy-start | bytes 786436
  30.8 6.9 %copy-start.3 = (f32[128,512]{1,0:T(8,128)S(1)}, f32[128,512]{1,0:T(8,128)}, u32[]{:S(2)}) copy-start(f32[128,512]{1,0:T(8,128)} %constant.24.clone.bottom_ref) | copy-start | bytes 786436
  30.8 6.9 %copy-start.7 = (f32[256,128]{1,0:T(8,128)S(1)}, f32[256,128]{1,0:T(8,128)}, u32[]{:S(2)}) copy-start(f32[256,128]{1,0:T(8,128)} %constant.21.clone.keep_ref) | copy-start | bytes 393220
  30.8 7.0 %copy-start.8 = (f32[256,128]{1,0:T(8,128)S(1)}, f32[256,128]{1,0:T(8,128)}, u32[]{:S(2)}) copy-start(f32[256,128]{1,0:T(8,128)} %constant.22.clone.swap_ref) | copy-start | bytes 393220
  30.8 7.0 %copy-start.13 = (f32[128,128]{1,0:T(8,128)S(1)}, f32[128,128]{1,0:T(8,128)}, u32[]{:S(2)}) copy-start(f32[128,128]{1,0:T(8,128)} %constant.20.clone.first_ref) | copy-start | bytes 196612
  30.8 18.2 %all-to-all-start.2 = ((f32[16,64,128]{2,1,0:T(8,128)}), f32[16,64,128]{2,1,0:T(8,128)S(1)}, u32[]{:S(2)}, u32[]{:S(2)}) async-start(f32[16,64,128]{2,1,0:T(8,128)} %get-tuple-element.7), calls=%async_computation.2 | async-start | bytes 1048576 | tf_op jit(solution)/shard_map/all_to_all | solution.py:456
  49.0 21.8 %all-to-all-start.1 = ((f32[256,2,128]{2,1,0:T(2,128)}), f32[256,2,128]{2,1,0:T(2,128)S(1)}, u32[]{:S(2)}, u32[]{:S(2)}) async-start(f32[256,2,128]{2,1,0:T(2,128)} %bitcast), calls=%async_computation.1 | async-start | bytes 524288 | tf_op jit(solution)/shard_map/all_to_all | solution.py:456
  70.8 26.6 %copy-start.11 = (f32[256,128]{1,0:T(8,128)S(1)}, f32[256,128]{1,0:T(8,128)}, u32[]{:S(2)}) copy-start(f32[256,128]{1,0:T(8,128)} %constant.26.clone.swap_ref) | copy-start | bytes 393220
  70.8 26.6 %copy-start.12 = (bf16[2,128,128]{2,1,0:T(8,128)(2,1)S(1)}, bf16[2,128,128]{2,1,0:T(8,128)(2,1)}, u32[]{:S(2)}) copy-start(bf16[2,128,128]{2,1,0:T(8,128)(2,1)} %constant.29.clone.last_ref) | copy-start | bytes 196612
  73.4 8.1 %copy-start.1 = (s32[32,2048]{1,0:T(8,128)S(1)}, s32[32,2048]{1,0:T(8,128)}, u32[]{:S(2)}) copy-start(s32[32,2048]{1,0:T(8,128)} %point_ref.3) | copy-start | bytes 786436
  73.4 24.0 %copy-start.6 = (bf16[2,256,256]{2,1,0:T(8,128)(2,1)S(1)}, bf16[2,256,256]{2,1,0:T(8,128)(2,1)}, u32[]{:S(2)}) copy-start(bf16[2,256,256]{2,1,0:T(8,128)(2,1)} %constant.28.clone.bottom_ref) | copy-start | bytes 786436
  73.4 24.0 %all-to-all-start.3 = ((f32[256,2,128]{2,1,0:T(2,128)}), f32[256,2,128]{2,1,0:T(2,128)S(1)}, u32[]{:S(2)}, u32[]{:S(2)}) async-start(f32[256,2,128]{2,1,0:T(2,128)} %bitcast.2), calls=%async_computation.3 | async-start | bytes 524288 | tf_op jit(solution)/shard_map/all_to_all | solution.py:456
  81.4 16.0 %copy-start.5 = (bf16[2,256,256]{2,1,0:T(8,128)(2,1)S(1)}, bf16[2,256,256]{2,1,0:T(8,128)(2,1)}, u32[]{:S(2)}) copy-start(bf16[2,256,256]{2,1,0:T(8,128)(2,1)} %constant.27.clone.top_ref) | copy-start | bytes 786436
  81.5 16.0 %copy-start.10 = (f32[256,128]{1,0:T(8,128)S(1)}, f32[256,128]{1,0:T(8,128)}, u32[]{:S(2)}) copy-start(f32[256,128]{1,0:T(8,128)} %constant.25.clone.keep_ref) | copy-start | bytes 393220
  126.1 15.9 %all-to-all-start.4 = ((f32[16,16,256]{2,1,0:T(8,128)}), f32[16,16,256]{2,1,0:T(8,128)S(1)}, u32[]{:S(2)}, u32[]{:S(2)}) async-start(f32[16,16,256]{2,1,0:T(8,128)} %shard_map.154), calls=%async_computation.4 | async-start | bytes 524288 | tf_op jit(solution)/shard_map/all_to_all | solution.py:456

commit v4 on v3

--- a/solution.py
+++ b/solution.py
@@ -137,19 +137,33 @@
         scale_out[16:24, lanes] = jnp.broadcast_to(up[7:8], (8, 128))
 
 
-def prep_kernel(tod_ref, point_ref, tod_out, tod_tmp, point_tmp):
+def prep_kernel(tod_ref, point_ref, tod_out, point_out, tod_in, point_in, tod_tmp, point_tmp, sems):
+    copies = []
     for octet in range(4):
+        rows = pl.ds(8 * octet, 8)
+        pair = [
+            pltpu.make_async_copy(src.at[rows], dst.at[rows], sems.at[octet, which])
+            for which, (src, dst) in enumerate(((tod_ref, tod_in), (point_ref, point_in)))
+        ]
+        for copy in pair:
+            copy.start()
+        copies.append(pair)
+    for octet in range(4):
+        for copy in copies[octet]:
+            copy.wait()
         for r in range(8):
             for h in range(2):
                 cols = pl.ds(256 * r + 128 * h, 128)
                 rows = pl.ds(256 * h + 64 * octet + r, 8, stride=8)
-                tod_tmp[rows, :] = tod_ref[8 * octet : 8 * octet + 8, cols]
-                point_tmp[rows, :] = point_ref[8 * octet : 8 * octet + 8, cols].astype(F32)
+                tod_tmp[rows, :] = tod_in[8 * octet : 8 * octet + 8, cols]
+                point_tmp[rows, :] = point_in[8 * octet : 8 * octet + 8, cols].astype(F32)
     for h in range(2):
         cols = slice(128 * h, 128 * h + 128)
         part = slice(256 * h, 256 * h + 256)
+        points = point_tmp[part, :].reshape(16, 2, 8, 128)
         tod_out[:, 0:16, cols] = tod_tmp[part, :].reshape(16, 16, 128)
-        tod_out[:, 16:32, cols] = point_tmp[part, :].reshape(16, 16, 128)
+        tod_out[:, 16:24, cols] = points[:, 0]
+        point_out[:, cols] = point_tmp[part, :]
 
 
 def _first_scale(scale_ref):
@@ -375,18 +389,15 @@
 
 
 def hits_kernel(point_ref, out_ref, high_ref, low_ref, grid_ref):
-    high_ref[...], low_ref[...] = _split_pixel(point_ref[...].astype(F32))
+    high_ref[...], low_ref[...] = _split_pixel(point_ref[...])
     one = jnp.ones((1, 256), F32)
 
     def step(r, acc):
-        for c in range(8):
-            cols = slice(256 * c, 256 * c + 256)
-            big = _pick(_one_hot(low_ref[pl.ds(r, 1), cols], 128), one, 128)
-            small = _pick(_one_hot(high_ref[pl.ds(r, 1), cols], 96), one, 96)
-            acc = acc + _tally(small, big)
-        return acc
-
-    grid_ref[...] = lax.fori_loop(0, 32, step, jnp.zeros((96, 128), F32), unroll=4)
+        big = _pick(_one_hot(low_ref[pl.ds(r, 1), :], 128), one, 128)
+        small = _pick(_one_hot(high_ref[pl.ds(r, 1), :], 96), one, 96)
+        return acc + _tally(small, big)
+
+    grid_ref[...] = lax.fori_loop(0, 256, step, jnp.zeros((96, 128), F32), unroll=32)
 
     def put(rows, value):
         out_ref[rows, :] = value
@@ -394,8 +405,7 @@
     _tiles(grid_ref, TPIX, put)
 
 
-def sums_kernel(value_ref, point_ref, hits_ref, out_ref, high_ref, low_ref, grid_ref):
-    high_ref[...], low_ref[...] = _split_pixel(point_ref[:, 16:32, :].reshape(256, 256))
+def _half_sums(value_ref, high_ref, low_ref):
     one = jnp.ones((1, 256), F32)
 
     def step(r, acc):
@@ -406,8 +416,21 @@
         small = jnp.concatenate([_pick(mask, upper, 96), _pick(mask, value - upper, 96)], axis=0)
         return acc + _tally(small, big)
 
-    acc = lax.fori_loop(0, 256, step, jnp.zeros((192, 128), F32), unroll=32)
-    grid_ref[...] = acc[:96] + acc[96:]
+    acc = lax.fori_loop(0, 128, step, jnp.zeros((192, 128), F32), unroll=32)
+    return acc[:96] + acc[96:]
+
+
+def early_kernel(series_ref, got_ref, point_ref, out_ref, high_out, low_out, value_ref, high_ref, low_ref):
+    high_ref[...], low_ref[...] = _split_pixel(got_ref[:, 16:24, :].reshape(128, 256))
+    value_ref[...] = series_ref[:, 0:8, :].reshape(128, 256)
+    own = point_ref[...].reshape(16, 16, 256)[:, 8:16, :].reshape(128, 256)
+    high_out[...], low_out[...] = _split_pixel(own)
+    out_ref[...] = _half_sums(value_ref, high_ref, low_ref)
+
+
+def late_kernel(series_ref, high_ref, low_ref, early_ref, hits_ref, out_ref, value_ref, grid_ref):
+    value_ref[...] = series_ref[:, 8:16, :].reshape(128, 256)
+    grid_ref[...] = early_ref[...] + _half_sums(value_ref, high_ref, low_ref)
 
     def put(rows, value):
         out_ref[rows, :] = value + hits_ref[rows, :]
@@ -433,9 +456,10 @@
 
 
 VMEM = pl.BlockSpec(memory_space=pltpu.VMEM)
-
-
-def call(kernel, outs, scratch=()):
+HBM = pl.BlockSpec(memory_space=pl.ANY)
+
+
+def call(kernel, outs, scratch=(), space=VMEM):
     many = isinstance(outs, list)
     shapes = [jax.ShapeDtypeStruct(s, d) for s, d in (outs if many else [outs])]
 
@@ -443,7 +467,7 @@
         return pl.pallas_call(
             kernel,
             out_shape=shapes if many else shapes[0],
-            in_specs=[VMEM] * len(args),
+            in_specs=[space] * len(args),
             out_specs=[VMEM] * len(shapes) if many else VMEM,
             scratch_shapes=list(scratch),
             compiler_params=pltpu.CompilerParams(vmem_limit_bytes=GRANT),
@@ -464,10 +488,17 @@
         [((16, 64, 128), F32), ((24, 256), F32)],
         scratch=[pltpu.VMEM((2, 32, 128), F32)],
     )(modes, noise_level)
-    send_tod = call(
+    send_tod, local_point = call(
         prep_kernel,
-        ((16, 32, 256), F32),
-        scratch=[pltpu.VMEM((512, 128), F32), pltpu.VMEM((512, 128), F32)],
+        [((16, 24, 256), F32), ((256, 256), F32)],
+        scratch=[
+            pltpu.VMEM((32, 2048), F32),
+            pltpu.VMEM((32, 2048), jnp.int32),
+            pltpu.VMEM((512, 128), F32),
+            pltpu.VMEM((512, 128), F32),
+            pltpu.SemaphoreType.DMA((4, 2)),
+        ],
+        space=HBM,
     )(tod, pointing)
     got_v = exchange(send_v, "det")
     got_tod = exchange(send_tod, "tm")
@@ -483,26 +514,26 @@
         hits_kernel,
         ((256, 128), F32),
         scratch=[
-            pltpu.VMEM((32, 2048), F32),
-            pltpu.VMEM((32, 2048), F32),
-            pltpu.VMEM((96, 128), F32),
-        ],
-    )(pointing)
-    back = exchange(weighted.reshape(256, 2, 128), ("det", "tm")).reshape(512, 128)
-    series = call(inverse_kernel, ((16, 16, 256), F32))(back, scale, *inverse)
-    got_series = exchange(series, "tm").reshape(256, 256)
-    bins = call(
-        sums_kernel,
-        ((256, 128), F32),
-        scratch=[
             pltpu.VMEM((256, 256), F32),
             pltpu.VMEM((256, 256), F32),
             pltpu.VMEM((96, 128), F32),
         ],
-    )(series.reshape(256, 256), got_tod, hits)
+    )(local_point)
+    back = exchange(weighted.reshape(256, 2, 128), ("det", "tm")).reshape(512, 128)
+    series = call(inverse_kernel, ((16, 16, 256), F32))(back, scale, *inverse)
+    got_series = exchange(series, "tm")
+    half = pltpu.VMEM((128, 256), F32)
+    early, high, low = call(
+        early_kernel,
+        [((96, 128), F32), ((128, 256), F32), ((128, 256), F32)],
+        scratch=[half, half, half],
+    )(series, got_tod, local_point)
+    bins = call(
+        late_kernel, ((256, 128), F32), scratch=[half, pltpu.VMEM((96, 128), F32)]
+    )(got_series, high, low, early, hits)
     filtered = call(
         spread_kernel, ((32, 2048), F32), scratch=[pltpu.VMEM((512, 128), F32)]
-    )(got_series)
+    )(got_series.reshape(256, 256))
     got_bins = exchange(bins, ("det", "tm"))
     binned = call(finish_kernel, ((1, TPIX), F32))(got_bins)
     return filtered, binned.reshape(TPIX)

time: 143 us -> 140 us (0.979)
  waiting for transfers between devices: 51.7 us -> 41.7 us
  blocking collectives: 18.2 us -> 23.8 us
    all_to_all x5, waiting for transfers between devices: 51.7 us -> 41.7 us  [exchange(): return lax.all_to_all(value, axes, split_axis=0, concat_axis=0, tiled=True)]
    all_to_all x1, blocking collectives: 18.2 us -> 23.8 us  [exchange(): return lax.all_to_all(value, axes, split_axis=0, concat_axis=0, tiled=True)]
    pallas_call x10 -> x11, Pallas kernels: 35.2 us -> 35.8 us  [run(): pl.pallas_call(kernel, out_shape=shapes if many else shapes[0], in_specs=...]
  transfers between devices with their start and end apart: 5 -> 5, of which waited for: 5 -> 5; matrix products, arithmetic and copies ran while one was open for 0% -> 0% of each run, Pallas kernels for 14% -> 18%
where the time goes in v4:
time: 140 us; the launch traced here: 139 us
  waiting for transfers between devices  41.7 us (30%)
  Pallas kernels  35.8 us (26%)
  starting transfers between devices  35.2 us (25%)
  blocking collectives  23.8 us (17%)
  local copies, waits for them, and re-layouts  1.95 us (1%)
    all_to_all x5, waiting for transfers between devices, exchange(): return lax.all_to_all(value, axes, split_axis=0, concat_axis=0, tiled=True)  41.7 us
    pallas_call x11, Pallas kernels, run(): pl.pallas_call(kernel, out_shape=shapes if many else shapes[0], in_specs=...  35.8 us
    all_to_all x5, starting transfers between devices, exchange(): return lax.all_to_all(value, axes, split_axis=0, concat_axis=0, tiled=True)  35.2 us
    all_to_all x1, blocking collectives, exchange(): return lax.all_to_all(value, axes, split_axis=0, concat_axis=0, tiled=True)  23.8 us
  transfers between devices with their start and end apart: 5, of which 5 were waited for; matrix products, arithmetic and copies ran while one was open for 0% of the time, Pallas kernels for 18%

profile of v4, /device:TPU:1, one launch (start us, length us, event | category | flops | bytes accessed | tf_op | source)
XLA Modules:
  0.0 139.3 jit_solution(17766406667408807791)
XLA Ops:
  0.6 0.0 copy-start
  0.6 0.9 copy-done
  1.6 0.0 copy-start.1
  1.6 0.9 copy-done.1
  2.5 1.6 %shard_map.149 = (f32[16,24,256]{2,1,0:T(8,128)}, f32[256,256]{1,0:T(8,128)S(1)}) custom-call(f32[32,2048]{1,0:T(8,128)S(1)} %copy-done, s32[32,2048]{1,0:T(8,128)S(1)} %copy-done.1), custom_call_target="tpu_custom_call" | custom-call | tf_op jit(solution)/shard_map/pallas_call | solution.py:467
  4.2 0.0 copy-start.8
  4.2 0.0 copy-start.13
  4.2 10.1 %all-to-all-start = ((f32[16,24,256]{2,1,0:T(8,128)}), f32[16,24,256]{2,1,0:T(8,128)S(1)}, u32[]{:S(2)}, u32[]{:S(2)}) async-start(f32[16,24,256]{2,1,0:T(8,128)} %get-tuple-element.11), calls=%async_computation | async-start | bytes 786432 | tf_op jit(solution)/shard_map/all_to_all | solution.py:480
  14.3 0.0 copy-done.8
  14.3 0.0 copy-done.13
  14.3 1.0 shard_map.150
  15.3 13.5 %all-to-all-done.x_ref.got_ref = f32[16,24,256]{2,1,0:T(8,128)S(1)} async-done(((f32[16,24,256]{2,1,0:T(8,128)}), f32[16,24,256]{2,1,0:T(8,128)S(1)}, u32[]{:S(2)}, u32[]{:S(2)}) %all-to-all-start) | async-done | bytes 393248 | tf_op jit(solution)/shard_map/all_to_all | solution.py:480
  28.8 0.0 copy-start.4
  28.8 0.0 copy-start.5
  28.8 0.0 copy-start.6
  28.8 0.0 copy-start.7
  28.8 0.0 copy-start.12
  28.8 6.9 %all-to-all-start.2 = ((f32[16,64,128]{2,1,0:T(8,128)}), f32[16,64,128]{2,1,0:T(8,128)S(1)}, u32[]{:S(2)}, u32[]{:S(2)}) async-start(f32[16,64,128]{2,1,0:T(8,128)} %get-tuple-element.13), calls=%async_computation.2 | async-start | bytes 1048576 | tf_op jit(solution)/shard_map/all_to_all | solution.py:480
  35.7 0.0 copy-done.4
  35.7 0.0 copy-done.5
  35.7 0.0 copy-done.6
  35.8 0.0 copy-done.7
  35.8 0.0 copy-done.12
  35.8 2.0 %shard_map.151 = f32[512,128]{1,0:T(8,128)} custom-call(f32[16,24,256]{2,1,0:T(8,128)S(1)} %all-to-all-done.x_ref.got_ref, f32[24,256]{1,0:T(8,128)S(1)} %get-tuple-element.12.scale_ref, f32[128,128]{1,0:T(8,128)S(1)} %copy-done.12, f32[256,128]{1,0:T(8,128)S(1)} %copy-done.7, f32[256,128]{1,0:T(8,128)S(1)} %copy-done.6, f32[128,512]{1,0:T(8,128)S(1)} %copy-done.5, ...), custom_call_target="tpu_custom_call" | custom-call | tf_op jit(solution)/shard_map/pallas_call | solution.py:467
  37.8 10.0 %all-to-all-done.2.v_ref = f32[16,64,128]{2,1,0:T(8,128)S(1)} async-done(((f32[16,64,128]{2,1,0:T(8,128)}), f32[16,64,128]{2,1,0:T(8,128)S(1)}, u32[]{:S(2)}, u32[]{:S(2)}) %all-to-all-start.2) | async-done | bytes 524320 | tf_op jit(solution)/shard_map/all_to_all | solution.py:480
  47.7 5.4 %all-to-all-start.1 = ((f32[256,2,128]{2,1,0:T(2,128)}), f32[256,2,128]{2,1,0:T(2,128)S(1)}, u32[]{:S(2)}, u32[]{:S(2)}) async-start(f32[256,2,128]{2,1,0:T(2,128)} %bitcast), calls=%async_computation.1 | async-start | bytes 524288 | tf_op jit(solution)/shard_map/all_to_all | solution.py:480
  53.2 10.2 %shard_map.152 = (f32[2,256,256]{2,1,0:T(8,128)S(1)}, f32[2,256,256]{2,1,0:T(8,128)S(1)}) custom-call(f32[16,64,128]{2,1,0:T(8,128)S(1)} %all-to-all-done.2.v_ref), custom_call_target="tpu_custom_call" | custom-call | tf_op jit(solution)/shard_map/pallas_call | solution.py:467
  63.4 5.8 %all-to-all-done.1 = f32[256,2,128]{2,1,0:T(2,128)S(1)} async-done(((f32[256,2,128]{2,1,0:T(2,128)}), f32[256,2,128]{2,1,0:T(2,128)S(1)}, u32[]{:S(2)}, u32[]{:S(2)}) %all-to-all-start.1) | async-done | bytes 262176 | tf_op jit(solution)/shard_map/all_to_all | solution.py:480
  69.3 0.0 copy-start.9
  69.3 0.0 copy-start.10
  69.3 0.0 copy-start.11
  69.3 1.9 %shard_map.153 = f32[512,128]{1,0:T(8,128)S(1)} custom-call(f32[512,128]{1,0:T(8,128)S(1)} %bitcast.11, f32[2,256,256]{2,1,0:T(8,128)S(1)} %get-tuple-element.14.trans_ref, f32[2,256,256]{2,1,0:T(8,128)S(1)} %get-tuple-element.15.gain_ref), custom_call_target="tpu_custom_call" | custom-call | tf_op jit(solution)/shard_map/pallas_call | solution.py:467
  71.1 0.0 copy-start.2
  71.2 0.0 copy-start.3
  71.2 23.8 %all_to_all.36 = f32[256,2,128]{2,1,0:T(2,128)S(1)} all-to-all(f32[256,2,128]{2,1,0:T(2,128)S(1)} %bitcast.13), channel_id=1, replica_groups=mesh['det'=16,'tm'=16] {'det','tm'}, dimensions={0} | all-to-all | bytes 524288 | tf_op jit(solution)/shard_map/all_to_all | solution.py:480
  95.0 0.0 copy-done.9
  95.0 0.0 copy-done.10
  95.0 0.0 copy-done.11
  95.0 0.0 copy-done.2
  95.0 0.0 copy-done.3
  95.0 1.5 %shard_map.154.series_ref = f32[16,16,256]{2,1,0:T(8,128)} custom-call(f32[512,128]{1,0:T(8,128)S(1)} %bitcast.12, f32[24,256]{1,0:T(8,128)S(1)} %get-tuple-element.12.scale_ref, f32[256,128]{1,0:T(8,128)S(1)} %copy-done.10, f32[256,128]{1,0:T(8,128)S(1)} %copy-done.9, bf16[2,256,256]{2,1,0:T(8,128)(2,1)S(1)} %copy-done.3, ...), custom_call_target="tpu_custom_call" | custom-call | tf_op jit(solution)/shard_map/pallas_call | solution.py:467
  96.5 3.8 %all-to-all-start.4 = ((f32[16,16,256]{2,1,0:T(8,128)}), f32[16,16,256]{2,1,0:T(8,128)S(1)}, u32[]{:S(2)}, u32[]{:S(2)}) async-start(f32[16,16,256]{2,1,0:T(8,128)} %shard_map.154.series_ref), calls=%async_computation.4 | async-start | bytes 524288 | tf_op jit(solution)/shard_map/all_to_all | solution.py:480
  100.3 6.6 %shard_map.157.hits_ref = f32[256,128]{1,0:T(8,128)S(1)} custom-call(f32[256,256]{1,0:T(8,128)S(1)} %get-tuple-element.16.point_ref), custom_call_target="tpu_custom_call" | custom-call | tf_op jit(solution)/shard_map/pallas_call | solution.py:467
  106.8 4.9 %shard_map.156 = (f32[96,128]{1,0:T(8,128)S(1)}, f32[128,256]{1,0:T(8,128)S(1)}, f32[128,256]{1,0:T(8,128)S(1)}) custom-call(f32[16,16,256]{2,1,0:T(8,128)} %shard_map.154.series_ref, f32[16,24,256]{2,1,0:T(8,128)S(1)} %all-to-all-done.x_ref.got_ref, f32[256,256]{1,0:T(8,128)S(1)} %get-tuple-element.16.point_ref), custom_call_target="tpu_custom_call" | custom-call | tf_op jit(solution)/shard_map/pallas_call | solution.py:467
  111.8 0.2 all-to-all-done.4.series_ref
  112.0 4.7 %shard_map.158 = f32[256,128]{1,0:T(8,128)} custom-call(f32[16,16,256]{2,1,0:T(8,128)S(1)} %all-to-all-done.4.series_ref, f32[128,256]{1,0:T(8,128)S(1)} %get-tuple-element.17.high_ref, f32[128,256]{1,0:T(8,128)S(1)} %get-tuple-element.18.low_ref, f32[96,128]{1,0:T(8,128)S(1)} %get-tuple-element.19.early_ref, f32[256,128]{1,0:T(8,128)S(1)} %shard_map.157.hits_ref), custom_call_target="tpu_custom_call" | custom-call | tf_op jit(solution)/shard_map/pallas_call | solution.py:467
  116.7 9.0 %all-to-all-start.5 = ((f32[256,1,128]{2,1,0:T(1,128)}), f32[256,1,128]{2,1,0:T(1,128)S(1)}, u32[]{:S(2)}, u32[]{:S(2)}) async-start(f32[256,1,128]{2,1,0:T(1,128)} %bitcast.6), calls=%async_computation.5 | async-start | bytes 262144 | tf_op jit(solution)/shard_map/all_to_all | solution.py:480
  125.7 0.8 shard_map.155
  126.5 12.2 %all-to-all-done.5 = f32[256,1,128]{2,1,0:T(1,128)S(1)} async-done(((f32[256,1,128]{2,1,0:T(1,128)}), f32[256,1,128]{2,1,0:T(1,128)S(1)}, u32[]{:S(2)}, u32[]{:S(2)}) %all-to-all-start.5) | async-done | bytes 131104 | tf_op jit(solution)/shard_map/all_to_all | solution.py:480
  138.7 0.6 shard_map.159
Async XLA Ops:
  0.6 1.0 copy-start
  1.6 0.9 copy-start.1
  4.2 10.1 %copy-start.8 = (f32[8,32,128]{2,1,0:T(8,128)S(1)}, f32[8,32,128]{2,1,0:T(8,128)}, u32[]{:S(2)}) copy-start(f32[8,32,128]{2,1,0:T(8,128)} %modes_ref.1) | copy-start | bytes 393220
  4.2 10.1 %copy-start.13 = (f32[8,32]{1,0:T(8,128)S(1)}, f32[8,32]{1,0:T(8,128)}, u32[]{:S(2)}) copy-start(f32[8,32]{1,0:T(8,128)} %noise_ref.1) | copy-start | bytes 3076
  4.2 24.6 %all-to-all-start = ((f32[16,24,256]{2,1,0:T(8,128)}), f32[16,24,256]{2,1,0:T(8,128)S(1)}, u32[]{:S(2)}, u32[]{:S(2)}) async-start(f32[16,24,256]{2,1,0:T(8,128)} %get-tuple-element.11), calls=%async_computation | async-start | bytes 786432 | tf_op jit(solution)/shard_map/all_to_all | solution.py:480
  28.8 6.9 %copy-start.4 = (f32[128,512]{1,0:T(8,128)S(1)}, f32[128,512]{1,0:T(8,128)}, u32[]{:S(2)}) copy-start(f32[128,512]{1,0:T(8,128)} %constant.24.clone.bottom_ref) | copy-start | bytes 786436
  28.8 6.9 %copy-start.5 = (f32[128,512]{1,0:T(8,128)S(1)}, f32[128,512]{1,0:T(8,128)}, u32[]{:S(2)}) copy-start(f32[128,512]{1,0:T(8,128)} %constant.23.clone.top_ref) | copy-start | bytes 786436
  28.8 6.9 %copy-start.6 = (f32[256,128]{1,0:T(8,128)S(1)}, f32[256,128]{1,0:T(8,128)}, u32[]{:S(2)}) copy-start(f32[256,128]{1,0:T(8,128)} %constant.22.clone.swap_ref) | copy-start | bytes 393220
  28.8 7.0 %copy-start.7 = (f32[256,128]{1,0:T(8,128)S(1)}, f32[256,128]{1,0:T(8,128)}, u32[]{:S(2)}) copy-start(f32[256,128]{1,0:T(8,128)} %constant.21.clone.keep_ref) | copy-start | bytes 393220
  28.8 7.0 %copy-start.12 = (f32[128,128]{1,0:T(8,128)S(1)}, f32[128,128]{1,0:T(8,128)}, u32[]{:S(2)}) copy-start(f32[128,128]{1,0:T(8,128)} %constant.20.clone.first_ref) | copy-start | bytes 196612
  28.8 18.9 %all-to-all-start.2 = ((f32[16,64,128]{2,1,0:T(8,128)}), f32[16,64,128]{2,1,0:T(8,128)S(1)}, u32[]{:S(2)}, u32[]{:S(2)}) async-start(f32[16,64,128]{2,1,0:T(8,128)} %get-tuple-element.13), calls=%async_computation.2 | async-start | bytes 1048576 | tf_op jit(solution)/shard_map/all_to_all | solution.py:480
  47.7 21.5 %all-to-all-start.1 = ((f32[256,2,128]{2,1,0:T(2,128)}), f32[256,2,128]{2,1,0:T(2,128)S(1)}, u32[]{:S(2)}, u32[]{:S(2)}) async-start(f32[256,2,128]{2,1,0:T(2,128)} %bitcast), calls=%async_computation.1 | async-start | bytes 524288 | tf_op jit(solution)/shard_map/all_to_all | solution.py:480
  69.3 25.7 %copy-start.9 = (f32[256,128]{1,0:T(8,128)S(1)}, f32[256,128]{1,0:T(8,128)}, u32[]{:S(2)}) copy-start(f32[256,128]{1,0:T(8,128)} %constant.26.clone.swap_ref) | copy-start | bytes 393220
  69.3 25.7 %copy-start.10 = (f32[256,128]{1,0:T(8,128)S(1)}, f32[256,128]{1,0:T(8,128)}, u32[]{:S(2)}) copy-start(f32[256,128]{1,0:T(8,128)} %constant.25.clone.keep_ref) | copy-start | bytes 393220
  69.3 25.7 %copy-start.11 = (bf16[2,128,128]{2,1,0:T(8,128)(2,1)S(1)}, bf16[2,128,128]{2,1,0:T(8,128)(2,1)}, u32[]{:S(2)}) copy-start(bf16[2,128,128]{2,1,0:T(8,128)(2,1)} %constant.29.clone.last_ref) | copy-start | bytes 196612
  71.1 23.8 %copy-start.2 = (bf16[2,256,256]{2,1,0:T(8,128)(2,1)S(1)}, bf16[2,256,256]{2,1,0:T(8,128)(2,1)}, u32[]{:S(2)}) copy-start(bf16[2,256,256]{2,1,0:T(8,128)(2,1)} %constant.28.clone.bottom_ref) | copy-start | bytes 786436
  71.2 23.8 %copy-start.3 = (bf16[2,256,256]{2,1,0:T(8,128)(2,1)S(1)}, bf16[2,256,256]{2,1,0:T(8,128)(2,1)}, u32[]{:S(2)}) copy-start(bf16[2,256,256]{2,1,0:T(8,128)(2,1)} %constant.27.clone.top_ref) | copy-start | bytes 786436
  96.5 15.5 %all-to-all-start.4 = ((f32[16,16,256]{2,1,0:T(8,128)}), f32[16,16,256]{2,1,0:T(8,128)S(1)}, u32[]{:S(2)}, u32[]{:S(2)}) async-start(f32[16,16,256]{2,1,0:T(8,128)} %shard_map.154.series_ref), calls=%async_computation.4 | async-start | bytes 524288 | tf_op jit(solution)/shard_map/all_to_all | solution.py:480
  116.7 21.9 %all-to-all-start.5 = ((f32[256,1,128]{2,1,0:T(1,128)}), f32[256,1,128]{2,1,0:T(1,128)S(1)}, u32[]{:S(2)}, u32[]{:S(2)}) async-start(f32[256,1,128]{2,1,0:T(1,128)} %bitcast.6), calls=%async_computation.5 | async-start | bytes 262144 | tf_op jit(solution)/shard_map/all_to_all | solution.py:480

commit v5 on v3

--- a/solution.py
+++ b/solution.py
@@ -14,6 +14,7 @@
 BANDS = 8
 TPIX = 48
 GRANT = 12 << 20
+WIDE_GRANT = 60 << 20
 F32 = jnp.float32
 BF16 = jnp.bfloat16
 
@@ -137,19 +138,28 @@
         scale_out[16:24, lanes] = jnp.broadcast_to(up[7:8], (8, 128))
 
 
-def prep_kernel(tod_ref, point_ref, tod_out, tod_tmp, point_tmp):
+def _spread_rows(source_ref, tmp_ref, octet):
+    for r in range(8):
+        for h in range(2):
+            cols = pl.ds(256 * r + 128 * h, 128)
+            rows = pl.ds(256 * h + 64 * octet + r, 8, stride=8)
+            tmp_ref[rows, :] = source_ref[8 * octet : 8 * octet + 8, cols].astype(F32)
+
+
+def prep_kernel(tod_ref, tod_out, tod_in, tod_tmp, sems):
+    copies = []
     for octet in range(4):
-        for r in range(8):
-            for h in range(2):
-                cols = pl.ds(256 * r + 128 * h, 128)
-                rows = pl.ds(256 * h + 64 * octet + r, 8, stride=8)
-                tod_tmp[rows, :] = tod_ref[8 * octet : 8 * octet + 8, cols]
-                point_tmp[rows, :] = point_ref[8 * octet : 8 * octet + 8, cols].astype(F32)
-    for h in range(2):
-        cols = slice(128 * h, 128 * h + 128)
-        part = slice(256 * h, 256 * h + 256)
-        tod_out[:, 0:16, cols] = tod_tmp[part, :].reshape(16, 16, 128)
-        tod_out[:, 16:32, cols] = point_tmp[part, :].reshape(16, 16, 128)
+        rows = pl.ds(8 * octet, 8)
+        copy = pltpu.make_async_copy(tod_ref.at[rows], tod_in.at[rows], sems.at[octet])
+        copy.start()
+        copies.append(copy)
+    for octet in range(4):
+        copies[octet].wait()
+        _spread_rows(tod_in, tod_tmp, octet)
+        for h in range(2):
+            cols = slice(128 * h, 128 * h + 128)
+            low = 256 * h + 64 * octet
+            tod_out[64 * octet : 64 * octet + 64, cols] = tod_tmp[low : low + 64, :]
 
 
 def _first_scale(scale_ref):
@@ -374,19 +384,22 @@
     return high, point - 128.0 * high
 
 
-def hits_kernel(point_ref, out_ref, high_ref, low_ref, grid_ref):
-    high_ref[...], low_ref[...] = _split_pixel(point_ref[...].astype(F32))
+def hits_kernel(point_ref, out_ref, high_ref, low_ref, tmp_ref, grid_ref):
+    for octet in range(4):
+        _spread_rows(point_ref, tmp_ref, octet)
+    for h in range(2):
+        cols = slice(128 * h, 128 * h + 128)
+        high, low = _split_pixel(tmp_ref[256 * h : 256 * h + 256, :])
+        high_ref[:, cols] = high
+        low_ref[:, cols] = low
     one = jnp.ones((1, 256), F32)
 
     def step(r, acc):
-        for c in range(8):
-            cols = slice(256 * c, 256 * c + 256)
-            big = _pick(_one_hot(low_ref[pl.ds(r, 1), cols], 128), one, 128)
-            small = _pick(_one_hot(high_ref[pl.ds(r, 1), cols], 96), one, 96)
-            acc = acc + _tally(small, big)
-        return acc
-
-    grid_ref[...] = lax.fori_loop(0, 32, step, jnp.zeros((96, 128), F32), unroll=4)
+        big = _pick(_one_hot(low_ref[pl.ds(r, 1), :], 128), one, 128)
+        small = _pick(_one_hot(high_ref[pl.ds(r, 1), :], 96), one, 96)
+        return acc + _tally(small, big)
+
+    grid_ref[...] = lax.fori_loop(0, 256, step, jnp.zeros((96, 128), F32), unroll=32)
 
     def put(rows, value):
         out_ref[rows, :] = value
@@ -394,8 +407,7 @@
     _tiles(grid_ref, TPIX, put)
 
 
-def sums_kernel(value_ref, point_ref, hits_ref, out_ref, high_ref, low_ref, grid_ref):
-    high_ref[...], low_ref[...] = _split_pixel(point_ref[:, 16:32, :].reshape(256, 256))
+def sums_kernel(value_ref, high_ref, low_ref, hits_ref, out_ref, grid_ref):
     one = jnp.ones((1, 256), F32)
 
     def step(r, acc):
@@ -406,7 +418,7 @@
         small = jnp.concatenate([_pick(mask, upper, 96), _pick(mask, value - upper, 96)], axis=0)
         return acc + _tally(small, big)
 
-    acc = lax.fori_loop(0, 256, step, jnp.zeros((192, 128), F32), unroll=32)
+    acc = lax.fori_loop(0, 256, step, jnp.zeros((192, 128), F32), unroll=64)
     grid_ref[...] = acc[:96] + acc[96:]
 
     def put(rows, value):
@@ -433,9 +445,10 @@
 
 
 VMEM = pl.BlockSpec(memory_space=pltpu.VMEM)
-
-
-def call(kernel, outs, scratch=()):
+HBM = pl.BlockSpec(memory_space=pltpu.HBM)
+
+
+def call(kernel, outs, scratch=(), space=VMEM, grant=GRANT):
     many = isinstance(outs, list)
     shapes = [jax.ShapeDtypeStruct(s, d) for s, d in (outs if many else [outs])]
 
@@ -443,10 +456,10 @@
         return pl.pallas_call(
             kernel,
             out_shape=shapes if many else shapes[0],
-            in_specs=[VMEM] * len(args),
+            in_specs=[space] * len(args),
             out_specs=[VMEM] * len(shapes) if many else VMEM,
             scratch_shapes=list(scratch),
-            compiler_params=pltpu.CompilerParams(vmem_limit_bytes=GRANT),
+            compiler_params=pltpu.CompilerParams(vmem_limit_bytes=grant),
         )(*args)
 
     return run
@@ -466,9 +479,15 @@
     )(modes, noise_level)
     send_tod = call(
         prep_kernel,
-        ((16, 32, 256), F32),
-        scratch=[pltpu.VMEM((512, 128), F32), pltpu.VMEM((512, 128), F32)],
-    )(tod, pointing)
+        ((256, 256), F32),
+        scratch=[
+            pltpu.VMEM((32, 2048), F32),
+            pltpu.VMEM((512, 128), F32),
+            pltpu.SemaphoreType.DMA((4,)),
+        ],
+        space=HBM,
+        grant=WIDE_GRANT,
+    )(tod).reshape(16, 16, 256)
     got_v = exchange(send_v, "det")
     got_tod = exchange(send_tod, "tm")
     spectra = call(forward_kernel, ((512, 128), F32))(got_tod, scale, *forward)
@@ -479,27 +498,17 @@
     )(got_v)
     mixed = exchange(spectra.reshape(256, 2, 128), ("det", "tm")).reshape(512, 128)
     weighted = call(apply_kernel, ((512, 128), F32))(mixed, trans, gain)
-    hits = call(
+    hits, high, low = call(
         hits_kernel,
-        ((256, 128), F32),
-        scratch=[
-            pltpu.VMEM((32, 2048), F32),
-            pltpu.VMEM((32, 2048), F32),
-            pltpu.VMEM((96, 128), F32),
-        ],
+        [((256, 128), F32), ((256, 256), F32), ((256, 256), F32)],
+        scratch=[pltpu.VMEM((512, 128), F32), pltpu.VMEM((96, 128), F32)],
     )(pointing)
     back = exchange(weighted.reshape(256, 2, 128), ("det", "tm")).reshape(512, 128)
     series = call(inverse_kernel, ((16, 16, 256), F32))(back, scale, *inverse)
     got_series = exchange(series, "tm").reshape(256, 256)
     bins = call(
-        sums_kernel,
-        ((256, 128), F32),
-        scratch=[
-            pltpu.VMEM((256, 256), F32),
-            pltpu.VMEM((256, 256), F32),
-            pltpu.VMEM((96, 128), F32),
-        ],
-    )(series.reshape(256, 256), got_tod, hits)
+        sums_kernel, ((256, 128), F32), scratch=[pltpu.VMEM((96, 128), F32)]
+    )(got_series, high, low, hits)
     filtered = call(
         spread_kernel, ((32, 2048), F32), scratch=[pltpu.VMEM((512, 128), F32)]
     )(got_series)

time: 143 us -> 134 us (0.937)
  waiting for transfers between devices: 51.7 us -> 42.4 us
  blocking collectives: 18.2 us -> 23.8 us
  starting transfers between devices: 35 us -> 32.4 us
  local copies, waits for them, and re-layouts: 1.95 us -> 0.06 us
    all_to_all x5, waiting for transfers between devices: 51.7 us -> 42.4 us  [exchange(): return lax.all_to_all(value, axes, split_axis=0, concat_axis=0, tiled=True)]
    all_to_all x1, blocking collectives: 18.2 us -> 23.8 us  [exchange(): return lax.all_to_all(value, axes, split_axis=0, concat_axis=0, tiled=True)]
    all_to_all x5, starting transfers between devices: 35 us -> 32.4 us  [exchange(): return lax.all_to_all(value, axes, split_axis=0, concat_axis=0, tiled=True)]
    unnamed x30 -> x26, local copies, waits for them, and re-layouts: 1.95 us -> 0.06 us
  transfers between devices with their start and end apart: 5 -> 5, of which waited for: 5 -> 5; matrix products, arithmetic and copies ran while one was open for 0% -> 0% of each run, Pallas kernels for 14% -> 15%
where the time goes in v5:
time: 134 us
  waiting for transfers between devices  42.4 us (32%)
  Pallas kernels  34.2 us (26%)
  starting transfers between devices  32.4 us (24%)
  blocking collectives  23.8 us (18%)
    all_to_all x5, waiting for transfers between devices, exchange(): return lax.all_to_all(value, axes, split_axis=0, concat_axis=0, tiled=True)  42.4 us
    pallas_call x10, Pallas kernels, run(): pl.pallas_call(kernel, out_shape=shapes if many else shapes[0], in_specs=...  34.2 us
    all_to_all x5, starting transfers between devices, exchange(): return lax.all_to_all(value, axes, split_axis=0, concat_axis=0, tiled=True)  32.4 us
    all_to_all x1, blocking collectives, exchange(): return lax.all_to_all(value, axes, split_axis=0, concat_axis=0, tiled=True)  23.8 us
  transfers between devices with their start and end apart: 5, of which 5 were waited for; matrix products, arithmetic and copies ran while one was open for 0% of the time, Pallas kernels for 15%

profile of v5, /device:TPU:1, one launch (start us, length us, event | category | flops | bytes accessed | tf_op | source)
XLA Modules:
  0.0 133.8 jit_solution(2127982458227686716)
XLA Ops:
  0.6 1.7 %shard_map.149 = f32[256,256]{1,0:T(8,128)} custom-call(f32[32,2048]{1,0:T(8,128)} %tod_ref.1), custom_call_target="tpu_custom_call" | custom-call | tf_op jit(solution)/shard_map/pallas_call | solution.py:456
  2.3 0.0 copy-start.5
  2.3 0.0 copy-start.12
  2.4 10.1 %all-to-all-start = ((f32[16,16,256]{2,1,0:T(8,128)}), f32[16,16,256]{2,1,0:T(8,128)S(1)}, u32[]{:S(2)}, u32[]{:S(2)}) async-start(f32[16,16,256]{2,1,0:T(8,128)} %bitcast.17), calls=%async_computation | async-start | bytes 524288 | tf_op jit(solution)/shard_map/all_to_all | solution.py:469
  12.5 0.0 copy-done.5
  12.5 0.0 copy-done.12
  12.5 1.0 shard_map.150
  13.4 10.6 %all-to-all-done.x_ref = f32[16,16,256]{2,1,0:T(8,128)S(1)} async-done(((f32[16,16,256]{2,1,0:T(8,128)}), f32[16,16,256]{2,1,0:T(8,128)S(1)}, u32[]{:S(2)}, u32[]{:S(2)}) %all-to-all-start) | async-done | bytes 262176 | tf_op jit(solution)/shard_map/all_to_all | solution.py:469
  24.1 0.0 copy-start.3
  24.1 0.0 copy-start.4
  24.1 0.0 copy-start.8
  24.1 0.0 copy-start.9
  24.1 0.0 copy-start.11
  24.1 6.9 %all-to-all-start.2 = ((f32[16,64,128]{2,1,0:T(8,128)}), f32[16,64,128]{2,1,0:T(8,128)S(1)}, u32[]{:S(2)}, u32[]{:S(2)}) async-start(f32[16,64,128]{2,1,0:T(8,128)} %get-tuple-element.10), calls=%async_computation.2 | async-start | bytes 1048576 | tf_op jit(solution)/shard_map/all_to_all | solution.py:469
  31.0 0.0 copy-done.3
  31.0 0.0 copy-done.4
  31.0 0.0 copy-done.8
  31.0 0.0 copy-done.9
  31.0 0.0 copy-done.11
  31.0 2.0 %shard_map.151 = f32[512,128]{1,0:T(8,128)} custom-call(f32[16,16,256]{2,1,0:T(8,128)S(1)} %all-to-all-done.x_ref, f32[24,256]{1,0:T(8,128)S(1)} %get-tuple-element.9.scale_ref, f32[128,128]{1,0:T(8,128)S(1)} %copy-done.11, f32[256,128]{1,0:T(8,128)S(1)} %copy-done.8, f32[256,128]{1,0:T(8,128)S(1)} %copy-done.9, f32[128,512]{1,0:T(8,128)S(1)} %copy-done.3, ...), custom_call_target="tpu_custom_call" | custom-call | tf_op jit(solution)/shard_map/pallas_call | solution.py:456
  33.0 9.0 %all-to-all-done.2.v_ref = f32[16,64,128]{2,1,0:T(8,128)S(1)} async-done(((f32[16,64,128]{2,1,0:T(8,128)}), f32[16,64,128]{2,1,0:T(8,128)S(1)}, u32[]{:S(2)}, u32[]{:S(2)}) %all-to-all-start.2) | async-done | bytes 524320 | tf_op jit(solution)/shard_map/all_to_all | solution.py:469
  42.0 6.4 %all-to-all-start.1 = ((f32[256,2,128]{2,1,0:T(2,128)}), f32[256,2,128]{2,1,0:T(2,128)S(1)}, u32[]{:S(2)}, u32[]{:S(2)}) async-start(f32[256,2,128]{2,1,0:T(2,128)} %bitcast.1), calls=%async_computation.1 | async-start | bytes 524288 | tf_op jit(solution)/shard_map/all_to_all | solution.py:469
  48.5 10.3 %shard_map.152 = (f32[2,256,256]{2,1,0:T(8,128)S(1)}, f32[2,256,256]{2,1,0:T(8,128)S(1)}) custom-call(f32[16,64,128]{2,1,0:T(8,128)S(1)} %all-to-all-done.2.v_ref), custom_call_target="tpu_custom_call" | custom-call | tf_op jit(solution)/shard_map/pallas_call | solution.py:456
  58.7 5.8 %all-to-all-done.1 = f32[256,2,128]{2,1,0:T(2,128)S(1)} async-done(((f32[256,2,128]{2,1,0:T(2,128)}), f32[256,2,128]{2,1,0:T(2,128)S(1)}, u32[]{:S(2)}, u32[]{:S(2)}) %all-to-all-start.1) | async-done | bytes 262176 | tf_op jit(solution)/shard_map/all_to_all | solution.py:469
  64.6 0.0 copy-start.6
  64.6 0.0 copy-start.7
  64.6 0.0 copy-start.10
  64.6 1.9 %shard_map.153 = f32[512,128]{1,0:T(8,128)S(1)} custom-call(f32[512,128]{1,0:T(8,128)S(1)} %bitcast.13, f32[2,256,256]{2,1,0:T(8,128)S(1)} %get-tuple-element.11.trans_ref, f32[2,256,256]{2,1,0:T(8,128)S(1)} %get-tuple-element.12.gain_ref), custom_call_target="tpu_custom_call" | custom-call | tf_op jit(solution)/shard_map/pallas_call | solution.py:456
  66.4 0.0 copy-start.1
  66.5 0.0 copy-start.2
  66.5 23.8 %all_to_all.36 = f32[256,2,128]{2,1,0:T(2,128)S(1)} all-to-all(f32[256,2,128]{2,1,0:T(2,128)S(1)} %bitcast.15), channel_id=1, replica_groups=mesh['det'=16,'tm'=16] {'det','tm'}, dimensions={0} | all-to-all | bytes 524288 | tf_op jit(solution)/shard_map/all_to_all | solution.py:469
  90.3 0.0 copy-done.6
  90.3 0.0 copy-done.7
  90.3 0.0 copy-done.10
  90.3 0.0 copy-done.1
  90.3 0.0 copy-done.2
  90.3 1.5 %shard_map.154 = f32[16,16,256]{2,1,0:T(8,128)} custom-call(f32[512,128]{1,0:T(8,128)S(1)} %bitcast.14, f32[24,256]{1,0:T(8,128)S(1)} %get-tuple-element.9.scale_ref, f32[256,128]{1,0:T(8,128)S(1)} %copy-done.6, f32[256,128]{1,0:T(8,128)S(1)} %copy-done.7, bf16[2,256,256]{2,1,0:T(8,128)(2,1)S(1)} %copy-done.1, bf16[2,256,256]{2,1,0:T(8,128)(2,1)S(1)} %copy-done.2, ...), custom_call_target="tpu_custom_call" | custom-call | tf_op jit(solution)/shard_map/pallas_call | solution.py:456
  91.8 0.0 copy-start
  91.8 3.9 %all-to-all-start.4 = ((f32[16,16,256]{2,1,0:T(8,128)}), f32[16,16,256]{2,1,0:T(8,128)S(1)}, u32[]{:S(2)}, u32[]{:S(2)}) async-start(f32[16,16,256]{2,1,0:T(8,128)} %shard_map.154), calls=%async_computation.4 | async-start | bytes 524288 | tf_op jit(solution)/shard_map/all_to_all | solution.py:469
  95.7 0.0 copy-done
  95.7 6.6 %shard_map.156 = (f32[256,128]{1,0:T(8,128)S(1)}, f32[256,256]{1,0:T(8,128)S(1)}, f32[256,256]{1,0:T(8,128)S(1)}) custom-call(s32[32,2048]{1,0:T(8,128)S(1)} %copy-done), custom_call_target="tpu_custom_call" | custom-call | tf_op jit(solution)/shard_map/pallas_call | solution.py:456
  102.3 5.1 %all-to-all-done.4 = f32[16,16,256]{2,1,0:T(8,128)S(1)} async-done(((f32[16,16,256]{2,1,0:T(8,128)}), f32[16,16,256]{2,1,0:T(8,128)S(1)}, u32[]{:S(2)}, u32[]{:S(2)}) %all-to-all-start.4) | async-done | bytes 262176 | tf_op jit(solution)/shard_map/all_to_all | solution.py:469
  107.5 7.9 %shard_map.157 = f32[256,128]{1,0:T(8,128)} custom-call(f32[256,256]{1,0:T(8,128)S(1)} %bitcast.11, f32[256,256]{1,0:T(8,128)S(1)} %get-tuple-element.13.high_ref, f32[256,256]{1,0:T(8,128)S(1)} %get-tuple-element.14.low_ref, f32[256,128]{1,0:T(8,128)S(1)} %get-tuple-element.15.hits_ref), custom_call_target="tpu_custom_call" | custom-call | tf_op jit(solution)/shard_map/pallas_call | solution.py:456
  115.4 5.1 %all-to-all-start.5 = ((f32[256,1,128]{2,1,0:T(1,128)}), f32[256,1,128]{2,1,0:T(1,128)S(1)}, u32[]{:S(2)}, u32[]{:S(2)}) async-start(f32[256,1,128]{2,1,0:T(1,128)} %bitcast.7), calls=%async_computation.5 | async-start | bytes 262144 | tf_op jit(solution)/shard_map/all_to_all | solution.py:469
  120.5 0.8 shard_map.155
  121.3 11.9 %all-to-all-done.5 = f32[256,1,128]{2,1,0:T(1,128)S(1)} async-done(((f32[256,1,128]{2,1,0:T(1,128)}), f32[256,1,128]{2,1,0:T(1,128)S(1)}, u32[]{:S(2)}, u32[]{:S(2)}) %all-to-all-start.5) | async-done | bytes 131104 | tf_op jit(solution)/shard_map/all_to_all | solution.py:469
  133.1 0.6 shard_map.158
Async XLA Ops:
  2.3 10.1 %copy-start.5 = (f32[8,32,128]{2,1,0:T(8,128)S(1)}, f32[8,32,128]{2,1,0:T(8,128)}, u32[]{:S(2)}) copy-start(f32[8,32,128]{2,1,0:T(8,128)} %modes_ref.1) | copy-start | bytes 393220
  2.3 10.1 %copy-start.12 = (f32[8,32]{1,0:T(8,128)S(1)}, f32[8,32]{1,0:T(8,128)}, u32[]{:S(2)}) copy-start(f32[8,32]{1,0:T(8,128)} %noise_ref.1) | copy-start | bytes 3076
  2.4 21.7 %all-to-all-start = ((f32[16,16,256]{2,1,0:T(8,128)}), f32[16,16,256]{2,1,0:T(8,128)S(1)}, u32[]{:S(2)}, u32[]{:S(2)}) async-start(f32[16,16,256]{2,1,0:T(8,128)} %bitcast.17), calls=%async_computation | async-start | bytes 524288 | tf_op jit(solution)/shard_map/all_to_all | solution.py:469
  24.1 6.9 %copy-start.3 = (f32[128,512]{1,0:T(8,128)S(1)}, f32[128,512]{1,0:T(8,128)}, u32[]{:S(2)}) copy-start(f32[128,512]{1,0:T(8,128)} %constant.23.clone.top_ref) | copy-start | bytes 786436
  24.1 6.9 %copy-start.4 = (f32[128,512]{1,0:T(8,128)S(1)}, f32[128,512]{1,0:T(8,128)}, u32[]{:S(2)}) copy-start(f32[128,512]{1,0:T(8,128)} %constant.24.clone.bottom_ref) | copy-start | bytes 786436
  24.1 6.9 %copy-start.8 = (f32[256,128]{1,0:T(8,128)S(1)}, f32[256,128]{1,0:T(8,128)}, u32[]{:S(2)}) copy-start(f32[256,128]{1,0:T(8,128)} %constant.21.clone.keep_ref) | copy-start | bytes 393220
  24.1 7.0 %copy-start.9 = (f32[256,128]{1,0:T(8,128)S(1)}, f32[256,128]{1,0:T(8,128)}, u32[]{:S(2)}) copy-start(f32[256,128]{1,0:T(8,128)} %constant.22.clone.swap_ref) | copy-start | bytes 393220
  24.1 7.0 %copy-start.11 = (f32[128,128]{1,0:T(8,128)S(1)}, f32[128,128]{1,0:T(8,128)}, u32[]{:S(2)}) copy-start(f32[128,128]{1,0:T(8,128)} %constant.20.clone.first_ref) | copy-start | bytes 196612
  24.1 17.9 %all-to-all-start.2 = ((f32[16,64,128]{2,1,0:T(8,128)}), f32[16,64,128]{2,1,0:T(8,128)S(1)}, u32[]{:S(2)}, u32[]{:S(2)}) async-start(f32[16,64,128]{2,1,0:T(8,128)} %get-tuple-element.10), calls=%async_computation.2 | async-start | bytes 1048576 | tf_op jit(solution)/shard_map/all_to_all | solution.py:469
  42.0 22.5 %all-to-all-start.1 = ((f32[256,2,128]{2,1,0:T(2,128)}), f32[256,2,128]{2,1,0:T(2,128)S(1)}, u32[]{:S(2)}, u32[]{:S(2)}) async-start(f32[256,2,128]{2,1,0:T(2,128)} %bitcast.1), calls=%async_computation.1 | async-start | bytes 524288 | tf_op jit(solution)/shard_map/all_to_all | solution.py:469
  64.6 25.7 %copy-start.6 = (f32[256,128]{1,0:T(8,128)S(1)}, f32[256,128]{1,0:T(8,128)}, u32[]{:S(2)}) copy-start(f32[256,128]{1,0:T(8,128)} %constant.25.clone.keep_ref) | copy-start | bytes 393220
  64.6 25.7 %copy-start.7 = (f32[256,128]{1,0:T(8,128)S(1)}, f32[256,128]{1,0:T(8,128)}, u32[]{:S(2)}) copy-start(f32[256,128]{1,0:T(8,128)} %constant.26.clone.swap_ref) | copy-start | bytes 393220
  64.6 25.7 %copy-start.10 = (bf16[2,128,128]{2,1,0:T(8,128)(2,1)S(1)}, bf16[2,128,128]{2,1,0:T(8,128)(2,1)}, u32[]{:S(2)}) copy-start(bf16[2,128,128]{2,1,0:T(8,128)(2,1)} %constant.29.clone.last_ref) | copy-start | bytes 196612
  66.4 23.9 %copy-start.1 = (bf16[2,256,256]{2,1,0:T(8,128)(2,1)S(1)}, bf16[2,256,256]{2,1,0:T(8,128)(2,1)}, u32[]{:S(2)}) copy-start(bf16[2,256,256]{2,1,0:T(8,128)(2,1)} %constant.27.clone.top_ref) | copy-start | bytes 786436
  66.5 23.9 %copy-start.2 = (bf16[2,256,256]{2,1,0:T(8,128)(2,1)S(1)}, bf16[2,256,256]{2,1,0:T(8,128)(2,1)}, u32[]{:S(2)}) copy-start(bf16[2,256,256]{2,1,0:T(8,128)(2,1)} %constant.28.clone.bottom_ref) | copy-start | bytes 786436
  91.8 3.9 %copy-start = (s32[32,2048]{1,0:T(8,128)S(1)}, s32[32,2048]{1,0:T(8,128)}, u32[]{:S(2)}) copy-start(s32[32,2048]{1,0:T(8,128)} %point_ref.1) | copy-start | bytes 786436
  91.8 15.7 %all-to-all-start.4 = ((f32[16,16,256]{2,1,0:T(8,128)}), f32[16,16,256]{2,1,0:T(8,128)S(1)}, u32[]{:S(2)}, u32[]{:S(2)}) async-start(f32[16,16,256]{2,1,0:T(8,128)} %shard_map.154), calls=%async_computation.4 | async-start | bytes 524288 | tf_op jit(solution)/shard_map/all_to_all | solution.py:469
  115.4 17.7 %all-to-all-start.5 = ((f32[256,1,128]{2,1,0:T(1,128)}), f32[256,1,128]{2,1,0:T(1,128)S(1)}, u32[]{:S(2)}, u32[]{:S(2)}) async-start(f32[256,1,128]{2,1,0:T(1,128)} %bitcast.7), calls=%async_computation.5 | async-start | bytes 262144 | tf_op jit(solution)/shard_map/all_to_all | solution.py:469

commit v6 on v5

--- a/solution.py
+++ b/solution.py
@@ -1,3 +1,5 @@
+import functools
+
 import numpy as np
 import jax
 import jax.numpy as jnp
@@ -123,10 +125,8 @@
         col = jnp.sum(jnp.where(eye, row, 0.0), axis=1, keepdims=True)
         tmp_ref[part] = modes_ref[which] * col
         for e in range(2):
-            vee = tmp_ref[part, pl.ds(e, 16, stride=2), :]
             low = 32 * part + 16 * e
-            for dest in range(16):
-                v_out[dest, low : low + 16, :] = vee
+            v_out[0, low : low + 16, :] = tmp_ref[part, pl.ds(e, 16, stride=2), :]
     flipped = jnp.concatenate([root[BANDS - 1 - j : BANDS - j] for j in range(BANDS)], axis=0)
     for e in range(2):
         mask = _lanes((BANDS, 32)) == 2 * pos + e
@@ -274,14 +274,16 @@
     lax.fori_loop(0, 32, step, 0)
 
 
-def gram_kernel(v_ref, trans_ref, gain_ref, *mat_refs):
-    parts = []
-    for e in range(2):
-        row = []
-        for part in range(2):
-            low = 32 * part + 0
-            row.append(v_ref[:, low + 16 * e : low + 16 * e + 16, :].reshape(256, 128))
-        parts.append(row)
+def gram_kernel(near_ref, far_ref, trans_ref, gain_ref, vees_ref, *mat_refs):
+    dev, _ = _position()
+    for j in range(16):
+        source = near_ref if j < 8 else far_ref
+        rows = pl.ds(pl.multiple_of((dev ^ j) * 16, 16), 16)
+        for e in range(2):
+            for part in range(2):
+                low = 32 * part + 16 * e
+                vees_ref[e, rows, 128 * part : 128 * part + 128] = source[j % 8, low : low + 16, :]
+    parts = [[vees_ref[e, :, 128 * part : 128 * part + 128] for part in range(2)] for e in range(2)]
     eye = lax.broadcasted_iota(jnp.int32, (128, 128), 0) == _lanes((128, 128))
     for part in range(2):
         mat_refs[part][...] = (
@@ -384,12 +386,17 @@
     return high, point - 128.0 * high
 
 
-def hits_kernel(point_ref, out_ref, high_ref, low_ref, tmp_ref, grid_ref):
-    for octet in range(4):
-        _spread_rows(point_ref, tmp_ref, octet)
+def hits_kernel(half, point_ref, out_ref, high_ref, low_ref, tmp_ref, grid_ref):
+    for octet in range(2):
+        for r in range(8):
+            for h in range(2):
+                cols = pl.ds(256 * r + 128 * h, 128)
+                rows = pl.ds(128 * h + 64 * octet + r, 8, stride=8)
+                low = 16 * half + 8 * octet
+                tmp_ref[rows, :] = point_ref[low : low + 8, cols].astype(F32)
     for h in range(2):
         cols = slice(128 * h, 128 * h + 128)
-        high, low = _split_pixel(tmp_ref[256 * h : 256 * h + 256, :])
+        high, low = _split_pixel(tmp_ref[128 * h : 128 * h + 128, :])
         high_ref[:, cols] = high
         low_ref[:, cols] = low
     one = jnp.ones((1, 256), F32)
@@ -399,7 +406,7 @@
         small = _pick(_one_hot(high_ref[pl.ds(r, 1), :], 96), one, 96)
         return acc + _tally(small, big)
 
-    grid_ref[...] = lax.fori_loop(0, 256, step, jnp.zeros((96, 128), F32), unroll=32)
+    grid_ref[...] = lax.fori_loop(0, 128, step, jnp.zeros((96, 128), F32), unroll=32)
 
     def put(rows, value):
         out_ref[rows, :] = value
@@ -407,22 +414,25 @@
     _tiles(grid_ref, TPIX, put)
 
 
-def sums_kernel(value_ref, high_ref, low_ref, hits_ref, out_ref, grid_ref):
+def sums_kernel(value_ref, first_refs, second_refs, out_ref, grid_ref):
     one = jnp.ones((1, 256), F32)
 
-    def step(r, acc):
-        value = value_ref[pl.ds(r, 1), :]
+    def step(base, high_ref, low_ref, r, acc):
+        value = value_ref[pl.ds(base + r, 1), :]
         upper = value.astype(BF16).astype(F32)
         big = _pick(_one_hot(low_ref[pl.ds(r, 1), :], 128), one, 128)
         mask = _one_hot(high_ref[pl.ds(r, 1), :], 96)
         small = jnp.concatenate([_pick(mask, upper, 96), _pick(mask, value - upper, 96)], axis=0)
         return acc + _tally(small, big)
 
-    acc = lax.fori_loop(0, 256, step, jnp.zeros((192, 128), F32), unroll=64)
+    acc = jnp.zeros((192, 128), F32)
+    for base, (_, high_ref, low_ref) in ((0, first_refs), (128, second_refs)):
+        turn = functools.partial(step, base, high_ref, low_ref)
+        acc = lax.fori_loop(0, 128, turn, acc, unroll=64)
     grid_ref[...] = acc[:96] + acc[96:]
 
     def put(rows, value):
-        out_ref[rows, :] = value + hits_ref[rows, :]
+        out_ref[rows, :] = value + first_refs[0][rows, :] + second_refs[0][rows, :]
 
     _tiles(grid_ref, 0, put)
 
@@ -474,7 +484,7 @@
     inverse = [jnp.asarray(a) for a in _inverse_tables()]
     send_v, scale = call(
         basis_kernel,
-        [((16, 64, 128), F32), ((24, 256), F32)],
+        [((1, 64, 128), F32), ((24, 256), F32)],
         scratch=[pltpu.VMEM((2, 32, 128), F32)],
     )(modes, noise_level)
     send_tod = call(
@@ -488,27 +498,41 @@
         space=HBM,
         grant=WIDE_GRANT,
     )(tod).reshape(16, 16, 256)
-    got_v = exchange(send_v, "det")
+    near = send_v
+    for bit in range(4):
+        pairs = [(i, i ^ (1 << bit)) for i in range(16)]
+        far = lax.ppermute(near, "det", pairs)
+        if bit < 3:
+            near = jnp.concatenate([near, far], axis=0)
     got_tod = exchange(send_tod, "tm")
     spectra = call(forward_kernel, ((512, 128), F32))(got_tod, scale, *forward)
     trans, gain = call(
         gram_kernel,
         [((2, 256, 256), F32), ((2, 256, 256), F32)],
-        scratch=[pltpu.VMEM((128, 128), F32), pltpu.VMEM((128, 128), F32)],
-    )(got_v)
+        scratch=[
+            pltpu.VMEM((2, 256, 256), F32),
+            pltpu.VMEM((128, 128), F32),
+            pltpu.VMEM((128, 128), F32),
+        ],
+    )(near, far)
     mixed = exchange(spectra.reshape(256, 2, 128), ("det", "tm")).reshape(512, 128)
     weighted = call(apply_kernel, ((512, 128), F32))(mixed, trans, gain)
-    hits, high, low = call(
-        hits_kernel,
-        [((256, 128), F32), ((256, 256), F32), ((256, 256), F32)],
-        scratch=[pltpu.VMEM((512, 128), F32), pltpu.VMEM((96, 128), F32)],
-    )(pointing)
+    counted = [
+        call(
+            functools.partial(hits_kernel, half),
+            [((256, 128), F32), ((128, 256), F32), ((128, 256), F32)],
+            scratch=[pltpu.VMEM((256, 128), F32), pltpu.VMEM((96, 128), F32)],
+        )(pointing)
+        for half in range(2)
+    ]
     back = exchange(weighted.reshape(256, 2, 128), ("det", "tm")).reshape(512, 128)
     series = call(inverse_kernel, ((16, 16, 256), F32))(back, scale, *inverse)
     got_series = exchange(series, "tm").reshape(256, 256)
     bins = call(
-        sums_kernel, ((256, 128), F32), scratch=[pltpu.VMEM((96, 128), F32)]
-    )(got_series, high, low, hits)
+        lambda value, *refs: sums_kernel(value, refs[0:3], refs[3:6], *refs[6:]),
+        ((256, 128), F32),
+        scratch=[pltpu.VMEM((96, 128), F32)],
+    )(got_series, *counted[0], *counted[1])
     filtered = call(
         spread_kernel, ((32, 2048), F32), scratch=[pltpu.VMEM((512, 128), F32)]
     )(got_series)

time: 134 us -> 135 us (level)
  waiting for transfers between devices: 42.4 us -> 30 us
  starting transfers between devices: 32.4 us -> 40.2 us
  blocking collectives: 23.8 us -> 29.5 us
    all_to_all x5 -> x4, waiting for transfers between devices: 42.4 us -> 19.2 us  [exchange(): return lax.all_to_all(value, axes, split_axis=0, concat_axis=0, tiled=True)]
    ppermute x0 -> x4, waiting for transfers between devices: none -> 10.7 us  [steps(): far = lax.ppermute(near, 'det', pairs)]
    ppermute x0 -> x4, starting transfers between devices: none -> 8.54 us  [steps(): far = lax.ppermute(near, 'det', pairs)]
    all_to_all x1, blocking collectives: 23.8 us -> 29.5 us  [exchange(): return lax.all_to_all(value, axes, split_axis=0, concat_axis=0, tiled=True)]
    all_to_all x5 -> x4, starting transfers between devices: 32.4 us -> 31.7 us  [exchange(): return lax.all_to_all(value, axes, split_axis=0, concat_axis=0, tiled=True)]
    pallas_call x10 -> x11, Pallas kernels: 34.2 us -> 33.5 us  [run(): pl.pallas_call(kernel, out_shape=shapes if many else shapes[0], in_specs=...]
  transfers between devices with their start and end apart: 5 -> 8, of which waited for: 5 -> 6; matrix products, arithmetic and copies ran while one was open for 0% -> 0% of each run, Pallas kernels for 15% -> 15%
where the time goes in v6:
time: 135 us; the launch traced here: 134 us
  starting transfers between devices  40.2 us (30%)
  Pallas kernels  33.5 us (25%)
  waiting for transfers between devices  30 us (22%)
  blocking collectives  29.5 us (22%)
    pallas_call x11, Pallas kernels, run(): pl.pallas_call(kernel, out_shape=shapes if many else shapes[0], in_specs=...  33.5 us
    all_to_all x4, starting transfers between devices, exchange(): return lax.all_to_all(value, axes, split_axis=0, concat_axis=0, tiled=True)  31.7 us
    all_to_all x1, blocking collectives, exchange(): return lax.all_to_all(value, axes, split_axis=0, concat_axis=0, tiled=True)  29.5 us
    all_to_all x4, waiting for transfers between devices, exchange(): return lax.all_to_all(value, axes, split_axis=0, concat_axis=0, tiled=True)  19.2 us
    ppermute x4, waiting for transfers between devices, steps(): far = lax.ppermute(near, 'det', pairs)  10.7 us
    ppermute x4, starting transfers between devices, steps(): far = lax.ppermute(near, 'det', pairs)  8.54 us
  transfers between devices with their start and end apart: 8, of which 6 were waited for; matrix products, arithmetic and copies ran while one was open for 0% of the time, Pallas kernels for 15%

profile of v6, /device:TPU:1, one launch (start us, length us, event | category | flops | bytes accessed | tf_op | source)
XLA Modules:
  0.0 134.2 jit_solution(8323558991914995860)
XLA Ops:
  0.6 1.7 %shard_map.149 = f32[256,256]{1,0:T(8,128)} custom-call(f32[32,2048]{1,0:T(8,128)} %tod_ref.1), custom_call_target="tpu_custom_call" | custom-call | tf_op jit(solution)/shard_map/pallas_call | solution.py:466
  2.3 0.0 copy-start.5
  2.3 0.0 copy-start.12
  2.4 0.0 copy-start.8
  2.4 0.0 copy-start.9
  2.4 10.1 %all-to-all-start = ((f32[16,16,256]{2,1,0:T(8,128)}), f32[16,16,256]{2,1,0:T(8,128)S(1)}, u32[]{:S(2)}, u32[]{:S(2)}) async-start(f32[16,16,256]{2,1,0:T(8,128)} %bitcast.17), calls=%async_computation | async-start | bytes 524288 | tf_op jit(solution)/shard_map/all_to_all | solution.py:479
  12.5 0.0 copy-done.5
  12.5 0.0 copy-done.12
  12.5 0.0 copy-start.4
  12.5 0.1 shard_map.150
  12.6 0.0 copy-start.3
  12.6 1.4 %collective-permute-start = (f32[1,64,128]{2,1,0:T(8,128)S(1)}, f32[1,64,128]{2,1,0:T(8,128)S(1)}, u32[]{:S(2)}, u32[]{:S(2)}) collective-permute-start(f32[1,64,128]{2,1,0:T(8,128)S(1)} %get-tuple-element.13), channel_id=1, source_target_pairs={{0,16},{16,0},{32,48},{48,32},{64,80},{80,64},{96,112},{112,96},{1... | collective-permute-start | bytes 98312 | tf_op jit(solution)/shard_map/ppermute | solution.py:504
  14.0 1.5 %collective-permute-done = f32[1,64,128]{2,1,0:T(8,128)S(1)} collective-permute-done((f32[1,64,128]{2,1,0:T(8,128)S(1)}, f32[1,64,128]{2,1,0:T(8,128)S(1)}, u32[]{:S(2)}, u32[]{:S(2)}) %collective-permute-start) | collective-permute-done | bytes 32800 | tf_op jit(solution)/shard_map/ppermute | solution.py:504
  15.5 2.9 %collective-permute-start.1 = (f32[2,64,128]{2,1,0:T(8,128)S(1)}, f32[2,64,128]{2,1,0:T(8,128)S(1)}, u32[]{:S(2)}, u32[]{:S(2)}) collective-permute-start(f32[2,64,128]{2,1,0:T(8,128)S(1)} %pad_maximum_fusion.1), channel_id=1, source_target_pairs={{0,32},{16,48},{32,0},{48,16},{64,96},{80,112},{96,64},{112,80},{1... | collective-permute-start | bytes 196616 | tf_op jit(solution)/shard_map/ppermute | solution.py:504
  18.4 0.0 copy-start.11
  18.4 2.0 %collective-permute-done.1 = f32[2,64,128]{2,1,0:T(8,128)S(1)} collective-permute-done((f32[2,64,128]{2,1,0:T(8,128)S(1)}, f32[2,64,128]{2,1,0:T(8,128)S(1)}, u32[]{:S(2)}, u32[]{:S(2)}) %collective-permute-start.1) | collective-permute-done | bytes 65568 | tf_op jit(solution)/shard_map/ppermute | solution.py:504
  20.4 1.3 collective-permute-start.2
  21.7 2.4 %all-to-all-done.x_ref = f32[16,16,256]{2,1,0:T(8,128)S(1)} async-done(((f32[16,16,256]{2,1,0:T(8,128)}), f32[16,16,256]{2,1,0:T(8,128)S(1)}, u32[]{:S(2)}, u32[]{:S(2)}) %all-to-all-start) | async-done | bytes 262176 | tf_op jit(solution)/shard_map/all_to_all | solution.py:479
  24.1 0.0 copy-done.8
  24.1 0.0 copy-done.9
  24.1 0.0 copy-done.4
  24.1 0.0 copy-done.3
  24.1 0.0 copy-done.11
  24.1 2.0 %shard_map.151 = f32[512,128]{1,0:T(8,128)} custom-call(f32[16,16,256]{2,1,0:T(8,128)S(1)} %all-to-all-done.x_ref, f32[24,256]{1,0:T(8,128)S(1)} %get-tuple-element.12.scale_ref, f32[128,128]{1,0:T(8,128)S(1)} %copy-done.11, f32[256,128]{1,0:T(8,128)S(1)} %copy-done.8, f32[256,128]{1,0:T(8,128)S(1)} %copy-done.9, f32[128,512]{1,0:T(8,128)S(1)} %copy-done.3, ...), custom_call_target="tpu_custom_call" | custom-call | tf_op jit(solution)/shard_map/pallas_call | solution.py:466
  26.1 12.5 %all-to-all-start.1 = ((f32[256,2,128]{2,1,0:T(2,128)}), f32[256,2,128]{2,1,0:T(2,128)S(1)}, u32[]{:S(2)}, u32[]{:S(2)}) async-start(f32[256,2,128]{2,1,0:T(2,128)} %bitcast.1), calls=%async_computation.1 | async-start | bytes 524288 | tf_op jit(solution)/shard_map/all_to_all | solution.py:479
  38.7 0.0 collective-permute-done.2
  38.7 2.9 %collective-permute-start.3 = (f32[8,64,128]{2,1,0:T(8,128)S(1)}, f32[8,64,128]{2,1,0:T(8,128)S(1)}, u32[]{:S(2)}, u32[]{:S(2)}) collective-permute-start(f32[8,64,128]{2,1,0:T(8,128)S(1)} %constant_dynamic-update-slice_fusion.near_ref), channel_id=1, source_target_pairs={{0,128},{16,144},{32,160},{48,176},{64,192},{80,208},{96,224},{112... | collective-permute-start | bytes 786440 | tf_op jit(solution)/shard_map/ppermute | solution.py:504
  41.7 7.3 %collective-permute-done.3.far_ref = f32[8,64,128]{2,1,0:T(8,128)S(1)} collective-permute-done((f32[8,64,128]{2,1,0:T(8,128)S(1)}, f32[8,64,128]{2,1,0:T(8,128)S(1)}, u32[]{:S(2)}, u32[]{:S(2)}) %collective-permute-start.3) | collective-permute-done | bytes 262176 | tf_op jit(solution)/shard_map/ppermute | solution.py:504
  48.9 10.3 %shard_map.152 = (f32[2,256,256]{2,1,0:T(8,128)S(1)}, f32[2,256,256]{2,1,0:T(8,128)S(1)}) custom-call(f32[8,64,128]{2,1,0:T(8,128)S(1)} %constant_dynamic-update-slice_fusion.near_ref, f32[8,64,128]{2,1,0:T(8,128)S(1)} %collective-permute-done.3.far_ref), custom_call_target="tpu_custom_call" | custom-call | tf_op jit(solution)/shard_map/pallas_call | solution.py:466
  59.2 0.0 all-to-all-done.1
  59.2 0.0 copy-start.6
  59.2 0.0 copy-start.7
  59.3 0.0 copy-start.10
  59.3 1.9 %shard_map.153 = f32[512,128]{1,0:T(8,128)S(1)} custom-call(f32[512,128]{1,0:T(8,128)S(1)} %bitcast.13, f32[2,256,256]{2,1,0:T(8,128)S(1)} %get-tuple-element.14.trans_ref, f32[2,256,256]{2,1,0:T(8,128)S(1)} %get-tuple-element.15.gain_ref), custom_call_target="tpu_custom_call" | custom-call | tf_op jit(solution)/shard_map/pallas_call | solution.py:466
  61.2 0.0 copy-start.1
  61.2 0.0 copy-start.2
  61.2 29.5 %all_to_all.31 = f32[256,2,128]{2,1,0:T(2,128)S(1)} all-to-all(f32[256,2,128]{2,1,0:T(2,128)S(1)} %bitcast.15), channel_id=1, replica_groups=mesh['det'=16,'tm'=16] {'det','tm'}, dimensions={0} | all-to-all | bytes 524288 | tf_op jit(solution)/shard_map/all_to_all | solution.py:479
  90.7 0.0 copy-done.6
  90.7 0.0 copy-done.7
  90.7 0.0 copy-done.10
  90.7 0.0 copy-done.1
  90.8 0.0 copy-done.2
  90.8 1.5 %shard_map.154 = f32[16,16,256]{2,1,0:T(8,128)} custom-call(f32[512,128]{1,0:T(8,128)S(1)} %bitcast.14, f32[24,256]{1,0:T(8,128)S(1)} %get-tuple-element.12.scale_ref, f32[256,128]{1,0:T(8,128)S(1)} %copy-done.6, f32[256,128]{1,0:T(8,128)S(1)} %copy-done.7, bf16[2,256,256]{2,1,0:T(8,128)(2,1)S(1)} %copy-done.1, bf16[2,256,256]{2,1,0:T(8,128)(2,1)S(1)} %copy-done.2, ...), custom_call_target="tpu_custom_call" | custom-call | tf_op jit(solution)/shard_map/pallas_call | solution.py:466
  92.2 0.0 copy-start
  92.3 3.9 %all-to-all-start.3 = ((f32[16,16,256]{2,1,0:T(8,128)}), f32[16,16,256]{2,1,0:T(8,128)S(1)}, u32[]{:S(2)}, u32[]{:S(2)}) async-start(f32[16,16,256]{2,1,0:T(8,128)} %shard_map.154), calls=%async_computation.3 | async-start | bytes 524288 | tf_op jit(solution)/shard_map/all_to_all | solution.py:479
  96.2 0.0 copy-done
  96.2 3.4 %shard_map.156 = (f32[256,128]{1,0:T(8,128)S(1)}, f32[128,256]{1,0:T(8,128)S(1)}, f32[128,256]{1,0:T(8,128)S(1)}) custom-call(s32[32,2048]{1,0:T(8,128)S(1)} %copy-done), custom_call_target="tpu_custom_call" | custom-call | tf_op jit(solution)/shard_map/pallas_call | solution.py:466
  99.5 3.4 %shard_map.157 = (f32[256,128]{1,0:T(8,128)S(1)}, f32[128,256]{1,0:T(8,128)S(1)}, f32[128,256]{1,0:T(8,128)S(1)}) custom-call(s32[32,2048]{1,0:T(8,128)S(1)} %copy-done), custom_call_target="tpu_custom_call" | custom-call | tf_op jit(solution)/shard_map/pallas_call | solution.py:466
  102.9 5.0 %all-to-all-done.3 = f32[16,16,256]{2,1,0:T(8,128)S(1)} async-done(((f32[16,16,256]{2,1,0:T(8,128)}), f32[16,16,256]{2,1,0:T(8,128)S(1)}, u32[]{:S(2)}, u32[]{:S(2)}) %all-to-all-start.3) | async-done | bytes 262176 | tf_op jit(solution)/shard_map/all_to_all | solution.py:479
  107.9 7.9 %shard_map.158 = f32[256,128]{1,0:T(8,128)} custom-call(f32[256,256]{1,0:T(8,128)S(1)} %bitcast.11, f32[256,128]{1,0:T(8,128)S(1)} %get-tuple-element.16.refs_0_, f32[128,256]{1,0:T(8,128)S(1)} %get-tuple-element.17.refs_1_, f32[128,256]{1,0:T(8,128)S(1)} %get-tuple-element.18.refs_2_, f32[256,128]{1,0:T(8,128)S(1)} %get-tuple-element.19.refs_3_, ...), custom_call_target="tpu_custom_call" | custom-call | tf_op jit(solution)/shard_map/pallas_call | solution.py:466
  115.9 5.1 %all-to-all-start.4 = ((f32[256,1,128]{2,1,0:T(1,128)}), f32[256,1,128]{2,1,0:T(1,128)S(1)}, u32[]{:S(2)}, u32[]{:S(2)}) async-start(f32[256,1,128]{2,1,0:T(1,128)} %bitcast.7), calls=%async_computation.4 | async-start | bytes 262144 | tf_op jit(solution)/shard_map/all_to_all | solution.py:479
  121.0 0.8 shard_map.155
  121.8 11.8 %all-to-all-done.4 = f32[256,1,128]{2,1,0:T(1,128)S(1)} async-done(((f32[256,1,128]{2,1,0:T(1,128)}), f32[256,1,128]{2,1,0:T(1,128)S(1)}, u32[]{:S(2)}, u32[]{:S(2)}) %all-to-all-start.4) | async-done | bytes 131104 | tf_op jit(solution)/shard_map/all_to_all | solution.py:479
  133.6 0.6 shard_map.159
  (6 shorter events, 0.0 us)
Async XLA Ops:
  2.3 10.2 %copy-start.5 = (f32[8,32,128]{2,1,0:T(8,128)S(1)}, f32[8,32,128]{2,1,0:T(8,128)}, u32[]{:S(2)}) copy-start(f32[8,32,128]{2,1,0:T(8,128)} %modes_ref.1) | copy-start | bytes 393220
  2.3 10.2 %copy-start.12 = (f32[8,32]{1,0:T(8,128)S(1)}, f32[8,32]{1,0:T(8,128)}, u32[]{:S(2)}) copy-start(f32[8,32]{1,0:T(8,128)} %noise_ref.1) | copy-start | bytes 3076
  2.4 21.7 %copy-start.8 = (f32[256,128]{1,0:T(8,128)S(1)}, f32[256,128]{1,0:T(8,128)}, u32[]{:S(2)}) copy-start(f32[256,128]{1,0:T(8,128)} %constant.21.clone.keep_ref) | copy-start | bytes 393220
  2.4 21.7 %copy-start.9 = (f32[256,128]{1,0:T(8,128)S(1)}, f32[256,128]{1,0:T(8,128)}, u32[]{:S(2)}) copy-start(f32[256,128]{1,0:T(8,128)} %constant.22.clone.swap_ref) | copy-start | bytes 393220
  2.4 21.7 %all-to-all-start = ((f32[16,16,256]{2,1,0:T(8,128)}), f32[16,16,256]{2,1,0:T(8,128)S(1)}, u32[]{:S(2)}, u32[]{:S(2)}) async-start(f32[16,16,256]{2,1,0:T(8,128)} %bitcast.17), calls=%async_computation | async-start | bytes 524288 | tf_op jit(solution)/shard_map/all_to_all | solution.py:479
  12.5 11.6 %copy-start.4 = (f32[128,512]{1,0:T(8,128)S(1)}, f32[128,512]{1,0:T(8,128)}, u32[]{:S(2)}) copy-start(f32[128,512]{1,0:T(8,128)} %constant.24.clone.bottom_ref) | copy-start | bytes 786436
  12.6 11.5 %copy-start.3 = (f32[128,512]{1,0:T(8,128)S(1)}, f32[128,512]{1,0:T(8,128)}, u32[]{:S(2)}) copy-start(f32[128,512]{1,0:T(8,128)} %constant.23.clone.top_ref) | copy-start | bytes 786436
  12.6 2.9 %collective-permute-start = (f32[1,64,128]{2,1,0:T(8,128)S(1)}, f32[1,64,128]{2,1,0:T(8,128)S(1)}, u32[]{:S(2)}, u32[]{:S(2)}) collective-permute-start(f32[1,64,128]{2,1,0:T(8,128)S(1)} %get-tuple-element.13), channel_id=1, source_target_pairs={{0,16},{16,0},{32,48},{48,32},{64,80},{80,64},{96,112},{112,96},{1... | collective-permute-start | bytes 98312 | tf_op jit(solution)/shard_map/ppermute | solution.py:504
  15.5 4.9 %collective-permute-start.1 = (f32[2,64,128]{2,1,0:T(8,128)S(1)}, f32[2,64,128]{2,1,0:T(8,128)S(1)}, u32[]{:S(2)}, u32[]{:S(2)}) collective-permute-start(f32[2,64,128]{2,1,0:T(8,128)S(1)} %pad_maximum_fusion.1), channel_id=1, source_target_pairs={{0,32},{16,48},{32,0},{48,16},{64,96},{80,112},{96,64},{112,80},{1... | collective-permute-start | bytes 196616 | tf_op jit(solution)/shard_map/ppermute | solution.py:504
  18.4 5.7 %copy-start.11 = (f32[128,128]{1,0:T(8,128)S(1)}, f32[128,128]{1,0:T(8,128)}, u32[]{:S(2)}) copy-start(f32[128,128]{1,0:T(8,128)} %constant.20.clone.first_ref) | copy-start | bytes 196612
  20.4 18.3 %collective-permute-start.2 = (f32[4,64,128]{2,1,0:T(8,128)S(1)}, f32[4,64,128]{2,1,0:T(8,128)S(1)}, u32[]{:S(2)}, u32[]{:S(2)}) collective-permute-start(f32[4,64,128]{2,1,0:T(8,128)S(1)} %pad_maximum_fusion), channel_id=1, source_target_pairs={{0,64},{16,80},{32,96},{48,112},{64,0},{80,16},{96,32},{112,48},{1... | collective-permute-start | bytes 393224 | tf_op jit(solution)/shard_map/ppermute | solution.py:504
  26.1 33.1 %all-to-all-start.1 = ((f32[256,2,128]{2,1,0:T(2,128)}), f32[256,2,128]{2,1,0:T(2,128)S(1)}, u32[]{:S(2)}, u32[]{:S(2)}) async-start(f32[256,2,128]{2,1,0:T(2,128)} %bitcast.1), calls=%async_computation.1 | async-start | bytes 524288 | tf_op jit(solution)/shard_map/all_to_all | solution.py:479
  38.7 10.2 %collective-permute-start.3 = (f32[8,64,128]{2,1,0:T(8,128)S(1)}, f32[8,64,128]{2,1,0:T(8,128)S(1)}, u32[]{:S(2)}, u32[]{:S(2)}) collective-permute-start(f32[8,64,128]{2,1,0:T(8,128)S(1)} %constant_dynamic-update-slice_fusion.near_ref), channel_id=1, source_target_pairs={{0,128},{16,144},{32,160},{48,176},{64,192},{80,208},{96,224},{112... | collective-permute-start | bytes 786440 | tf_op jit(solution)/shard_map/ppermute | solution.py:504
  59.2 31.5 %copy-start.6 = (f32[256,128]{1,0:T(8,128)S(1)}, f32[256,128]{1,0:T(8,128)}, u32[]{:S(2)}) copy-start(f32[256,128]{1,0:T(8,128)} %constant.25.clone.keep_ref) | copy-start | bytes 393220
  59.2 31.5 %copy-start.7 = (f32[256,128]{1,0:T(8,128)S(1)}, f32[256,128]{1,0:T(8,128)}, u32[]{:S(2)}) copy-start(f32[256,128]{1,0:T(8,128)} %constant.26.clone.swap_ref) | copy-start | bytes 393220
  59.3 31.5 %copy-start.10 = (bf16[2,128,128]{2,1,0:T(8,128)(2,1)S(1)}, bf16[2,128,128]{2,1,0:T(8,128)(2,1)}, u32[]{:S(2)}) copy-start(bf16[2,128,128]{2,1,0:T(8,128)(2,1)} %constant.29.clone.last_ref) | copy-start | bytes 196612
  61.2 29.6 %copy-start.1 = (bf16[2,256,256]{2,1,0:T(8,128)(2,1)S(1)}, bf16[2,256,256]{2,1,0:T(8,128)(2,1)}, u32[]{:S(2)}) copy-start(bf16[2,256,256]{2,1,0:T(8,128)(2,1)} %constant.27.clone.top_ref) | copy-start | bytes 786436
  61.2 29.6 %copy-start.2 = (bf16[2,256,256]{2,1,0:T(8,128)(2,1)S(1)}, bf16[2,256,256]{2,1,0:T(8,128)(2,1)}, u32[]{:S(2)}) copy-start(bf16[2,256,256]{2,1,0:T(8,128)(2,1)} %constant.28.clone.bottom_ref) | copy-start | bytes 786436
  92.2 3.9 %copy-start = (s32[32,2048]{1,0:T(8,128)S(1)}, s32[32,2048]{1,0:T(8,128)}, u32[]{:S(2)}) copy-start(s32[32,2048]{1,0:T(8,128)} %point_ref.3) | copy-start | bytes 786436
  92.3 15.7 %all-to-all-start.3 = ((f32[16,16,256]{2,1,0:T(8,128)}), f32[16,16,256]{2,1,0:T(8,128)S(1)}, u32[]{:S(2)}, u32[]{:S(2)}) async-start(f32[16,16,256]{2,1,0:T(8,128)} %shard_map.154), calls=%async_computation.3 | async-start | bytes 524288 | tf_op jit(solution)/shard_map/all_to_all | solution.py:479
  115.9 17.7 %all-to-all-start.4 = ((f32[256,1,128]{2,1,0:T(1,128)}), f32[256,1,128]{2,1,0:T(1,128)S(1)}, u32[]{:S(2)}, u32[]{:S(2)}) async-start(f32[256,1,128]{2,1,0:T(1,128)} %bitcast.7), calls=%async_computation.4 | async-start | bytes 262144 | tf_op jit(solution)/shard_map/all_to_all | solution.py:479

commit v7 on v6

--- a/solution.py
+++ b/solution.py
@@ -24,7 +24,7 @@
 def _slots():
     dev, step = np.meshgrid(np.arange(16), np.arange(8), indexing="ij")
     top = (16 * step + dev).reshape(-1)
-    bottom = (16 * (step + 8) + dev).reshape(-1)
+    bottom = (16 * (15 - step) + dev).reshape(-1)
     return top, bottom
 
 
@@ -116,7 +116,7 @@
 
 def basis_kernel(modes_ref, noise_ref, v_out, scale_out, tmp_ref):
     _, pos = _position()
-    band = jnp.where(pos < BANDS, pos, 2 * BANDS - 1 - pos)
+    band = pos // 2
     root = lax.rsqrt(noise_ref[...])
     eye = lax.broadcasted_iota(jnp.int32, (32, 32), 0) == _lanes((32, 32))
     row_of = lax.broadcasted_iota(jnp.int32, (BANDS, 32), 0)
@@ -124,18 +124,14 @@
         row = jnp.sum(jnp.where(row_of == which, root, 0.0), axis=0, keepdims=True)
         col = jnp.sum(jnp.where(eye, row, 0.0), axis=1, keepdims=True)
         tmp_ref[part] = modes_ref[which] * col
-        for e in range(2):
-            low = 32 * part + 16 * e
-            v_out[0, low : low + 16, :] = tmp_ref[part, pl.ds(e, 16, stride=2), :]
-    flipped = jnp.concatenate([root[BANDS - 1 - j : BANDS - j] for j in range(BANDS)], axis=0)
+        even, odd = [tmp_ref[part, pl.ds(e, 16, stride=2), :] for e in range(2)]
+        v_out[0, 16 * part : 16 * part + 16, :] = jnp.where(pos % 2 == 0, even, odd)
     for e in range(2):
         mask = _lanes((BANDS, 32)) == 2 * pos + e
         lanes = pl.ds(128 * e, 128)
         up = jnp.sum(jnp.where(mask, root, 0.0), axis=1, keepdims=True)
-        down = jnp.sum(jnp.where(mask, flipped, 0.0), axis=1, keepdims=True)
         scale_out[0:8, lanes] = jnp.broadcast_to(up, (8, 128))
-        scale_out[8:16, lanes] = jnp.broadcast_to(down, (8, 128))
-        scale_out[16:24, lanes] = jnp.broadcast_to(up[7:8], (8, 128))
+        scale_out[8:16, lanes] = jnp.broadcast_to(up[7:8], (8, 128))
 
 
 def _spread_rows(source_ref, tmp_ref, octet):
@@ -165,7 +161,7 @@
 def _first_scale(scale_ref):
     lane = _lanes((8, 256)) % 128
     row = lax.broadcasted_iota(jnp.int32, (8, 256), 0)
-    return jnp.where((lane == 64) & (row == 0), scale_ref[16:24, :], scale_ref[0:8, :])
+    return jnp.where((lane == 64) & (row == 0), scale_ref[8:16, :], scale_ref[0:8, :])
 
 
 def forward_kernel(x_ref, scale_ref, first_ref, keep_ref, swap_ref, top_ref, bottom_ref, out_ref):
@@ -197,11 +193,11 @@
             up = (up + jnp.where(row0, nyq, 0.0)) * _first_scale(scale_ref)
         else:
             up = up * scale_ref[0:8, :]
-        down = out_bottom[8 * d : 8 * d + 8] * scale_ref[8:16, :]
+        down = out_bottom[8 * d : 8 * d + 8] * scale_ref[0:8, :]
         for e in range(2):
             cols = slice(128 * e, 128 * e + 128)
-            out_ref[pl.ds(32 * d + e, 8, stride=2), :] = up[:, cols]
-            out_ref[pl.ds(32 * d + 16 + e, 8, stride=2), :] = down[:, cols]
+            out_ref[pl.ds(32 * d + e, 8, stride=4), :] = up[:, cols]
+            out_ref[pl.ds(32 * d + 2 + e, 8, stride=4), :] = down[:, cols]
 
 
 def _pair_inverse(a, b, c):
@@ -274,15 +270,17 @@
     lax.fori_loop(0, 32, step, 0)
 
 
-def gram_kernel(near_ref, far_ref, trans_ref, gain_ref, vees_ref, *mat_refs):
-    dev, _ = _position()
+def gram_kernel(near_ref, far_ref, other_ref, trans_ref, gain_ref, vees_ref, *mat_refs):
+    dev, pos = _position()
+    parity = pos % 2
     for j in range(16):
-        source = near_ref if j < 8 else far_ref
+        own = near_ref if j < 8 else far_ref
         rows = pl.ds(pl.multiple_of((dev ^ j) * 16, 16), 16)
-        for e in range(2):
-            for part in range(2):
-                low = 32 * part + 16 * e
-                vees_ref[e, rows, 128 * part : 128 * part + 128] = source[j % 8, low : low + 16, :]
+        for part in range(2):
+            cols = slice(128 * part, 128 * part + 128)
+            low = slice(16 * part, 16 * part + 16)
+            vees_ref[parity, rows, cols] = own[j % 8, low, :]
+            vees_ref[1 - parity, rows, cols] = other_ref[j, low, :]
     parts = [[vees_ref[e, :, 128 * part : 128 * part + 128] for part in range(2)] for e in range(2)]
     eye = lax.broadcasted_iota(jnp.int32, (128, 128), 0) == _lanes((128, 128))
     for part in range(2):
@@ -317,12 +315,12 @@
     for d in range(16):
         up, down = [
             jnp.concatenate(
-                [y_ref[pl.ds(32 * d + 16 * half + e, 8, stride=2), :] for e in range(2)], axis=1
+                [y_ref[pl.ds(32 * d + 2 * half + e, 8, stride=4), :] for e in range(2)], axis=1
             )
             for half in range(2)
         ]
         ups.append(up * (_first_scale(scale_ref) if d == 0 else scale_ref[0:8, :]))
-        downs.append(down * scale_ref[8:16, :])
+        downs.append(down * scale_ref[0:8, :])
     top = jnp.concatenate(ups, axis=0)
     bottom = jnp.concatenate(downs, axis=0)
 
@@ -484,7 +482,7 @@
     inverse = [jnp.asarray(a) for a in _inverse_tables()]
     send_v, scale = call(
         basis_kernel,
-        [((1, 64, 128), F32), ((24, 256), F32)],
+        [((1, 32, 128), F32), ((16, 256), F32)],
         scratch=[pltpu.VMEM((2, 32, 128), F32)],
     )(modes, noise_level)
     send_tod = call(
@@ -504,6 +502,8 @@
         far = lax.ppermute(near, "det", pairs)
         if bit < 3:
             near = jnp.concatenate([near, far], axis=0)
+    gathered = jnp.concatenate([near, far], axis=0)
+    other = lax.ppermute(gathered, "tm", [(i, i ^ 1) for i in range(16)])
     got_tod = exchange(send_tod, "tm")
     spectra = call(forward_kernel, ((512, 128), F32))(got_tod, scale, *forward)
     trans, gain = call(
@@ -514,7 +514,7 @@
             pltpu.VMEM((128, 128), F32),
             pltpu.VMEM((128, 128), F32),
         ],
-    )(near, far)
+    )(near, far, other)
     mixed = exchange(spectra.reshape(256, 2, 128), ("det", "tm")).reshape(512, 128)
     weighted = call(apply_kernel, ((512, 128), F32))(mixed, trans, gain)
     counted = [

time: 135 us -> 133 us (0.985)
  blocking collectives: 29.5 us -> 27.6 us
  local copies, waits for them, and re-layouts: 0.11 us -> 1.68 us
    ppermute x4, waiting for transfers between devices: 10.7 us -> 5.51 us  [steps(): far = lax.ppermute(near, 'det', pairs)]
    all_to_all x4, starting transfers between devices: 31.7 us -> 27 us  [exchange(): return lax.all_to_all(value, axes, split_axis=0, concat_axis=0, tiled=True)]
    all_to_all x4, waiting for transfers between devices: 19.2 us -> 22.8 us  [exchange(): return lax.all_to_all(value, axes, split_axis=0, concat_axis=0, tiled=True)]
    ppermute x0 -> x1, starting transfers between devices: none -> 3.02 us  [steps(): other = lax.ppermute(gathered, 'tm', [(i, i ^ 1) for i in range(16)])]
    all_to_all x1, blocking collectives: 29.5 us -> 27.6 us  [exchange(): return lax.all_to_all(value, axes, split_axis=0, concat_axis=0, tiled=True)]
    unnamed x29 -> x30, local copies, waits for them, and re-layouts: 0.1 us -> 1.67 us
  transfers between devices with their start and end apart: 8 -> 9, of which waited for: 6 -> 6; matrix products, arithmetic and copies ran while one was open for 0% -> 0% of each run, Pallas kernels for 15% -> 16%
where the time goes in v7:
time: 133 us; the launch traced here: 132 us
  starting transfers between devices  39.1 us (29%)
  Pallas kernels  33.5 us (25%)
  waiting for transfers between devices  29.5 us (22%)
  blocking collectives  27.6 us (21%)
  local copies, waits for them, and re-layouts  1.68 us (1%)
    pallas_call x11, Pallas kernels, run(): pl.pallas_call(kernel, out_shape=shapes if many else shapes[0], in_specs=...  33.5 us
    all_to_all x1, blocking collectives, exchange(): return lax.all_to_all(value, axes, split_axis=0, concat_axis=0, tiled=True)  27.6 us
    all_to_all x4, starting transfers between devices, exchange(): return lax.all_to_all(value, axes, split_axis=0, concat_axis=0, tiled=True)  27 us
    all_to_all x4, waiting for transfers between devices, exchange(): return lax.all_to_all(value, axes, split_axis=0, concat_axis=0, tiled=True)  22.8 us
    ppermute x4, starting transfers between devices, steps(): far = lax.ppermute(near, 'det', pairs)  9.06 us
    ppermute x4, waiting for transfers between devices, steps(): far = lax.ppermute(near, 'det', pairs)  5.51 us
    ppermute x1, starting transfers between devices, steps(): other = lax.ppermute(gathered, 'tm', [(i, i ^ 1) for i in range(16)])  3.02 us
  transfers between devices with their start and end apart: 9, of which 6 were waited for; matrix products, arithmetic and copies ran while one was open for 0% of the time, Pallas kernels for 16%

profile of v7, /device:TPU:1, one launch (start us, length us, event | category | flops | bytes accessed | tf_op | source)
XLA Modules:
  0.0 132.2 jit_solution(2275554958766074666)
XLA Ops:
  0.6 0.0 copy-start.5
  0.6 0.9 copy-done.5
  1.5 0.0 copy-start.12
  1.5 0.7 copy-done.12
  2.2 0.1 shard_map.150
  2.3 2.2 %collective-permute-start = (f32[1,32,128]{2,1,0:T(8,128)S(1)}, f32[1,32,128]{2,1,0:T(8,128)S(1)}, u32[]{:S(2)}, u32[]{:S(2)}) collective-permute-start(f32[1,32,128]{2,1,0:T(8,128)S(1)} %get-tuple-element.13), channel_id=1, source_target_pairs={{0,16},{16,0},{32,48},{48,32},{64,80},{80,64},{96,112},{112,96},{1... | collective-permute-start | bytes 49160 | tf_op jit(solution)/shard_map/ppermute | solution.py:502
  4.5 1.7 %shard_map.149 = f32[256,256]{1,0:T(8,128)} custom-call(f32[32,2048]{1,0:T(8,128)} %tod_ref.1), custom_call_target="tpu_custom_call" | custom-call | tf_op jit(solution)/shard_map/pallas_call | solution.py:464
  6.2 0.0 copy-start.4
  6.2 0.0 copy-start.9
  6.3 0.0 copy-start.11
  6.3 9.6 %all-to-all-start = ((f32[16,16,256]{2,1,0:T(8,128)}), f32[16,16,256]{2,1,0:T(8,128)S(1)}, u32[]{:S(2)}, u32[]{:S(2)}) async-start(f32[16,16,256]{2,1,0:T(8,128)} %bitcast.17), calls=%async_computation | async-start | bytes 524288 | tf_op jit(solution)/shard_map/all_to_all | solution.py:477
  15.8 0.0 copy-start.3
  15.9 0.0 collective-permute-done
  15.9 2.7 %collective-permute-start.1 = (f32[2,32,128]{2,1,0:T(8,128)S(1)}, f32[2,32,128]{2,1,0:T(8,128)S(1)}, u32[]{:S(2)}, u32[]{:S(2)}) collective-permute-start(f32[2,32,128]{2,1,0:T(8,128)S(1)} %pad_maximum_fusion.1), channel_id=1, source_target_pairs={{0,32},{16,48},{32,0},{48,16},{64,96},{80,112},{96,64},{112,80},{1... | collective-permute-start | bytes 98312 | tf_op jit(solution)/shard_map/ppermute | solution.py:502
  18.6 0.0 copy-start.8
  18.6 1.6 %collective-permute-done.1 = f32[2,32,128]{2,1,0:T(8,128)S(1)} collective-permute-done((f32[2,32,128]{2,1,0:T(8,128)S(1)}, f32[2,32,128]{2,1,0:T(8,128)S(1)}, u32[]{:S(2)}, u32[]{:S(2)}) %collective-permute-start.1) | collective-permute-done | bytes 32800 | tf_op jit(solution)/shard_map/ppermute | solution.py:502
  20.3 1.2 collective-permute-start.2
  21.5 6.0 %all-to-all-done.x_ref = f32[16,16,256]{2,1,0:T(8,128)S(1)} async-done(((f32[16,16,256]{2,1,0:T(8,128)}), f32[16,16,256]{2,1,0:T(8,128)S(1)}, u32[]{:S(2)}, u32[]{:S(2)}) %all-to-all-start) | async-done | bytes 262176 | tf_op jit(solution)/shard_map/all_to_all | solution.py:477
  27.4 0.0 copy-done.4
  27.4 0.0 copy-done.9
  27.4 0.0 copy-done.11
  27.4 0.0 copy-done.3
  27.5 0.0 copy-done.8
  27.5 2.0 %shard_map.151 = f32[512,128]{1,0:T(8,128)} custom-call(f32[16,16,256]{2,1,0:T(8,128)S(1)} %all-to-all-done.x_ref, f32[16,256]{1,0:T(8,128)S(1)} %get-tuple-element.12.scale_ref, f32[128,128]{1,0:T(8,128)S(1)} %copy-done.11, f32[256,128]{1,0:T(8,128)S(1)} %copy-done.8, f32[256,128]{1,0:T(8,128)S(1)} %copy-done.9, f32[128,512]{1,0:T(8,128)S(1)} %copy-done.3, ...), custom_call_target="tpu_custom_call" | custom-call | tf_op jit(solution)/shard_map/pallas_call | solution.py:464
  29.4 8.4 %all-to-all-start.1 = ((f32[256,2,128]{2,1,0:T(2,128)}), f32[256,2,128]{2,1,0:T(2,128)S(1)}, u32[]{:S(2)}, u32[]{:S(2)}) async-start(f32[256,2,128]{2,1,0:T(2,128)} %bitcast.1), calls=%async_computation.1 | async-start | bytes 524288 | tf_op jit(solution)/shard_map/all_to_all | solution.py:477
  37.8 0.0 collective-permute-done.2
  37.8 2.9 %collective-permute-start.3 = (f32[8,32,128]{2,1,0:T(8,128)S(1)}, f32[8,32,128]{2,1,0:T(8,128)S(1)}, u32[]{:S(2)}, u32[]{:S(2)}) collective-permute-start(f32[8,32,128]{2,1,0:T(8,128)S(1)} %get-tuple-element.23.near_ref), channel_id=1, source_target_pairs={{0,128},{16,144},{32,160},{48,176},{64,192},{80,208},{96,224},{112... | collective-permute-start | bytes 393224 | tf_op jit(solution)/shard_map/ppermute | solution.py:502
  40.8 3.9 %collective-permute-done.3.far_ref = f32[8,32,128]{2,1,0:T(8,128)S(1)} collective-permute-done((f32[8,32,128]{2,1,0:T(8,128)S(1)}, f32[8,32,128]{2,1,0:T(8,128)S(1)}, u32[]{:S(2)}, u32[]{:S(2)}) %collective-permute-start.3) | collective-permute-done | bytes 131104 | tf_op jit(solution)/shard_map/ppermute | solution.py:502
  44.7 3.0 %collective-permute-start.4 = (f32[16,32,128]{2,1,0:T(8,128)S(1)}, f32[16,32,128]{2,1,0:T(8,128)S(1)}, u32[]{:S(2)}, u32[]{:S(2)}) collective-permute-start(f32[16,32,128]{2,1,0:T(8,128)S(1)} %constant_dynamic-update-slice_fusion.4), channel_id=1, source_target_pairs={{0,1},{1,0},{2,3},{3,2},{4,5},{5,4},{6,7},{7,6},{8,9},{9,8},{10,11... | collective-permute-start | bytes 786440 | tf_op jit(solution)/shard_map/ppermute | solution.py:506
  47.7 1.2 collective-permute-done.4.other_ref
  48.9 10.3 %shard_map.152 = (f32[2,256,256]{2,1,0:T(8,128)S(1)}, f32[2,256,256]{2,1,0:T(8,128)S(1)}) custom-call(f32[8,32,128]{2,1,0:T(8,128)S(1)} %get-tuple-element.23.near_ref, f32[8,32,128]{2,1,0:T(8,128)S(1)} %collective-permute-done.3.far_ref, f32[16,32,128]{2,1,0:T(8,128)S(1)} %collective-permute-done.4.other_ref), custom_call_target="tpu_custom_call" | custom-call | tf_op jit(solution)/shard_map/pallas_call | solution.py:464
  59.1 0.0 all-to-all-done.1
  59.2 0.0 copy-start.6
  59.2 0.0 copy-start.7
  59.2 0.0 copy-start.10
  59.2 1.9 %shard_map.153 = f32[512,128]{1,0:T(8,128)S(1)} custom-call(f32[512,128]{1,0:T(8,128)S(1)} %bitcast.13, f32[2,256,256]{2,1,0:T(8,128)S(1)} %get-tuple-element.14.trans_ref, f32[2,256,256]{2,1,0:T(8,128)S(1)} %get-tuple-element.15.gain_ref), custom_call_target="tpu_custom_call" | custom-call | tf_op jit(solution)/shard_map/pallas_call | solution.py:464
  61.1 0.0 copy-start.1
  61.1 0.0 copy-start.2
  61.1 27.6 %all_to_all.31 = f32[256,2,128]{2,1,0:T(2,128)S(1)} all-to-all(f32[256,2,128]{2,1,0:T(2,128)S(1)} %bitcast.15), channel_id=1, replica_groups=mesh['det'=16,'tm'=16] {'det','tm'}, dimensions={0} | all-to-all | bytes 524288 | tf_op jit(solution)/shard_map/all_to_all | solution.py:477
  88.7 0.0 copy-done.6
  88.7 0.0 copy-done.7
  88.7 0.0 copy-done.10
  88.7 0.0 copy-done.1
  88.7 0.0 copy-done.2
  88.7 1.5 %shard_map.154 = f32[16,16,256]{2,1,0:T(8,128)} custom-call(f32[512,128]{1,0:T(8,128)S(1)} %bitcast.14, f32[16,256]{1,0:T(8,128)S(1)} %get-tuple-element.12.scale_ref, f32[256,128]{1,0:T(8,128)S(1)} %copy-done.6, f32[256,128]{1,0:T(8,128)S(1)} %copy-done.7, bf16[2,256,256]{2,1,0:T(8,128)(2,1)S(1)} %copy-done.1, bf16[2,256,256]{2,1,0:T(8,128)(2,1)S(1)} %copy-done.2, ...), custom_call_target="tpu_custom_call" | custom-call | tf_op jit(solution)/shard_map/pallas_call | solution.py:464
  90.2 0.0 copy-start
  90.2 3.9 %all-to-all-start.3 = ((f32[16,16,256]{2,1,0:T(8,128)}), f32[16,16,256]{2,1,0:T(8,128)S(1)}, u32[]{:S(2)}, u32[]{:S(2)}) async-start(f32[16,16,256]{2,1,0:T(8,128)} %shard_map.154), calls=%async_computation.3 | async-start | bytes 524288 | tf_op jit(solution)/shard_map/all_to_all | solution.py:477
  94.1 0.0 copy-done
  94.1 3.4 %shard_map.156 = (f32[256,128]{1,0:T(8,128)S(1)}, f32[128,256]{1,0:T(8,128)S(1)}, f32[128,256]{1,0:T(8,128)S(1)}) custom-call(s32[32,2048]{1,0:T(8,128)S(1)} %copy-done), custom_call_target="tpu_custom_call" | custom-call | tf_op jit(solution)/shard_map/pallas_call | solution.py:464
  97.5 3.4 %shard_map.157 = (f32[256,128]{1,0:T(8,128)S(1)}, f32[128,256]{1,0:T(8,128)S(1)}, f32[128,256]{1,0:T(8,128)S(1)}) custom-call(s32[32,2048]{1,0:T(8,128)S(1)} %copy-done), custom_call_target="tpu_custom_call" | custom-call | tf_op jit(solution)/shard_map/pallas_call | solution.py:464
  100.9 5.1 %all-to-all-done.3 = f32[16,16,256]{2,1,0:T(8,128)S(1)} async-done(((f32[16,16,256]{2,1,0:T(8,128)}), f32[16,16,256]{2,1,0:T(8,128)S(1)}, u32[]{:S(2)}, u32[]{:S(2)}) %all-to-all-start.3) | async-done | bytes 262176 | tf_op jit(solution)/shard_map/all_to_all | solution.py:477
  105.9 7.9 %shard_map.158 = f32[256,128]{1,0:T(8,128)} custom-call(f32[256,256]{1,0:T(8,128)S(1)} %bitcast.11, f32[256,128]{1,0:T(8,128)S(1)} %get-tuple-element.16.refs_0_, f32[128,256]{1,0:T(8,128)S(1)} %get-tuple-element.17.refs_1_, f32[128,256]{1,0:T(8,128)S(1)} %get-tuple-element.18.refs_2_, f32[256,128]{1,0:T(8,128)S(1)} %get-tuple-element.19.refs_3_, ...), custom_call_target="tpu_custom_call" | custom-call | tf_op jit(solution)/shard_map/pallas_call | solution.py:464
  113.9 5.1 %all-to-all-start.4 = ((f32[256,1,128]{2,1,0:T(1,128)}), f32[256,1,128]{2,1,0:T(1,128)S(1)}, u32[]{:S(2)}, u32[]{:S(2)}) async-start(f32[256,1,128]{2,1,0:T(1,128)} %bitcast.7), calls=%async_computation.4 | async-start | bytes 262144 | tf_op jit(solution)/shard_map/all_to_all | solution.py:477
  119.0 0.8 shard_map.155
  119.8 11.8 %all-to-all-done.4 = f32[256,1,128]{2,1,0:T(1,128)S(1)} async-done(((f32[256,1,128]{2,1,0:T(1,128)}), f32[256,1,128]{2,1,0:T(1,128)S(1)}, u32[]{:S(2)}, u32[]{:S(2)}) %all-to-all-start.4) | async-done | bytes 131104 | tf_op jit(solution)/shard_map/all_to_all | solution.py:477
  131.6 0.6 shard_map.159
  (7 shorter events, 0.0 us)
Async XLA Ops:
  0.6 0.9 copy-start.5
  1.5 0.7 copy-start.12
  2.3 13.5 %collective-permute-start = (f32[1,32,128]{2,1,0:T(8,128)S(1)}, f32[1,32,128]{2,1,0:T(8,128)S(1)}, u32[]{:S(2)}, u32[]{:S(2)}) collective-permute-start(f32[1,32,128]{2,1,0:T(8,128)S(1)} %get-tuple-element.13), channel_id=1, source_target_pairs={{0,16},{16,0},{32,48},{48,32},{64,80},{80,64},{96,112},{112,96},{1... | collective-permute-start | bytes 49160 | tf_op jit(solution)/shard_map/ppermute | solution.py:502
  6.2 21.2 %copy-start.4 = (f32[128,512]{1,0:T(8,128)S(1)}, f32[128,512]{1,0:T(8,128)}, u32[]{:S(2)}) copy-start(f32[128,512]{1,0:T(8,128)} %constant.24.clone.bottom_ref) | copy-start | bytes 786436
  6.2 21.2 %copy-start.9 = (f32[256,128]{1,0:T(8,128)S(1)}, f32[256,128]{1,0:T(8,128)}, u32[]{:S(2)}) copy-start(f32[256,128]{1,0:T(8,128)} %constant.22.clone.swap_ref) | copy-start | bytes 393220
  6.3 21.2 %copy-start.11 = (f32[128,128]{1,0:T(8,128)S(1)}, f32[128,128]{1,0:T(8,128)}, u32[]{:S(2)}) copy-start(f32[128,128]{1,0:T(8,128)} %constant.20.clone.first_ref) | copy-start | bytes 196612
  6.3 21.2 %all-to-all-start = ((f32[16,16,256]{2,1,0:T(8,128)}), f32[16,16,256]{2,1,0:T(8,128)S(1)}, u32[]{:S(2)}, u32[]{:S(2)}) async-start(f32[16,16,256]{2,1,0:T(8,128)} %bitcast.17), calls=%async_computation | async-start | bytes 524288 | tf_op jit(solution)/shard_map/all_to_all | solution.py:477
  15.8 11.6 %copy-start.3 = (f32[128,512]{1,0:T(8,128)S(1)}, f32[128,512]{1,0:T(8,128)}, u32[]{:S(2)}) copy-start(f32[128,512]{1,0:T(8,128)} %constant.23.clone.top_ref) | copy-start | bytes 786436
  15.9 4.4 %collective-permute-start.1 = (f32[2,32,128]{2,1,0:T(8,128)S(1)}, f32[2,32,128]{2,1,0:T(8,128)S(1)}, u32[]{:S(2)}, u32[]{:S(2)}) collective-permute-start(f32[2,32,128]{2,1,0:T(8,128)S(1)} %pad_maximum_fusion.1), channel_id=1, source_target_pairs={{0,32},{16,48},{32,0},{48,16},{64,96},{80,112},{96,64},{112,80},{1... | collective-permute-start | bytes 98312 | tf_op jit(solution)/shard_map/ppermute | solution.py:502
  18.6 8.9 %copy-start.8 = (f32[256,128]{1,0:T(8,128)S(1)}, f32[256,128]{1,0:T(8,128)}, u32[]{:S(2)}) copy-start(f32[256,128]{1,0:T(8,128)} %constant.21.clone.keep_ref) | copy-start | bytes 393220
  20.3 17.6 %collective-permute-start.2 = (f32[4,32,128]{2,1,0:T(8,128)S(1)}, f32[4,32,128]{2,1,0:T(8,128)S(1)}, u32[]{:S(2)}, u32[]{:S(2)}) collective-permute-start(f32[4,32,128]{2,1,0:T(8,128)S(1)} %pad_maximum_fusion), channel_id=1, source_target_pairs={{0,64},{16,80},{32,96},{48,112},{64,0},{80,16},{96,32},{112,48},{1... | collective-permute-start | bytes 196616 | tf_op jit(solution)/shard_map/ppermute | solution.py:502
  29.4 29.7 %all-to-all-start.1 = ((f32[256,2,128]{2,1,0:T(2,128)}), f32[256,2,128]{2,1,0:T(2,128)S(1)}, u32[]{:S(2)}, u32[]{:S(2)}) async-start(f32[256,2,128]{2,1,0:T(2,128)} %bitcast.1), calls=%async_computation.1 | async-start | bytes 524288 | tf_op jit(solution)/shard_map/all_to_all | solution.py:477
  37.8 6.8 %collective-permute-start.3 = (f32[8,32,128]{2,1,0:T(8,128)S(1)}, f32[8,32,128]{2,1,0:T(8,128)S(1)}, u32[]{:S(2)}, u32[]{:S(2)}) collective-permute-start(f32[8,32,128]{2,1,0:T(8,128)S(1)} %get-tuple-element.23.near_ref), channel_id=1, source_target_pairs={{0,128},{16,144},{32,160},{48,176},{64,192},{80,208},{96,224},{112... | collective-permute-start | bytes 393224 | tf_op jit(solution)/shard_map/ppermute | solution.py:502
  44.7 4.2 %collective-permute-start.4 = (f32[16,32,128]{2,1,0:T(8,128)S(1)}, f32[16,32,128]{2,1,0:T(8,128)S(1)}, u32[]{:S(2)}, u32[]{:S(2)}) collective-permute-start(f32[16,32,128]{2,1,0:T(8,128)S(1)} %constant_dynamic-update-slice_fusion.4), channel_id=1, source_target_pairs={{0,1},{1,0},{2,3},{3,2},{4,5},{5,4},{6,7},{7,6},{8,9},{9,8},{10,11... | collective-permute-start | bytes 786440 | tf_op jit(solution)/shard_map/ppermute | solution.py:506
  59.2 29.6 %copy-start.6 = (f32[256,128]{1,0:T(8,128)S(1)}, f32[256,128]{1,0:T(8,128)}, u32[]{:S(2)}) copy-start(f32[256,128]{1,0:T(8,128)} %constant.25.clone.keep_ref) | copy-start | bytes 393220
  59.2 29.5 %copy-start.7 = (f32[256,128]{1,0:T(8,128)S(1)}, f32[256,128]{1,0:T(8,128)}, u32[]{:S(2)}) copy-start(f32[256,128]{1,0:T(8,128)} %constant.26.clone.swap_ref) | copy-start | bytes 393220
  59.2 29.5 %copy-start.10 = (bf16[2,128,128]{2,1,0:T(8,128)(2,1)S(1)}, bf16[2,128,128]{2,1,0:T(8,128)(2,1)}, u32[]{:S(2)}) copy-start(bf16[2,128,128]{2,1,0:T(8,128)(2,1)} %constant.29.clone.last_ref) | copy-start | bytes 196612
  61.1 27.6 %copy-start.1 = (bf16[2,256,256]{2,1,0:T(8,128)(2,1)S(1)}, bf16[2,256,256]{2,1,0:T(8,128)(2,1)}, u32[]{:S(2)}) copy-start(bf16[2,256,256]{2,1,0:T(8,128)(2,1)} %constant.27.clone.top_ref) | copy-start | bytes 786436
  61.1 27.6 %copy-start.2 = (bf16[2,256,256]{2,1,0:T(8,128)(2,1)S(1)}, bf16[2,256,256]{2,1,0:T(8,128)(2,1)}, u32[]{:S(2)}) copy-start(bf16[2,256,256]{2,1,0:T(8,128)(2,1)} %constant.28.clone.bottom_ref) | copy-start | bytes 786436
  90.2 3.9 %copy-start = (s32[32,2048]{1,0:T(8,128)S(1)}, s32[32,2048]{1,0:T(8,128)}, u32[]{:S(2)}) copy-start(s32[32,2048]{1,0:T(8,128)} %point_ref.3) | copy-start | bytes 786436
  90.2 15.7 %all-to-all-start.3 = ((f32[16,16,256]{2,1,0:T(8,128)}), f32[16,16,256]{2,1,0:T(8,128)S(1)}, u32[]{:S(2)}, u32[]{:S(2)}) async-start(f32[16,16,256]{2,1,0:T(8,128)} %shard_map.154), calls=%async_computation.3 | async-start | bytes 524288 | tf_op jit(solution)/shard_map/all_to_all | solution.py:477
  113.9 17.7 %all-to-all-start.4 = ((f32[256,1,128]{2,1,0:T(1,128)}), f32[256,1,128]{2,1,0:T(1,128)S(1)}, u32[]{:S(2)}, u32[]{:S(2)}) async-start(f32[256,1,128]{2,1,0:T(1,128)} %bitcast.7), calls=%async_computation.4 | async-start | bytes 262144 | tf_op jit(solution)/shard_map/all_to_all | solution.py:477

commit v8 on v6

--- a/solution.py
+++ b/solution.py
@@ -114,16 +114,25 @@
     return lax.axis_index("det"), lax.axis_index("tm")
 
 
-def basis_kernel(modes_ref, noise_ref, v_out, scale_out, tmp_ref):
+def basis_kernel(modes_hbm, noise_hbm, v_out, scale_out, tmp_ref, modes_ref, noise_ref, sems):
     _, pos = _position()
     band = jnp.where(pos < BANDS, pos, 2 * BANDS - 1 - pos)
+    copies = [
+        pltpu.make_async_copy(noise_hbm, noise_ref, sems.at[0]),
+        pltpu.make_async_copy(modes_hbm.at[band], modes_ref.at[0], sems.at[1]),
+        pltpu.make_async_copy(modes_hbm.at[BANDS - 1], modes_ref.at[1], sems.at[2]),
+    ]
+    for copy in copies:
+        copy.start()
+    for copy in copies:
+        copy.wait()
     root = lax.rsqrt(noise_ref[...])
     eye = lax.broadcasted_iota(jnp.int32, (32, 32), 0) == _lanes((32, 32))
     row_of = lax.broadcasted_iota(jnp.int32, (BANDS, 32), 0)
     for part, which in enumerate((band, BANDS - 1)):
         row = jnp.sum(jnp.where(row_of == which, root, 0.0), axis=0, keepdims=True)
         col = jnp.sum(jnp.where(eye, row, 0.0), axis=1, keepdims=True)
-        tmp_ref[part] = modes_ref[which] * col
+        tmp_ref[part] = modes_ref[part] * col
         for e in range(2):
             low = 32 * part + 16 * e
             v_out[0, low : low + 16, :] = tmp_ref[part, pl.ds(e, 16, stride=2), :]
@@ -485,7 +494,14 @@
     send_v, scale = call(
         basis_kernel,
         [((1, 64, 128), F32), ((24, 256), F32)],
-        scratch=[pltpu.VMEM((2, 32, 128), F32)],
+        scratch=[
+            pltpu.VMEM((2, 32, 128), F32),
+            pltpu.VMEM((2, 32, 128), F32),
+            pltpu.VMEM((BANDS, 32), F32),
+            pltpu.SemaphoreType.DMA((3,)),
+        ],
+        space=HBM,
+        grant=WIDE_GRANT,
     )(modes, noise_level)
     send_tod = call(
         prep_kernel,

time: 135 us -> 138 us (1.022)
  waiting for transfers between devices: 30 us -> 27.3 us
  starting transfers between devices: 40.2 us -> 42.3 us
  other arithmetic: 0.01 us -> 1.53 us
  Pallas kernels: 33.5 us -> 34.9 us
    all_to_all x4, waiting for transfers between devices: 19.2 us -> 16.8 us  [exchange(): return lax.all_to_all(value, axes, split_axis=0, concat_axis=0, tiled=True)]
    all_to_all x4, starting transfers between devices: 31.7 us -> 33.8 us  [exchange(): return lax.all_to_all(value, axes, split_axis=0, concat_axis=0, tiled=True)]
    concatenate x2, other arithmetic: 0.01 us -> 1.53 us  [steps(): near = jnp.concatenate([near, far], axis=0)]
    pallas_call x11, Pallas kernels: 33.5 us -> 34.9 us  [run(): pl.pallas_call(kernel, out_shape=shapes if many else shapes[0], in_specs=...]
  transfers between devices with their start and end apart: 8 -> 8, of which waited for: 6 -> 5; matrix products, arithmetic and copies ran while one was open for 0% -> 2% of each run, Pallas kernels for 15% -> 16%
where the time goes in v8:
time: 138 us; the launch traced here: 137 us
  starting transfers between devices  42.3 us (31%)
  Pallas kernels  34.9 us (25%)
  blocking collectives  29.5 us (21%)
  waiting for transfers between devices  27.3 us (20%)
  other arithmetic  1.53 us (1%)
    pallas_call x11, Pallas kernels, run(): pl.pallas_call(kernel, out_shape=shapes if many else shapes[0], in_specs=...  34.9 us
    all_to_all x4, starting transfers between devices, exchange(): return lax.all_to_all(value, axes, split_axis=0, concat_axis=0, tiled=True)  33.8 us
    all_to_all x1, blocking collectives, exchange(): return lax.all_to_all(value, axes, split_axis=0, concat_axis=0, tiled=True)  29.5 us
    all_to_all x4, waiting for transfers between devices, exchange(): return lax.all_to_all(value, axes, split_axis=0, concat_axis=0, tiled=True)  16.8 us
    ppermute x4, waiting for transfers between devices, steps(): far = lax.ppermute(near, 'det', pairs)  10.5 us
    ppermute x4, starting transfers between devices, steps(): far = lax.ppermute(near, 'det', pairs)  8.54 us
  transfers between devices with their start and end apart: 8, of which 5 were waited for; matrix products, arithmetic and copies ran while one was open for 2% of the time, Pallas kernels for 16%

profile of v8, /device:TPU:1, one launch (start us, length us, event | category | flops | bytes accessed | tf_op | source)
XLA Modules:
  0.0 137.4 jit_solution(8332021771988431017)
XLA Ops:
  0.6 1.7 %shard_map.149 = f32[256,256]{1,0:T(8,128)} custom-call(f32[32,2048]{1,0:T(8,128)} %tod_ref.1), custom_call_target="tpu_custom_call" | custom-call | tf_op jit(solution)/shard_map/pallas_call | solution.py:475
  2.3 0.0 copy-start.7
  2.3 0.0 copy-start.8
  2.4 0.0 copy-start.11
  2.4 10.1 %all-to-all-start = ((f32[16,16,256]{2,1,0:T(8,128)}), f32[16,16,256]{2,1,0:T(8,128)S(1)}, u32[]{:S(2)}, u32[]{:S(2)}) async-start(f32[16,16,256]{2,1,0:T(8,128)} %bitcast.17), calls=%async_computation | async-start | bytes 524288 | tf_op jit(solution)/shard_map/all_to_all | solution.py:488
  12.5 0.0 copy-start.4
  12.5 1.5 %shard_map.150 = (f32[1,64,128]{2,1,0:T(8,128)}, f32[24,256]{1,0:T(8,128)}) custom-call(f32[8,32,128]{2,1,0:T(8,128)} %modes_hbm.1, f32[8,32]{1,0:T(8,128)} %noise_hbm.1), custom_call_target="tpu_custom_call" | custom-call | tf_op jit(solution)/shard_map/pallas_call | solution.py:475
  14.0 0.0 copy-start.3
  14.0 1.4 %collective-permute-start = (f32[1,64,128]{2,1,0:T(8,128)}, f32[1,64,128]{2,1,0:T(8,128)S(1)}, u32[]{:S(2)}, u32[]{:S(2)}) collective-permute-start(f32[1,64,128]{2,1,0:T(8,128)} %get-tuple-element.13), channel_id=1, source_target_pairs={{0,16},{16,0},{32,48},{48,32},{64,80},{80,64},{96,112},{112,96},{1... | collective-permute-start | bytes 98312 | tf_op jit(solution)/shard_map/ppermute | solution.py:520
  15.4 2.0 %collective-permute-done = f32[1,64,128]{2,1,0:T(8,128)S(1)} collective-permute-done((f32[1,64,128]{2,1,0:T(8,128)}, f32[1,64,128]{2,1,0:T(8,128)S(1)}, u32[]{:S(2)}, u32[]{:S(2)}) %collective-permute-start) | collective-permute-done | bytes 32800 | tf_op jit(solution)/shard_map/ppermute | solution.py:520
  17.4 0.8 pad_maximum_fusion.1
  18.2 2.9 %collective-permute-start.1 = (f32[2,64,128]{2,1,0:T(8,128)S(1)}, f32[2,64,128]{2,1,0:T(8,128)S(1)}, u32[]{:S(2)}, u32[]{:S(2)}) collective-permute-start(f32[2,64,128]{2,1,0:T(8,128)S(1)} %pad_maximum_fusion.1), channel_id=1, source_target_pairs={{0,32},{16,48},{32,0},{48,16},{64,96},{80,112},{96,64},{112,80},{1... | collective-permute-start | bytes 196616 | tf_op jit(solution)/shard_map/ppermute | solution.py:520
  21.1 0.8 constant_dynamic-update-slice_fusion.3
  21.8 0.0 copy-start.9
  21.8 1.2 collective-permute-done.1
  23.1 0.8 pad_maximum_fusion
  23.9 1.3 collective-permute-start.2
  25.1 0.0 all-to-all-done.x_ref
  25.2 0.0 copy-done.7
  25.2 0.0 copy-done.8
  25.2 0.0 copy-done.11
  25.2 0.0 copy-done.4
  25.2 0.0 copy-done.3
  25.2 0.0 copy-done.9
  25.2 2.0 %shard_map.151 = f32[512,128]{1,0:T(8,128)} custom-call(f32[16,16,256]{2,1,0:T(8,128)S(1)} %all-to-all-done.x_ref, f32[24,256]{1,0:T(8,128)S(1)} %copy-done.9, f32[128,128]{1,0:T(8,128)S(1)} %copy-done.11, f32[256,128]{1,0:T(8,128)S(1)} %copy-done.7, f32[256,128]{1,0:T(8,128)S(1)} %copy-done.8, f32[128,512]{1,0:T(8,128)S(1)} %copy-done.3, ...), custom_call_target="tpu_custom_call" | custom-call | tf_op jit(solution)/shard_map/pallas_call | solution.py:475
  27.2 14.6 %all-to-all-start.1 = ((f32[256,2,128]{2,1,0:T(2,128)}), f32[256,2,128]{2,1,0:T(2,128)S(1)}, u32[]{:S(2)}, u32[]{:S(2)}) async-start(f32[256,2,128]{2,1,0:T(2,128)} %bitcast.1), calls=%async_computation.1 | async-start | bytes 524288 | tf_op jit(solution)/shard_map/all_to_all | solution.py:488
  41.8 0.0 collective-permute-done.2
  41.9 2.9 %collective-permute-start.3 = (f32[8,64,128]{2,1,0:T(8,128)S(1)}, f32[8,64,128]{2,1,0:T(8,128)S(1)}, u32[]{:S(2)}, u32[]{:S(2)}) collective-permute-start(f32[8,64,128]{2,1,0:T(8,128)S(1)} %constant_dynamic-update-slice_fusion.near_ref), channel_id=1, source_target_pairs={{0,128},{16,144},{32,160},{48,176},{64,192},{80,208},{96,224},{112... | collective-permute-start | bytes 786440 | tf_op jit(solution)/shard_map/ppermute | solution.py:520
  44.8 7.3 %collective-permute-done.3.far_ref = f32[8,64,128]{2,1,0:T(8,128)S(1)} collective-permute-done((f32[8,64,128]{2,1,0:T(8,128)S(1)}, f32[8,64,128]{2,1,0:T(8,128)S(1)}, u32[]{:S(2)}, u32[]{:S(2)}) %collective-permute-start.3) | collective-permute-done | bytes 262176 | tf_op jit(solution)/shard_map/ppermute | solution.py:520
  52.1 10.3 %shard_map.152 = (f32[2,256,256]{2,1,0:T(8,128)S(1)}, f32[2,256,256]{2,1,0:T(8,128)S(1)}) custom-call(f32[8,64,128]{2,1,0:T(8,128)S(1)} %constant_dynamic-update-slice_fusion.near_ref, f32[8,64,128]{2,1,0:T(8,128)S(1)} %collective-permute-done.3.far_ref), custom_call_target="tpu_custom_call" | custom-call | tf_op jit(solution)/shard_map/pallas_call | solution.py:475
  62.4 0.0 all-to-all-done.1
  62.4 0.0 copy-start.5
  62.4 0.0 copy-start.6
  62.4 0.0 copy-start.10
  62.4 1.9 %shard_map.153 = f32[512,128]{1,0:T(8,128)S(1)} custom-call(f32[512,128]{1,0:T(8,128)S(1)} %bitcast.13, f32[2,256,256]{2,1,0:T(8,128)S(1)} %get-tuple-element.14.trans_ref, f32[2,256,256]{2,1,0:T(8,128)S(1)} %get-tuple-element.15.gain_ref), custom_call_target="tpu_custom_call" | custom-call | tf_op jit(solution)/shard_map/pallas_call | solution.py:475
  64.3 0.0 copy-start.1
  64.3 0.0 copy-start.2
  64.3 29.5 %all_to_all.31 = f32[256,2,128]{2,1,0:T(2,128)S(1)} all-to-all(f32[256,2,128]{2,1,0:T(2,128)S(1)} %bitcast.15), channel_id=1, replica_groups=mesh['det'=16,'tm'=16] {'det','tm'}, dimensions={0} | all-to-all | bytes 524288 | tf_op jit(solution)/shard_map/all_to_all | solution.py:488
  93.9 0.0 copy-done.5
  93.9 0.0 copy-done.6
  93.9 0.0 copy-done.10
  93.9 0.0 copy-done.1
  93.9 0.0 copy-done.2
  93.9 1.5 %shard_map.154 = f32[16,16,256]{2,1,0:T(8,128)} custom-call(f32[512,128]{1,0:T(8,128)S(1)} %bitcast.14, f32[24,256]{1,0:T(8,128)S(1)} %copy-done.9, f32[256,128]{1,0:T(8,128)S(1)} %copy-done.5, f32[256,128]{1,0:T(8,128)S(1)} %copy-done.6, bf16[2,256,256]{2,1,0:T(8,128)(2,1)S(1)} %copy-done.1, bf16[2,256,256]{2,1,0:T(8,128)(2,1)S(1)} %copy-done.2, ...), custom_call_target="tpu_custom_call" | custom-call | tf_op jit(solution)/shard_map/pallas_call | solution.py:475
  95.4 0.0 copy-start
  95.4 3.9 %all-to-all-start.3 = ((f32[16,16,256]{2,1,0:T(8,128)}), f32[16,16,256]{2,1,0:T(8,128)S(1)}, u32[]{:S(2)}, u32[]{:S(2)}) async-start(f32[16,16,256]{2,1,0:T(8,128)} %shard_map.154), calls=%async_computation.3 | async-start | bytes 524288 | tf_op jit(solution)/shard_map/all_to_all | solution.py:488
  99.3 0.0 copy-done
  99.3 3.4 %shard_map.156 = (f32[256,128]{1,0:T(8,128)S(1)}, f32[128,256]{1,0:T(8,128)S(1)}, f32[128,256]{1,0:T(8,128)S(1)}) custom-call(s32[32,2048]{1,0:T(8,128)S(1)} %copy-done), custom_call_target="tpu_custom_call" | custom-call | tf_op jit(solution)/shard_map/pallas_call | solution.py:475
  102.7 3.4 %shard_map.157 = (f32[256,128]{1,0:T(8,128)S(1)}, f32[128,256]{1,0:T(8,128)S(1)}, f32[128,256]{1,0:T(8,128)S(1)}) custom-call(s32[32,2048]{1,0:T(8,128)S(1)} %copy-done), custom_call_target="tpu_custom_call" | custom-call | tf_op jit(solution)/shard_map/pallas_call | solution.py:475
  106.0 5.0 %all-to-all-done.3 = f32[16,16,256]{2,1,0:T(8,128)S(1)} async-done(((f32[16,16,256]{2,1,0:T(8,128)}), f32[16,16,256]{2,1,0:T(8,128)S(1)}, u32[]{:S(2)}, u32[]{:S(2)}) %all-to-all-start.3) | async-done | bytes 262176 | tf_op jit(solution)/shard_map/all_to_all | solution.py:488
  111.1 7.9 %shard_map.158 = f32[256,128]{1,0:T(8,128)} custom-call(f32[256,256]{1,0:T(8,128)S(1)} %bitcast.11, f32[256,128]{1,0:T(8,128)S(1)} %get-tuple-element.16.refs_0_, f32[128,256]{1,0:T(8,128)S(1)} %get-tuple-element.17.refs_1_, f32[128,256]{1,0:T(8,128)S(1)} %get-tuple-element.18.refs_2_, f32[256,128]{1,0:T(8,128)S(1)} %get-tuple-element.19.refs_3_, ...), custom_call_target="tpu_custom_call" | custom-call | tf_op jit(solution)/shard_map/pallas_call | solution.py:475
  119.0 5.2 %all-to-all-start.4 = ((f32[256,1,128]{2,1,0:T(1,128)}), f32[256,1,128]{2,1,0:T(1,128)S(1)}, u32[]{:S(2)}, u32[]{:S(2)}) async-start(f32[256,1,128]{2,1,0:T(1,128)} %bitcast.7), calls=%async_computation.4 | async-start | bytes 262144 | tf_op jit(solution)/shard_map/all_to_all | solution.py:488
  124.2 0.8 shard_map.155
  125.0 11.8 %all-to-all-done.4 = f32[256,1,128]{2,1,0:T(1,128)S(1)} async-done(((f32[256,1,128]{2,1,0:T(1,128)}), f32[256,1,128]{2,1,0:T(1,128)S(1)}, u32[]{:S(2)}, u32[]{:S(2)}) %all-to-all-start.4) | async-done | bytes 131104 | tf_op jit(solution)/shard_map/all_to_all | solution.py:488
  136.7 0.6 shard_map.159
  (3 shorter events, 0.0 us)
Async XLA Ops:
  2.3 22.8 %copy-start.7 = (f32[256,128]{1,0:T(8,128)S(1)}, f32[256,128]{1,0:T(8,128)}, u32[]{:S(2)}) copy-start(f32[256,128]{1,0:T(8,128)} %constant.21.clone.keep_ref) | copy-start | bytes 393220
  2.3 22.8 %copy-start.8 = (f32[256,128]{1,0:T(8,128)S(1)}, f32[256,128]{1,0:T(8,128)}, u32[]{:S(2)}) copy-start(f32[256,128]{1,0:T(8,128)} %constant.22.clone.swap_ref) | copy-start | bytes 393220
  2.4 22.8 %copy-start.11 = (f32[128,128]{1,0:T(8,128)S(1)}, f32[128,128]{1,0:T(8,128)}, u32[]{:S(2)}) copy-start(f32[128,128]{1,0:T(8,128)} %constant.20.clone.first_ref) | copy-start | bytes 196612
  2.4 22.8 %all-to-all-start = ((f32[16,16,256]{2,1,0:T(8,128)}), f32[16,16,256]{2,1,0:T(8,128)S(1)}, u32[]{:S(2)}, u32[]{:S(2)}) async-start(f32[16,16,256]{2,1,0:T(8,128)} %bitcast.17), calls=%async_computation | async-start | bytes 524288 | tf_op jit(solution)/shard_map/all_to_all | solution.py:488
  12.5 12.7 %copy-start.4 = (f32[128,512]{1,0:T(8,128)S(1)}, f32[128,512]{1,0:T(8,128)}, u32[]{:S(2)}) copy-start(f32[128,512]{1,0:T(8,128)} %constant.24.clone.bottom_ref) | copy-start | bytes 786436
  14.0 11.2 %copy-start.3 = (f32[128,512]{1,0:T(8,128)S(1)}, f32[128,512]{1,0:T(8,128)}, u32[]{:S(2)}) copy-start(f32[128,512]{1,0:T(8,128)} %constant.23.clone.top_ref) | copy-start | bytes 786436
  14.0 3.4 %collective-permute-start = (f32[1,64,128]{2,1,0:T(8,128)}, f32[1,64,128]{2,1,0:T(8,128)S(1)}, u32[]{:S(2)}, u32[]{:S(2)}) collective-permute-start(f32[1,64,128]{2,1,0:T(8,128)} %get-tuple-element.13), channel_id=1, source_target_pairs={{0,16},{16,0},{32,48},{48,32},{64,80},{80,64},{96,112},{112,96},{1... | collective-permute-start | bytes 98312 | tf_op jit(solution)/shard_map/ppermute | solution.py:520
  18.2 4.9 %collective-permute-start.1 = (f32[2,64,128]{2,1,0:T(8,128)S(1)}, f32[2,64,128]{2,1,0:T(8,128)S(1)}, u32[]{:S(2)}, u32[]{:S(2)}) collective-permute-start(f32[2,64,128]{2,1,0:T(8,128)S(1)} %pad_maximum_fusion.1), channel_id=1, source_target_pairs={{0,32},{16,48},{32,0},{48,16},{64,96},{80,112},{96,64},{112,80},{1... | collective-permute-start | bytes 196616 | tf_op jit(solution)/shard_map/ppermute | solution.py:520
  21.8 3.4 %copy-start.9 = (f32[24,256]{1,0:T(8,128)S(1)}, f32[24,256]{1,0:T(8,128)}, u32[]{:S(2)}) copy-start(f32[24,256]{1,0:T(8,128)} %get-tuple-element.12.scale_ref) | copy-start | bytes 73732
  23.9 18.0 %collective-permute-start.2 = (f32[4,64,128]{2,1,0:T(8,128)S(1)}, f32[4,64,128]{2,1,0:T(8,128)S(1)}, u32[]{:S(2)}, u32[]{:S(2)}) collective-permute-start(f32[4,64,128]{2,1,0:T(8,128)S(1)} %pad_maximum_fusion), channel_id=1, source_target_pairs={{0,64},{16,80},{32,96},{48,112},{64,0},{80,16},{96,32},{112,48},{1... | collective-permute-start | bytes 393224 | tf_op jit(solution)/shard_map/ppermute | solution.py:520
  27.2 35.2 %all-to-all-start.1 = ((f32[256,2,128]{2,1,0:T(2,128)}), f32[256,2,128]{2,1,0:T(2,128)S(1)}, u32[]{:S(2)}, u32[]{:S(2)}) async-start(f32[256,2,128]{2,1,0:T(2,128)} %bitcast.1), calls=%async_computation.1 | async-start | bytes 524288 | tf_op jit(solution)/shard_map/all_to_all | solution.py:488
  41.9 10.2 %collective-permute-start.3 = (f32[8,64,128]{2,1,0:T(8,128)S(1)}, f32[8,64,128]{2,1,0:T(8,128)S(1)}, u32[]{:S(2)}, u32[]{:S(2)}) collective-permute-start(f32[8,64,128]{2,1,0:T(8,128)S(1)} %constant_dynamic-update-slice_fusion.near_ref), channel_id=1, source_target_pairs={{0,128},{16,144},{32,160},{48,176},{64,192},{80,208},{96,224},{112... | collective-permute-start | bytes 786440 | tf_op jit(solution)/shard_map/ppermute | solution.py:520
  62.4 31.5 %copy-start.5 = (f32[256,128]{1,0:T(8,128)S(1)}, f32[256,128]{1,0:T(8,128)}, u32[]{:S(2)}) copy-start(f32[256,128]{1,0:T(8,128)} %constant.25.clone.keep_ref) | copy-start | bytes 393220
  62.4 31.5 %copy-start.6 = (f32[256,128]{1,0:T(8,128)S(1)}, f32[256,128]{1,0:T(8,128)}, u32[]{:S(2)}) copy-start(f32[256,128]{1,0:T(8,128)} %constant.26.clone.swap_ref) | copy-start | bytes 393220
  62.4 31.5 %copy-start.10 = (bf16[2,128,128]{2,1,0:T(8,128)(2,1)S(1)}, bf16[2,128,128]{2,1,0:T(8,128)(2,1)}, u32[]{:S(2)}) copy-start(bf16[2,128,128]{2,1,0:T(8,128)(2,1)} %constant.29.clone.last_ref) | copy-start | bytes 196612
  64.3 29.6 %copy-start.1 = (bf16[2,256,256]{2,1,0:T(8,128)(2,1)S(1)}, bf16[2,256,256]{2,1,0:T(8,128)(2,1)}, u32[]{:S(2)}) copy-start(bf16[2,256,256]{2,1,0:T(8,128)(2,1)} %constant.27.clone.top_ref) | copy-start | bytes 786436
  64.3 29.6 %copy-start.2 = (bf16[2,256,256]{2,1,0:T(8,128)(2,1)S(1)}, bf16[2,256,256]{2,1,0:T(8,128)(2,1)}, u32[]{:S(2)}) copy-start(bf16[2,256,256]{2,1,0:T(8,128)(2,1)} %constant.28.clone.bottom_ref) | copy-start | bytes 786436
  95.4 3.9 %copy-start = (s32[32,2048]{1,0:T(8,128)S(1)}, s32[32,2048]{1,0:T(8,128)}, u32[]{:S(2)}) copy-start(s32[32,2048]{1,0:T(8,128)} %point_ref.3) | copy-start | bytes 786436
  95.4 15.7 %all-to-all-start.3 = ((f32[16,16,256]{2,1,0:T(8,128)}), f32[16,16,256]{2,1,0:T(8,128)S(1)}, u32[]{:S(2)}, u32[]{:S(2)}) async-start(f32[16,16,256]{2,1,0:T(8,128)} %shard_map.154), calls=%async_computation.3 | async-start | bytes 524288 | tf_op jit(solution)/shard_map/all_to_all | solution.py:488
  119.0 17.7 %all-to-all-start.4 = ((f32[256,1,128]{2,1,0:T(1,128)}), f32[256,1,128]{2,1,0:T(1,128)S(1)}, u32[]{:S(2)}, u32[]{:S(2)}) async-start(f32[256,1,128]{2,1,0:T(1,128)} %bitcast.7), calls=%async_computation.4 | async-start | bytes 262144 | tf_op jit(solution)/shard_map/all_to_all | solution.py:488

commit v9 on v8

--- a/solution.py
+++ b/solution.py
@@ -15,6 +15,7 @@
 N2 = 256
 BANDS = 8
 TPIX = 48
+HOPS = (2, 8, 1, 4)
 GRANT = 12 << 20
 WIDE_GRANT = 60 << 20
 F32 = jnp.float32
@@ -287,7 +288,8 @@
     dev, _ = _position()
     for j in range(16):
         source = near_ref if j < 8 else far_ref
-        rows = pl.ds(pl.multiple_of((dev ^ j) * 16, 16), 16)
+        flip = sum(hop for bit, hop in enumerate(HOPS) if j >> bit & 1)
+        rows = pl.ds(pl.multiple_of((dev ^ flip) * 16, 16), 16)
         for e in range(2):
             for part in range(2):
                 low = 32 * part + 16 * e
@@ -437,7 +439,7 @@
     acc = jnp.zeros((192, 128), F32)
     for base, (_, high_ref, low_ref) in ((0, first_refs), (128, second_refs)):
         turn = functools.partial(step, base, high_ref, low_ref)
-        acc = lax.fori_loop(0, 128, turn, acc, unroll=64)
+        acc = lax.fori_loop(0, 128, turn, acc, unroll=128)
     grid_ref[...] = acc[:96] + acc[96:]
 
     def put(rows, value):
@@ -516,7 +518,7 @@
     )(tod).reshape(16, 16, 256)
     near = send_v
     for bit in range(4):
-        pairs = [(i, i ^ (1 << bit)) for i in range(16)]
+        pairs = [(i, i ^ HOPS[bit]) for i in range(16)]
         far = lax.ppermute(near, "det", pairs)
         if bit < 3:
             near = jnp.concatenate([near, far], axis=0)

time: 138 us -> 138 us (level)
  transfers between devices with their start and end apart: 8 -> 8, of which waited for: 5 -> 5; matrix products, arithmetic and copies ran while one was open for 2% -> 2% of each run, Pallas kernels for 16% -> 15%
where the time goes in v9:
time: 138 us
  starting transfers between devices  42.7 us (31%)
  Pallas kernels  34.4 us (25%)
  blocking collectives  30.2 us (22%)
  waiting for transfers between devices  27.2 us (20%)
  other arithmetic  1.53 us (1%)
    pallas_call x11, Pallas kernels, run(): pl.pallas_call(kernel, out_shape=shapes if many else shapes[0], in_specs=...  34.4 us
    all_to_all x4, starting transfers between devices, exchange(): return lax.all_to_all(value, axes, split_axis=0, concat_axis=0, tiled=True)  34.1 us
    all_to_all x1, blocking collectives, exchange(): return lax.all_to_all(value, axes, split_axis=0, concat_axis=0, tiled=True)  30.2 us
    all_to_all x4, waiting for transfers between devices, exchange(): return lax.all_to_all(value, axes, split_axis=0, concat_axis=0, tiled=True)  16.8 us
    ppermute x4, waiting for transfers between devices, steps(): far = lax.ppermute(near, 'det', pairs)  10.4 us
    ppermute x4, starting transfers between devices, steps(): far = lax.ppermute(near, 'det', pairs)  8.57 us
  transfers between devices with their start and end apart: 8, of which 5 were waited for; matrix products, arithmetic and copies ran while one was open for 2% of the time, Pallas kernels for 15%

profile of v9, /device:TPU:1, one launch (start us, length us, event | category | flops | bytes accessed | tf_op | source)
XLA Modules:
  0.0 137.7 jit_solution(13016683942605055391)
XLA Ops:
  0.6 1.7 %shard_map.149 = f32[256,256]{1,0:T(8,128)} custom-call(f32[32,2048]{1,0:T(8,128)} %tod_ref.1), custom_call_target="tpu_custom_call" | custom-call | tf_op jit(solution)/shard_map/pallas_call | solution.py:477
  2.3 0.0 copy-start.7
  2.3 0.0 copy-start.8
  2.4 0.0 copy-start.11
  2.4 10.1 %all-to-all-start = ((f32[16,16,256]{2,1,0:T(8,128)}), f32[16,16,256]{2,1,0:T(8,128)S(1)}, u32[]{:S(2)}, u32[]{:S(2)}) async-start(f32[16,16,256]{2,1,0:T(8,128)} %bitcast.17), calls=%async_computation | async-start | bytes 524288 | tf_op jit(solution)/shard_map/all_to_all | solution.py:490
  12.5 0.0 copy-start.4
  12.5 1.5 %shard_map.150 = (f32[1,64,128]{2,1,0:T(8,128)}, f32[24,256]{1,0:T(8,128)}) custom-call(f32[8,32,128]{2,1,0:T(8,128)} %modes_hbm.1, f32[8,32]{1,0:T(8,128)} %noise_hbm.1), custom_call_target="tpu_custom_call" | custom-call | tf_op jit(solution)/shard_map/pallas_call | solution.py:477
  14.0 0.0 copy-start.3
  14.0 3.0 %collective-permute-start = (f32[1,64,128]{2,1,0:T(8,128)}, f32[1,64,128]{2,1,0:T(8,128)S(1)}, u32[]{:S(2)}, u32[]{:S(2)}) collective-permute-start(f32[1,64,128]{2,1,0:T(8,128)} %get-tuple-element.13), channel_id=1, source_target_pairs={{0,32},{16,48},{32,0},{48,16},{64,96},{80,112},{96,64},{112,80},{1... | collective-permute-start | bytes 98312 | tf_op jit(solution)/shard_map/ppermute | solution.py:522
  17.0 1.9 %collective-permute-done = f32[1,64,128]{2,1,0:T(8,128)S(1)} collective-permute-done((f32[1,64,128]{2,1,0:T(8,128)}, f32[1,64,128]{2,1,0:T(8,128)S(1)}, u32[]{:S(2)}, u32[]{:S(2)}) %collective-permute-start) | collective-permute-done | bytes 32800 | tf_op jit(solution)/shard_map/ppermute | solution.py:522
  18.9 0.8 pad_maximum_fusion.1
  19.7 2.7 %collective-permute-start.1 = (f32[2,64,128]{2,1,0:T(8,128)S(1)}, f32[2,64,128]{2,1,0:T(8,128)S(1)}, u32[]{:S(2)}, u32[]{:S(2)}) collective-permute-start(f32[2,64,128]{2,1,0:T(8,128)S(1)} %pad_maximum_fusion.1), channel_id=1, source_target_pairs={{0,128},{16,144},{32,160},{48,176},{64,192},{80,208},{96,224},{112... | collective-permute-start | bytes 196616 | tf_op jit(solution)/shard_map/ppermute | solution.py:522
  22.4 0.8 constant_dynamic-update-slice_fusion.3
  23.2 0.0 copy-start.9
  23.2 1.1 collective-permute-done.1
  24.3 0.8 pad_maximum_fusion
  25.1 1.4 %collective-permute-start.2 = (f32[4,64,128]{2,1,0:T(8,128)S(1)}, f32[4,64,128]{2,1,0:T(8,128)S(1)}, u32[]{:S(2)}, u32[]{:S(2)}) collective-permute-start(f32[4,64,128]{2,1,0:T(8,128)S(1)} %pad_maximum_fusion), channel_id=1, source_target_pairs={{0,16},{16,0},{32,48},{48,32},{64,80},{80,64},{96,112},{112,96},{1... | collective-permute-start | bytes 393224 | tf_op jit(solution)/shard_map/ppermute | solution.py:522
  26.4 0.0 all-to-all-done.x_ref
  26.4 0.0 copy-done.7
  26.4 0.0 copy-done.8
  26.5 0.0 copy-done.11
  26.5 0.0 copy-done.4
  26.5 0.0 copy-done.3
  26.5 0.0 copy-done.9
  26.5 2.0 %shard_map.151 = f32[512,128]{1,0:T(8,128)} custom-call(f32[16,16,256]{2,1,0:T(8,128)S(1)} %all-to-all-done.x_ref, f32[24,256]{1,0:T(8,128)S(1)} %copy-done.9, f32[128,128]{1,0:T(8,128)S(1)} %copy-done.11, f32[256,128]{1,0:T(8,128)S(1)} %copy-done.7, f32[256,128]{1,0:T(8,128)S(1)} %copy-done.8, f32[128,512]{1,0:T(8,128)S(1)} %copy-done.3, ...), custom_call_target="tpu_custom_call" | custom-call | tf_op jit(solution)/shard_map/pallas_call | solution.py:477
  28.5 14.9 %all-to-all-start.1 = ((f32[256,2,128]{2,1,0:T(2,128)}), f32[256,2,128]{2,1,0:T(2,128)S(1)}, u32[]{:S(2)}, u32[]{:S(2)}) async-start(f32[256,2,128]{2,1,0:T(2,128)} %bitcast.1), calls=%async_computation.1 | async-start | bytes 524288 | tf_op jit(solution)/shard_map/all_to_all | solution.py:490
  43.4 0.0 collective-permute-done.2
  43.5 1.4 %collective-permute-start.3 = (f32[8,64,128]{2,1,0:T(8,128)S(1)}, f32[8,64,128]{2,1,0:T(8,128)S(1)}, u32[]{:S(2)}, u32[]{:S(2)}) collective-permute-start(f32[8,64,128]{2,1,0:T(8,128)S(1)} %constant_dynamic-update-slice_fusion.near_ref), channel_id=1, source_target_pairs={{0,64},{16,80},{32,96},{48,112},{64,0},{80,16},{96,32},{112,48},{1... | collective-permute-start | bytes 786440 | tf_op jit(solution)/shard_map/ppermute | solution.py:522
  44.9 7.4 %collective-permute-done.3.far_ref = f32[8,64,128]{2,1,0:T(8,128)S(1)} collective-permute-done((f32[8,64,128]{2,1,0:T(8,128)S(1)}, f32[8,64,128]{2,1,0:T(8,128)S(1)}, u32[]{:S(2)}, u32[]{:S(2)}) %collective-permute-start.3) | collective-permute-done | bytes 262176 | tf_op jit(solution)/shard_map/ppermute | solution.py:522
  52.3 10.3 %shard_map.152 = (f32[2,256,256]{2,1,0:T(8,128)S(1)}, f32[2,256,256]{2,1,0:T(8,128)S(1)}) custom-call(f32[8,64,128]{2,1,0:T(8,128)S(1)} %constant_dynamic-update-slice_fusion.near_ref, f32[8,64,128]{2,1,0:T(8,128)S(1)} %collective-permute-done.3.far_ref), custom_call_target="tpu_custom_call" | custom-call | tf_op jit(solution)/shard_map/pallas_call | solution.py:477
  62.6 0.0 all-to-all-done.1
  62.6 0.0 copy-start.5
  62.6 0.0 copy-start.6
  62.6 0.0 copy-start.10
  62.7 1.9 %shard_map.153 = f32[512,128]{1,0:T(8,128)S(1)} custom-call(f32[512,128]{1,0:T(8,128)S(1)} %bitcast.13, f32[2,256,256]{2,1,0:T(8,128)S(1)} %get-tuple-element.14.trans_ref, f32[2,256,256]{2,1,0:T(8,128)S(1)} %get-tuple-element.15.gain_ref), custom_call_target="tpu_custom_call" | custom-call | tf_op jit(solution)/shard_map/pallas_call | solution.py:477
  64.5 0.0 copy-start.1
  64.6 0.0 copy-start.2
  64.6 30.2 %all_to_all.31 = f32[256,2,128]{2,1,0:T(2,128)S(1)} all-to-all(f32[256,2,128]{2,1,0:T(2,128)S(1)} %bitcast.15), channel_id=1, replica_groups=mesh['det'=16,'tm'=16] {'det','tm'}, dimensions={0} | all-to-all | bytes 524288 | tf_op jit(solution)/shard_map/all_to_all | solution.py:490
  94.8 0.0 copy-done.5
  94.8 0.0 copy-done.6
  94.8 0.0 copy-done.10
  94.8 0.0 copy-done.1
  94.8 0.0 copy-done.2
  94.8 1.5 %shard_map.154 = f32[16,16,256]{2,1,0:T(8,128)} custom-call(f32[512,128]{1,0:T(8,128)S(1)} %bitcast.14, f32[24,256]{1,0:T(8,128)S(1)} %copy-done.9, f32[256,128]{1,0:T(8,128)S(1)} %copy-done.5, f32[256,128]{1,0:T(8,128)S(1)} %copy-done.6, bf16[2,256,256]{2,1,0:T(8,128)(2,1)S(1)} %copy-done.1, bf16[2,256,256]{2,1,0:T(8,128)(2,1)S(1)} %copy-done.2, ...), custom_call_target="tpu_custom_call" | custom-call | tf_op jit(solution)/shard_map/pallas_call | solution.py:477
  96.3 0.0 copy-start
  96.3 3.9 %all-to-all-start.3 = ((f32[16,16,256]{2,1,0:T(8,128)}), f32[16,16,256]{2,1,0:T(8,128)S(1)}, u32[]{:S(2)}, u32[]{:S(2)}) async-start(f32[16,16,256]{2,1,0:T(8,128)} %shard_map.154), calls=%async_computation.3 | async-start | bytes 524288 | tf_op jit(solution)/shard_map/all_to_all | solution.py:490
  100.2 0.0 copy-done
  100.2 3.4 %shard_map.156 = (f32[256,128]{1,0:T(8,128)S(1)}, f32[128,256]{1,0:T(8,128)S(1)}, f32[128,256]{1,0:T(8,128)S(1)}) custom-call(s32[32,2048]{1,0:T(8,128)S(1)} %copy-done), custom_call_target="tpu_custom_call" | custom-call | tf_op jit(solution)/shard_map/pallas_call | solution.py:477
  103.6 3.4 %shard_map.157 = (f32[256,128]{1,0:T(8,128)S(1)}, f32[128,256]{1,0:T(8,128)S(1)}, f32[128,256]{1,0:T(8,128)S(1)}) custom-call(s32[32,2048]{1,0:T(8,128)S(1)} %copy-done), custom_call_target="tpu_custom_call" | custom-call | tf_op jit(solution)/shard_map/pallas_call | solution.py:477
  106.9 5.0 %all-to-all-done.3 = f32[16,16,256]{2,1,0:T(8,128)S(1)} async-done(((f32[16,16,256]{2,1,0:T(8,128)}), f32[16,16,256]{2,1,0:T(8,128)S(1)}, u32[]{:S(2)}, u32[]{:S(2)}) %all-to-all-start.3) | async-done | bytes 262176 | tf_op jit(solution)/shard_map/all_to_all | solution.py:490
  112.0 7.4 %shard_map.158 = f32[256,128]{1,0:T(8,128)} custom-call(f32[256,256]{1,0:T(8,128)S(1)} %bitcast.11, f32[256,128]{1,0:T(8,128)S(1)} %get-tuple-element.16.refs_0_, f32[128,256]{1,0:T(8,128)S(1)} %get-tuple-element.17.refs_1_, f32[128,256]{1,0:T(8,128)S(1)} %get-tuple-element.18.refs_2_, f32[256,128]{1,0:T(8,128)S(1)} %get-tuple-element.19.refs_3_, ...), custom_call_target="tpu_custom_call" | custom-call | tf_op jit(solution)/shard_map/pallas_call | solution.py:477
  119.4 5.2 %all-to-all-start.4 = ((f32[256,1,128]{2,1,0:T(1,128)}), f32[256,1,128]{2,1,0:T(1,128)S(1)}, u32[]{:S(2)}, u32[]{:S(2)}) async-start(f32[256,1,128]{2,1,0:T(1,128)} %bitcast.7), calls=%async_computation.4 | async-start | bytes 262144 | tf_op jit(solution)/shard_map/all_to_all | solution.py:490
  124.6 0.8 shard_map.155
  125.3 11.8 %all-to-all-done.4 = f32[256,1,128]{2,1,0:T(1,128)S(1)} async-done(((f32[256,1,128]{2,1,0:T(1,128)}), f32[256,1,128]{2,1,0:T(1,128)S(1)}, u32[]{:S(2)}, u32[]{:S(2)}) %all-to-all-start.4) | async-done | bytes 131104 | tf_op jit(solution)/shard_map/all_to_all | solution.py:490
  137.1 0.6 shard_map.159
  (3 shorter events, 0.0 us)
Async XLA Ops:
  2.3 24.1 %copy-start.7 = (f32[256,128]{1,0:T(8,128)S(1)}, f32[256,128]{1,0:T(8,128)}, u32[]{:S(2)}) copy-start(f32[256,128]{1,0:T(8,128)} %constant.21.clone.keep_ref) | copy-start | bytes 393220
  2.3 24.1 %copy-start.8 = (f32[256,128]{1,0:T(8,128)S(1)}, f32[256,128]{1,0:T(8,128)}, u32[]{:S(2)}) copy-start(f32[256,128]{1,0:T(8,128)} %constant.22.clone.swap_ref) | copy-start | bytes 393220
  2.4 24.1 %copy-start.11 = (f32[128,128]{1,0:T(8,128)S(1)}, f32[128,128]{1,0:T(8,128)}, u32[]{:S(2)}) copy-start(f32[128,128]{1,0:T(8,128)} %constant.20.clone.first_ref) | copy-start | bytes 196612
  2.4 24.1 %all-to-all-start = ((f32[16,16,256]{2,1,0:T(8,128)}), f32[16,16,256]{2,1,0:T(8,128)S(1)}, u32[]{:S(2)}, u32[]{:S(2)}) async-start(f32[16,16,256]{2,1,0:T(8,128)} %bitcast.17), calls=%async_computation | async-start | bytes 524288 | tf_op jit(solution)/shard_map/all_to_all | solution.py:490
  12.5 14.0 %copy-start.4 = (f32[128,512]{1,0:T(8,128)S(1)}, f32[128,512]{1,0:T(8,128)}, u32[]{:S(2)}) copy-start(f32[128,512]{1,0:T(8,128)} %constant.24.clone.bottom_ref) | copy-start | bytes 786436
  14.0 12.4 %copy-start.3 = (f32[128,512]{1,0:T(8,128)S(1)}, f32[128,512]{1,0:T(8,128)}, u32[]{:S(2)}) copy-start(f32[128,512]{1,0:T(8,128)} %constant.23.clone.top_ref) | copy-start | bytes 786436
  14.0 4.9 %collective-permute-start = (f32[1,64,128]{2,1,0:T(8,128)}, f32[1,64,128]{2,1,0:T(8,128)S(1)}, u32[]{:S(2)}, u32[]{:S(2)}) collective-permute-start(f32[1,64,128]{2,1,0:T(8,128)} %get-tuple-element.13), channel_id=1, source_target_pairs={{0,32},{16,48},{32,0},{48,16},{64,96},{80,112},{96,64},{112,80},{1... | collective-permute-start | bytes 98312 | tf_op jit(solution)/shard_map/ppermute | solution.py:522
  19.7 4.6 %collective-permute-start.1 = (f32[2,64,128]{2,1,0:T(8,128)S(1)}, f32[2,64,128]{2,1,0:T(8,128)S(1)}, u32[]{:S(2)}, u32[]{:S(2)}) collective-permute-start(f32[2,64,128]{2,1,0:T(8,128)S(1)} %pad_maximum_fusion.1), channel_id=1, source_target_pairs={{0,128},{16,144},{32,160},{48,176},{64,192},{80,208},{96,224},{112... | collective-permute-start | bytes 196616 | tf_op jit(solution)/shard_map/ppermute | solution.py:522
  23.2 3.3 %copy-start.9 = (f32[24,256]{1,0:T(8,128)S(1)}, f32[24,256]{1,0:T(8,128)}, u32[]{:S(2)}) copy-start(f32[24,256]{1,0:T(8,128)} %get-tuple-element.12.scale_ref) | copy-start | bytes 73732
  25.1 18.4 %collective-permute-start.2 = (f32[4,64,128]{2,1,0:T(8,128)S(1)}, f32[4,64,128]{2,1,0:T(8,128)S(1)}, u32[]{:S(2)}, u32[]{:S(2)}) collective-permute-start(f32[4,64,128]{2,1,0:T(8,128)S(1)} %pad_maximum_fusion), channel_id=1, source_target_pairs={{0,16},{16,0},{32,48},{48,32},{64,80},{80,64},{96,112},{112,96},{1... | collective-permute-start | bytes 393224 | tf_op jit(solution)/shard_map/ppermute | solution.py:522
  28.5 34.1 %all-to-all-start.1 = ((f32[256,2,128]{2,1,0:T(2,128)}), f32[256,2,128]{2,1,0:T(2,128)S(1)}, u32[]{:S(2)}, u32[]{:S(2)}) async-start(f32[256,2,128]{2,1,0:T(2,128)} %bitcast.1), calls=%async_computation.1 | async-start | bytes 524288 | tf_op jit(solution)/shard_map/all_to_all | solution.py:490
  43.5 8.9 %collective-permute-start.3 = (f32[8,64,128]{2,1,0:T(8,128)S(1)}, f32[8,64,128]{2,1,0:T(8,128)S(1)}, u32[]{:S(2)}, u32[]{:S(2)}) collective-permute-start(f32[8,64,128]{2,1,0:T(8,128)S(1)} %constant_dynamic-update-slice_fusion.near_ref), channel_id=1, source_target_pairs={{0,64},{16,80},{32,96},{48,112},{64,0},{80,16},{96,32},{112,48},{1... | collective-permute-start | bytes 786440 | tf_op jit(solution)/shard_map/ppermute | solution.py:522
  62.6 32.2 %copy-start.5 = (f32[256,128]{1,0:T(8,128)S(1)}, f32[256,128]{1,0:T(8,128)}, u32[]{:S(2)}) copy-start(f32[256,128]{1,0:T(8,128)} %constant.25.clone.keep_ref) | copy-start | bytes 393220
  62.6 32.1 %copy-start.6 = (f32[256,128]{1,0:T(8,128)S(1)}, f32[256,128]{1,0:T(8,128)}, u32[]{:S(2)}) copy-start(f32[256,128]{1,0:T(8,128)} %constant.26.clone.swap_ref) | copy-start | bytes 393220
  62.6 32.1 %copy-start.10 = (bf16[2,128,128]{2,1,0:T(8,128)(2,1)S(1)}, bf16[2,128,128]{2,1,0:T(8,128)(2,1)}, u32[]{:S(2)}) copy-start(bf16[2,128,128]{2,1,0:T(8,128)(2,1)} %constant.29.clone.last_ref) | copy-start | bytes 196612
  64.5 30.2 %copy-start.1 = (bf16[2,256,256]{2,1,0:T(8,128)(2,1)S(1)}, bf16[2,256,256]{2,1,0:T(8,128)(2,1)}, u32[]{:S(2)}) copy-start(bf16[2,256,256]{2,1,0:T(8,128)(2,1)} %constant.27.clone.top_ref) | copy-start | bytes 786436
  64.6 30.2 %copy-start.2 = (bf16[2,256,256]{2,1,0:T(8,128)(2,1)S(1)}, bf16[2,256,256]{2,1,0:T(8,128)(2,1)}, u32[]{:S(2)}) copy-start(bf16[2,256,256]{2,1,0:T(8,128)(2,1)} %constant.28.clone.bottom_ref) | copy-start | bytes 786436
  96.3 3.9 %copy-start = (s32[32,2048]{1,0:T(8,128)S(1)}, s32[32,2048]{1,0:T(8,128)}, u32[]{:S(2)}) copy-start(s32[32,2048]{1,0:T(8,128)} %point_ref.3) | copy-start | bytes 786436
  96.3 15.7 %all-to-all-start.3 = ((f32[16,16,256]{2,1,0:T(8,128)}), f32[16,16,256]{2,1,0:T(8,128)S(1)}, u32[]{:S(2)}, u32[]{:S(2)}) async-start(f32[16,16,256]{2,1,0:T(8,128)} %shard_map.154), calls=%async_computation.3 | async-start | bytes 524288 | tf_op jit(solution)/shard_map/all_to_all | solution.py:490
  119.4 17.7 %all-to-all-start.4 = ((f32[256,1,128]{2,1,0:T(1,128)}), f32[256,1,128]{2,1,0:T(1,128)S(1)}, u32[]{:S(2)}, u32[]{:S(2)}) async-start(f32[256,1,128]{2,1,0:T(1,128)} %bitcast.7), calls=%async_computation.4 | async-start | bytes 262144 | tf_op jit(solution)/shard_map/all_to_all | solution.py:490

commit v10 on v9

--- a/solution.py
+++ b/solution.py
@@ -304,7 +304,7 @@
         )
     invert_in_place(mat_refs)
     for e in range(2):
-        trans_ref[e] = jnp.concatenate([parts[e][0], parts[e][1]], axis=1).T
+        trans_ref[:, 256 * e : 256 * e + 256] = vees_ref[e].T
         gain_ref[e] = jnp.concatenate(
             [_dot(parts[e][part], mat_refs[part][...]) for part in range(2)], axis=1
         )
@@ -312,7 +312,7 @@
 
 def apply_kernel(x_ref, trans_ref, gain_ref, out_ref):
     xs = [x_ref[pl.ds(e, 256, stride=2), :] for e in range(2)]
-    proj = _dot(trans_ref[0], xs[0]) + _dot(trans_ref[1], xs[1])
+    proj = _dot(trans_ref[...], jnp.concatenate(xs, axis=0))
     dev, pos = _position()
     special = (_lanes((256, 128)) == 64) & (dev * 16 + pos == 0)
     second = lax.broadcasted_iota(jnp.int32, (256, 128), 0) >= 128
@@ -526,7 +526,7 @@
     spectra = call(forward_kernel, ((512, 128), F32))(got_tod, scale, *forward)
     trans, gain = call(
         gram_kernel,
-        [((2, 256, 256), F32), ((2, 256, 256), F32)],
+        [((256, 512), F32), ((2, 256, 256), F32)],
         scratch=[
             pltpu.VMEM((2, 256, 256), F32),
             pltpu.VMEM((128, 128), F32),

time: 138 us -> 138 us (level)
  no operation moved by 1% of the time
where the time goes in v10:
time: 138 us
  starting transfers between devices  42.7 us (31%)
  Pallas kernels  34.4 us (25%)
  blocking collectives  30.2 us (22%)
  waiting for transfers between devices  27.2 us (20%)
  other arithmetic  1.53 us (1%)
    pallas_call x11, Pallas kernels, run(): pl.pallas_call(kernel, out_shape=shapes if many else shapes[0], in_specs=...  34.4 us
    all_to_all x4, starting transfers between devices, exchange(): return lax.all_to_all(value, axes, split_axis=0, concat_axis=0, tiled=True)  34.1 us
    all_to_all x1, blocking collectives, exchange(): return lax.all_to_all(value, axes, split_axis=0, concat_axis=0, tiled=True)  30.2 us
    all_to_all x4, waiting for transfers between devices, exchange(): return lax.all_to_all(value, axes, split_axis=0, concat_axis=0, tiled=True)  16.8 us
    ppermute x4, waiting for transfers between devices, steps(): far = lax.ppermute(near, 'det', pairs)  10.4 us
    ppermute x4, starting transfers between devices, steps(): far = lax.ppermute(near, 'det', pairs)  8.57 us
  transfers between devices with their start and end apart: 8, of which 5 were waited for; matrix products, arithmetic and copies ran while one was open for 2% of the time, Pallas kernels for 15%

profile of v10, /device:TPU:1, one launch (start us, length us, event | category | flops | bytes accessed | tf_op | source)
XLA Modules:
  0.0 137.7 jit_solution(7380683375590851177)
XLA Ops:
  0.6 1.7 %shard_map.149 = f32[256,256]{1,0:T(8,128)} custom-call(f32[32,2048]{1,0:T(8,128)} %tod_ref.1), custom_call_target="tpu_custom_call" | custom-call | tf_op jit(solution)/shard_map/pallas_call | solution.py:477
  2.3 0.0 copy-start.7
  2.3 0.0 copy-start.8
  2.4 0.0 copy-start.11
  2.4 10.1 %all-to-all-start = ((f32[16,16,256]{2,1,0:T(8,128)}), f32[16,16,256]{2,1,0:T(8,128)S(1)}, u32[]{:S(2)}, u32[]{:S(2)}) async-start(f32[16,16,256]{2,1,0:T(8,128)} %bitcast.17), calls=%async_computation | async-start | bytes 524288 | tf_op jit(solution)/shard_map/all_to_all | solution.py:490
  12.5 0.0 copy-start.4
  12.5 1.5 %shard_map.150 = (f32[1,64,128]{2,1,0:T(8,128)}, f32[24,256]{1,0:T(8,128)}) custom-call(f32[8,32,128]{2,1,0:T(8,128)} %modes_hbm.1, f32[8,32]{1,0:T(8,128)} %noise_hbm.1), custom_call_target="tpu_custom_call" | custom-call | tf_op jit(solution)/shard_map/pallas_call | solution.py:477
  14.0 0.0 copy-start.3
  14.0 3.0 %collective-permute-start = (f32[1,64,128]{2,1,0:T(8,128)}, f32[1,64,128]{2,1,0:T(8,128)S(1)}, u32[]{:S(2)}, u32[]{:S(2)}) collective-permute-start(f32[1,64,128]{2,1,0:T(8,128)} %get-tuple-element.13), channel_id=1, source_target_pairs={{0,32},{16,48},{32,0},{48,16},{64,96},{80,112},{96,64},{112,80},{1... | collective-permute-start | bytes 98312 | tf_op jit(solution)/shard_map/ppermute | solution.py:522
  17.0 1.9 %collective-permute-done = f32[1,64,128]{2,1,0:T(8,128)S(1)} collective-permute-done((f32[1,64,128]{2,1,0:T(8,128)}, f32[1,64,128]{2,1,0:T(8,128)S(1)}, u32[]{:S(2)}, u32[]{:S(2)}) %collective-permute-start) | collective-permute-done | bytes 32800 | tf_op jit(solution)/shard_map/ppermute | solution.py:522
  18.9 0.8 pad_maximum_fusion.1
  19.7 2.7 %collective-permute-start.1 = (f32[2,64,128]{2,1,0:T(8,128)S(1)}, f32[2,64,128]{2,1,0:T(8,128)S(1)}, u32[]{:S(2)}, u32[]{:S(2)}) collective-permute-start(f32[2,64,128]{2,1,0:T(8,128)S(1)} %pad_maximum_fusion.1), channel_id=1, source_target_pairs={{0,128},{16,144},{32,160},{48,176},{64,192},{80,208},{96,224},{112... | collective-permute-start | bytes 196616 | tf_op jit(solution)/shard_map/ppermute | solution.py:522
  22.4 0.8 constant_dynamic-update-slice_fusion.3
  23.2 0.0 copy-start.9
  23.2 1.1 collective-permute-done.1
  24.3 0.8 pad_maximum_fusion
  25.1 1.4 %collective-permute-start.2 = (f32[4,64,128]{2,1,0:T(8,128)S(1)}, f32[4,64,128]{2,1,0:T(8,128)S(1)}, u32[]{:S(2)}, u32[]{:S(2)}) collective-permute-start(f32[4,64,128]{2,1,0:T(8,128)S(1)} %pad_maximum_fusion), channel_id=1, source_target_pairs={{0,16},{16,0},{32,48},{48,32},{64,80},{80,64},{96,112},{112,96},{1... | collective-permute-start | bytes 393224 | tf_op jit(solution)/shard_map/ppermute | solution.py:522
  26.4 0.0 all-to-all-done.x_ref
  26.4 0.0 copy-done.7
  26.4 0.0 copy-done.8
  26.5 0.0 copy-done.11
  26.5 0.0 copy-done.4
  26.5 0.0 copy-done.3
  26.5 0.0 copy-done.9
  26.5 2.0 %shard_map.151 = f32[512,128]{1,0:T(8,128)} custom-call(f32[16,16,256]{2,1,0:T(8,128)S(1)} %all-to-all-done.x_ref, f32[24,256]{1,0:T(8,128)S(1)} %copy-done.9, f32[128,128]{1,0:T(8,128)S(1)} %copy-done.11, f32[256,128]{1,0:T(8,128)S(1)} %copy-done.7, f32[256,128]{1,0:T(8,128)S(1)} %copy-done.8, f32[128,512]{1,0:T(8,128)S(1)} %copy-done.3, ...), custom_call_target="tpu_custom_call" | custom-call | tf_op jit(solution)/shard_map/pallas_call | solution.py:477
  28.5 14.9 %all-to-all-start.1 = ((f32[256,2,128]{2,1,0:T(2,128)}), f32[256,2,128]{2,1,0:T(2,128)S(1)}, u32[]{:S(2)}, u32[]{:S(2)}) async-start(f32[256,2,128]{2,1,0:T(2,128)} %bitcast.1), calls=%async_computation.1 | async-start | bytes 524288 | tf_op jit(solution)/shard_map/all_to_all | solution.py:490
  43.4 0.0 collective-permute-done.2
  43.5 1.4 %collective-permute-start.3 = (f32[8,64,128]{2,1,0:T(8,128)S(1)}, f32[8,64,128]{2,1,0:T(8,128)S(1)}, u32[]{:S(2)}, u32[]{:S(2)}) collective-permute-start(f32[8,64,128]{2,1,0:T(8,128)S(1)} %constant_dynamic-update-slice_fusion.near_ref), channel_id=1, source_target_pairs={{0,64},{16,80},{32,96},{48,112},{64,0},{80,16},{96,32},{112,48},{1... | collective-permute-start | bytes 786440 | tf_op jit(solution)/shard_map/ppermute | solution.py:522
  44.9 7.4 %collective-permute-done.3.far_ref = f32[8,64,128]{2,1,0:T(8,128)S(1)} collective-permute-done((f32[8,64,128]{2,1,0:T(8,128)S(1)}, f32[8,64,128]{2,1,0:T(8,128)S(1)}, u32[]{:S(2)}, u32[]{:S(2)}) %collective-permute-start.3) | collective-permute-done | bytes 262176 | tf_op jit(solution)/shard_map/ppermute | solution.py:522
  52.3 10.3 %shard_map.152 = (f32[256,512]{1,0:T(8,128)S(1)}, f32[2,256,256]{2,1,0:T(8,128)S(1)}) custom-call(f32[8,64,128]{2,1,0:T(8,128)S(1)} %constant_dynamic-update-slice_fusion.near_ref, f32[8,64,128]{2,1,0:T(8,128)S(1)} %collective-permute-done.3.far_ref), custom_call_target="tpu_custom_call" | custom-call | tf_op jit(solution)/shard_map/pallas_call | solution.py:477
  62.6 0.0 all-to-all-done.1
  62.6 0.0 copy-start.5
  62.6 0.0 copy-start.6
  62.7 0.0 copy-start.10
  62.7 1.9 %shard_map.153 = f32[512,128]{1,0:T(8,128)S(1)} custom-call(f32[512,128]{1,0:T(8,128)S(1)} %bitcast.13, f32[256,512]{1,0:T(8,128)S(1)} %get-tuple-element.14.trans_ref, f32[2,256,256]{2,1,0:T(8,128)S(1)} %get-tuple-element.15.gain_ref), custom_call_target="tpu_custom_call" | custom-call | tf_op jit(solution)/shard_map/pallas_call | solution.py:477
  64.6 0.0 copy-start.1
  64.6 0.0 copy-start.2
  64.6 30.2 %all_to_all.31 = f32[256,2,128]{2,1,0:T(2,128)S(1)} all-to-all(f32[256,2,128]{2,1,0:T(2,128)S(1)} %bitcast.15), channel_id=1, replica_groups=mesh['det'=16,'tm'=16] {'det','tm'}, dimensions={0} | all-to-all | bytes 524288 | tf_op jit(solution)/shard_map/all_to_all | solution.py:490
  94.8 0.0 copy-done.5
  94.8 0.0 copy-done.6
  94.8 0.0 copy-done.10
  94.8 0.0 copy-done.1
  94.8 0.0 copy-done.2
  94.8 1.5 %shard_map.154 = f32[16,16,256]{2,1,0:T(8,128)} custom-call(f32[512,128]{1,0:T(8,128)S(1)} %bitcast.14, f32[24,256]{1,0:T(8,128)S(1)} %copy-done.9, f32[256,128]{1,0:T(8,128)S(1)} %copy-done.5, f32[256,128]{1,0:T(8,128)S(1)} %copy-done.6, bf16[2,256,256]{2,1,0:T(8,128)(2,1)S(1)} %copy-done.1, bf16[2,256,256]{2,1,0:T(8,128)(2,1)S(1)} %copy-done.2, ...), custom_call_target="tpu_custom_call" | custom-call | tf_op jit(solution)/shard_map/pallas_call | solution.py:477
  96.3 0.0 copy-start
  96.3 3.9 %all-to-all-start.3 = ((f32[16,16,256]{2,1,0:T(8,128)}), f32[16,16,256]{2,1,0:T(8,128)S(1)}, u32[]{:S(2)}, u32[]{:S(2)}) async-start(f32[16,16,256]{2,1,0:T(8,128)} %shard_map.154), calls=%async_computation.3 | async-start | bytes 524288 | tf_op jit(solution)/shard_map/all_to_all | solution.py:490
  100.2 0.0 copy-done
  100.2 3.4 %shard_map.156 = (f32[256,128]{1,0:T(8,128)S(1)}, f32[128,256]{1,0:T(8,128)S(1)}, f32[128,256]{1,0:T(8,128)S(1)}) custom-call(s32[32,2048]{1,0:T(8,128)S(1)} %copy-done), custom_call_target="tpu_custom_call" | custom-call | tf_op jit(solution)/shard_map/pallas_call | solution.py:477
  103.6 3.4 %shard_map.157 = (f32[256,128]{1,0:T(8,128)S(1)}, f32[128,256]{1,0:T(8,128)S(1)}, f32[128,256]{1,0:T(8,128)S(1)}) custom-call(s32[32,2048]{1,0:T(8,128)S(1)} %copy-done), custom_call_target="tpu_custom_call" | custom-call | tf_op jit(solution)/shard_map/pallas_call | solution.py:477
  107.0 5.0 %all-to-all-done.3 = f32[16,16,256]{2,1,0:T(8,128)S(1)} async-done(((f32[16,16,256]{2,1,0:T(8,128)}), f32[16,16,256]{2,1,0:T(8,128)S(1)}, u32[]{:S(2)}, u32[]{:S(2)}) %all-to-all-start.3) | async-done | bytes 262176 | tf_op jit(solution)/shard_map/all_to_all | solution.py:490
  112.0 7.4 %shard_map.158 = f32[256,128]{1,0:T(8,128)} custom-call(f32[256,256]{1,0:T(8,128)S(1)} %bitcast.11, f32[256,128]{1,0:T(8,128)S(1)} %get-tuple-element.16.refs_0_, f32[128,256]{1,0:T(8,128)S(1)} %get-tuple-element.17.refs_1_, f32[128,256]{1,0:T(8,128)S(1)} %get-tuple-element.18.refs_2_, f32[256,128]{1,0:T(8,128)S(1)} %get-tuple-element.19.refs_3_, ...), custom_call_target="tpu_custom_call" | custom-call | tf_op jit(solution)/shard_map/pallas_call | solution.py:477
  119.4 5.2 %all-to-all-start.4 = ((f32[256,1,128]{2,1,0:T(1,128)}), f32[256,1,128]{2,1,0:T(1,128)S(1)}, u32[]{:S(2)}, u32[]{:S(2)}) async-start(f32[256,1,128]{2,1,0:T(1,128)} %bitcast.7), calls=%async_computation.4 | async-start | bytes 262144 | tf_op jit(solution)/shard_map/all_to_all | solution.py:490
  124.6 0.8 shard_map.155
  125.3 11.8 %all-to-all-done.4 = f32[256,1,128]{2,1,0:T(1,128)S(1)} async-done(((f32[256,1,128]{2,1,0:T(1,128)}), f32[256,1,128]{2,1,0:T(1,128)S(1)}, u32[]{:S(2)}, u32[]{:S(2)}) %all-to-all-start.4) | async-done | bytes 131104 | tf_op jit(solution)/shard_map/all_to_all | solution.py:490
  137.1 0.6 shard_map.159
  (3 shorter events, 0.0 us)
Async XLA Ops:
  2.3 24.1 %copy-start.7 = (f32[256,128]{1,0:T(8,128)S(1)}, f32[256,128]{1,0:T(8,128)}, u32[]{:S(2)}) copy-start(f32[256,128]{1,0:T(8,128)} %constant.21.clone.keep_ref) | copy-start | bytes 393220
  2.3 24.1 %copy-start.8 = (f32[256,128]{1,0:T(8,128)S(1)}, f32[256,128]{1,0:T(8,128)}, u32[]{:S(2)}) copy-start(f32[256,128]{1,0:T(8,128)} %constant.22.clone.swap_ref) | copy-start | bytes 393220
  2.4 24.1 %copy-start.11 = (f32[128,128]{1,0:T(8,128)S(1)}, f32[128,128]{1,0:T(8,128)}, u32[]{:S(2)}) copy-start(f32[128,128]{1,0:T(8,128)} %constant.20.clone.first_ref) | copy-start | bytes 196612
  2.4 24.1 %all-to-all-start = ((f32[16,16,256]{2,1,0:T(8,128)}), f32[16,16,256]{2,1,0:T(8,128)S(1)}, u32[]{:S(2)}, u32[]{:S(2)}) async-start(f32[16,16,256]{2,1,0:T(8,128)} %bitcast.17), calls=%async_computation | async-start | bytes 524288 | tf_op jit(solution)/shard_map/all_to_all | solution.py:490
  12.5 14.0 %copy-start.4 = (f32[128,512]{1,0:T(8,128)S(1)}, f32[128,512]{1,0:T(8,128)}, u32[]{:S(2)}) copy-start(f32[128,512]{1,0:T(8,128)} %constant.24.clone.bottom_ref) | copy-start | bytes 786436
  14.0 12.4 %copy-start.3 = (f32[128,512]{1,0:T(8,128)S(1)}, f32[128,512]{1,0:T(8,128)}, u32[]{:S(2)}) copy-start(f32[128,512]{1,0:T(8,128)} %constant.23.clone.top_ref) | copy-start | bytes 786436
  14.0 4.9 %collective-permute-start = (f32[1,64,128]{2,1,0:T(8,128)}, f32[1,64,128]{2,1,0:T(8,128)S(1)}, u32[]{:S(2)}, u32[]{:S(2)}) collective-permute-start(f32[1,64,128]{2,1,0:T(8,128)} %get-tuple-element.13), channel_id=1, source_target_pairs={{0,32},{16,48},{32,0},{48,16},{64,96},{80,112},{96,64},{112,80},{1... | collective-permute-start | bytes 98312 | tf_op jit(solution)/shard_map/ppermute | solution.py:522
  19.7 4.6 %collective-permute-start.1 = (f32[2,64,128]{2,1,0:T(8,128)S(1)}, f32[2,64,128]{2,1,0:T(8,128)S(1)}, u32[]{:S(2)}, u32[]{:S(2)}) collective-permute-start(f32[2,64,128]{2,1,0:T(8,128)S(1)} %pad_maximum_fusion.1), channel_id=1, source_target_pairs={{0,128},{16,144},{32,160},{48,176},{64,192},{80,208},{96,224},{112... | collective-permute-start | bytes 196616 | tf_op jit(solution)/shard_map/ppermute | solution.py:522
  23.2 3.3 %copy-start.9 = (f32[24,256]{1,0:T(8,128)S(1)}, f32[24,256]{1,0:T(8,128)}, u32[]{:S(2)}) copy-start(f32[24,256]{1,0:T(8,128)} %get-tuple-element.12.scale_ref) | copy-start | bytes 73732
  25.1 18.4 %collective-permute-start.2 = (f32[4,64,128]{2,1,0:T(8,128)S(1)}, f32[4,64,128]{2,1,0:T(8,128)S(1)}, u32[]{:S(2)}, u32[]{:S(2)}) collective-permute-start(f32[4,64,128]{2,1,0:T(8,128)S(1)} %pad_maximum_fusion), channel_id=1, source_target_pairs={{0,16},{16,0},{32,48},{48,32},{64,80},{80,64},{96,112},{112,96},{1... | collective-permute-start | bytes 393224 | tf_op jit(solution)/shard_map/ppermute | solution.py:522
  28.5 34.1 %all-to-all-start.1 = ((f32[256,2,128]{2,1,0:T(2,128)}), f32[256,2,128]{2,1,0:T(2,128)S(1)}, u32[]{:S(2)}, u32[]{:S(2)}) async-start(f32[256,2,128]{2,1,0:T(2,128)} %bitcast.1), calls=%async_computation.1 | async-start | bytes 524288 | tf_op jit(solution)/shard_map/all_to_all | solution.py:490
  43.5 8.9 %collective-permute-start.3 = (f32[8,64,128]{2,1,0:T(8,128)S(1)}, f32[8,64,128]{2,1,0:T(8,128)S(1)}, u32[]{:S(2)}, u32[]{:S(2)}) collective-permute-start(f32[8,64,128]{2,1,0:T(8,128)S(1)} %constant_dynamic-update-slice_fusion.near_ref), channel_id=1, source_target_pairs={{0,64},{16,80},{32,96},{48,112},{64,0},{80,16},{96,32},{112,48},{1... | collective-permute-start | bytes 786440 | tf_op jit(solution)/shard_map/ppermute | solution.py:522
  62.6 32.2 %copy-start.5 = (f32[256,128]{1,0:T(8,128)S(1)}, f32[256,128]{1,0:T(8,128)}, u32[]{:S(2)}) copy-start(f32[256,128]{1,0:T(8,128)} %constant.25.clone.keep_ref) | copy-start | bytes 393220
  62.6 32.1 %copy-start.6 = (f32[256,128]{1,0:T(8,128)S(1)}, f32[256,128]{1,0:T(8,128)}, u32[]{:S(2)}) copy-start(f32[256,128]{1,0:T(8,128)} %constant.26.clone.swap_ref) | copy-start | bytes 393220
  62.7 32.1 %copy-start.10 = (bf16[2,128,128]{2,1,0:T(8,128)(2,1)S(1)}, bf16[2,128,128]{2,1,0:T(8,128)(2,1)}, u32[]{:S(2)}) copy-start(bf16[2,128,128]{2,1,0:T(8,128)(2,1)} %constant.29.clone.last_ref) | copy-start | bytes 196612
  64.6 30.2 %copy-start.1 = (bf16[2,256,256]{2,1,0:T(8,128)(2,1)S(1)}, bf16[2,256,256]{2,1,0:T(8,128)(2,1)}, u32[]{:S(2)}) copy-start(bf16[2,256,256]{2,1,0:T(8,128)(2,1)} %constant.27.clone.top_ref) | copy-start | bytes 786436
  64.6 30.2 %copy-start.2 = (bf16[2,256,256]{2,1,0:T(8,128)(2,1)S(1)}, bf16[2,256,256]{2,1,0:T(8,128)(2,1)}, u32[]{:S(2)}) copy-start(bf16[2,256,256]{2,1,0:T(8,128)(2,1)} %constant.28.clone.bottom_ref) | copy-start | bytes 786436
  96.3 3.9 %copy-start = (s32[32,2048]{1,0:T(8,128)S(1)}, s32[32,2048]{1,0:T(8,128)}, u32[]{:S(2)}) copy-start(s32[32,2048]{1,0:T(8,128)} %point_ref.3) | copy-start | bytes 786436
  96.3 15.7 %all-to-all-start.3 = ((f32[16,16,256]{2,1,0:T(8,128)}), f32[16,16,256]{2,1,0:T(8,128)S(1)}, u32[]{:S(2)}, u32[]{:S(2)}) async-start(f32[16,16,256]{2,1,0:T(8,128)} %shard_map.154), calls=%async_computation.3 | async-start | bytes 524288 | tf_op jit(solution)/shard_map/all_to_all | solution.py:490
  119.4 17.7 %all-to-all-start.4 = ((f32[256,1,128]{2,1,0:T(1,128)}), f32[256,1,128]{2,1,0:T(1,128)S(1)}, u32[]{:S(2)}, u32[]{:S(2)}) async-start(f32[256,1,128]{2,1,0:T(1,128)} %bitcast.7), calls=%async_computation.4 | async-start | bytes 262144 | tf_op jit(solution)/shard_map/all_to_all | solution.py:490
